TPU v7x, 256 devices: a whole 4x4x8 slice. The times are simulated.
256 devices in a mesh: gx: 16 (over x_lo, z), gy: 4 (over y), gz: 4 (over x_hi, core).
Axes of the slice: x: 4 (x_hi: 2, x_lo: 2; x = x_hi * 2 + x_lo), y: 4, z: 8, core: 2. Of those that a mesh axis runs over, the one named last changes fastest.
Arguments:
- concentration: float32 [256, 512, 1024], P('gz', 'gx', 'gy'), may hold values from -6 to 6
- pit_mask: int32 [256, 512, 1024], P('gz', 'gx', 'gy'), may hold values 0 or 1
- phase_ids: int32 [256, 512, 1024], P('gz', 'gx', 'gy'), may hold values from 0 to 3
- bond_offsets: int32 [28, 2], replicated, may hold values from -3 to 3, as said below
- damage: int32 [256, 512, 1024], P('gz', 'gx', 'gy'), may hold values 0 or 1
- bond_weight: float32 [28], replicated, may hold values from 0.25 to 1
- phase_diffusivity: float32 [4], replicated, may hold values from 0.25 to 1
- phase_rate: float32 [4], replicated, may hold values from 0.5 to 2
Outputs:
- updated: float32 [256, 512, 1024], P('gz', 'gx', 'gy')
Inputs may be any that keep to these rules, and one draw needn't show every extreme that they name: `bond_offsets`: each row is a distinct nonzero lateral offset; the four offsets (3, 0), (-3, 0), (0, 3), (0, -3) are always among them.
All inputs are finite; a program needn't handle non-finite values. No bound on the sum of `pit_mask` or of `damage` on one device may be relied on, other than what follows from the above.
Results may differ from a plain program's by a relative error of at most 0.0006.
Values sent between devices are 32-bit elements; how exact they have to be, the bound alone decides.
No kernel may reach another device: no remote copies, remote signals or barrier semaphores. Data moves between devices by JAX's collectives and lax.ppermute only.
A program may use at most 128 MiB of HBM per device.

v0:
```python
import jax
import jax.numpy as jnp
from jax import lax
from jax.sharding import PartitionSpec as P

NPHASE = 4
SUBSTEPS = 2


lateral_step = 0.02
dissolve_step = 0.25


def with_halo(block, sides, width):
    for axis, dim in sides:
        count = lax.axis_size(axis)
        forward = [(i, i + 1) for i in range(count - 1)]
        forward.append((count - 1, 0))
        backward = [(target, source) for source, target in forward]
        low = lax.ppermute(
            lax.slice_in_dim(block, block.shape[dim] - width, None, axis=dim), axis, forward
        )
        high = lax.ppermute(lax.slice_in_dim(block, 0, width, axis=dim), axis, backward)
        block = jnp.concatenate([low, block, high], axis=dim)
    return block


def phase_lookup(phase_ids, table):
    total = jnp.zeros(phase_ids.shape, jnp.float32)
    for phase in range(NPHASE):
        total = total + jnp.where(phase_ids == phase, table[phase], jnp.float32(0.0))
    return total


def stencil_weights(bond_offsets, bond_weight):
    places = jnp.arange(7, dtype=jnp.int32)
    match_x = (bond_offsets[:, 0:1] + 3 == places[None, :]).astype(jnp.float32)
    match_y = (bond_offsets[:, 1:2] + 3 == places[None, :]).astype(jnp.float32)
    return jnp.sum(bond_weight[:, None, None] * match_x[:, :, None] * match_y[:, None, :], axis=0)


def lateral(padded, mobility, source, stencil_table, rows, columns):
    center = padded[:, 3 : 3 + rows, 3 : 3 + columns]
    flux = jnp.zeros_like(center)
    for first in range(7):
        for second in range(7):
            if first == 3 and second == 3:
                continue
            piece = padded[:, first : first + rows, second : second + columns]
            flux = flux + stencil_table[first, second] * (piece - center)
    return center + lateral_step * mobility * flux + dissolve_step * source * (1.0 - center)


def invert_two(matrix):
    determinant = matrix[0, 0] * matrix[1, 1] - matrix[0, 1] * matrix[1, 0]
    top_row = jnp.stack([matrix[1, 1], -matrix[0, 1]])
    low_row = jnp.stack([-matrix[1, 0], matrix[0, 0]])
    return jnp.stack([top_row, low_row]) / determinant


def times_two(left, right):
    return jnp.dot(left, right, precision=lax.Precision.HIGHEST)


def apply_two(matrix, rows):
    return jnp.tensordot(matrix, rows, axes=1, precision=lax.Precision.HIGHEST)


def block_inverse(depth, stiff, is_top, is_bottom):
    middle = jnp.full((depth,), 1.0 + 2.0 * stiff, jnp.float32)
    if is_top:
        middle = middle.at[0].set(1.0 + stiff)
    if is_bottom:
        middle = middle.at[depth - 1].set(1.0 + stiff)
    lower = jnp.full((depth,), -stiff, jnp.float32).at[0].set(0.0)
    upper = jnp.full((depth,), -stiff, jnp.float32).at[depth - 1].set(0.0)
    return lax.linalg.tridiagonal_solve(lower, middle, upper, jnp.eye(depth, dtype=jnp.float32))


def local(
    concentration,
    pit_mask,
    phase_ids,
    bond_offsets,
    damage,
    bond_weight,
    phase_diffusivity,
    phase_rate,
):
    depth, rows, columns = concentration.shape
    mobility = phase_lookup(phase_ids, phase_diffusivity) * (1.0 + 0.5 * damage.astype(jnp.float32))
    source = phase_lookup(phase_ids, phase_rate) * pit_mask.astype(jnp.float32)
    stencil_table = stencil_weights(bond_offsets, bond_weight)
    field = concentration
    for substep in range(SUBSTEPS):
        padded = with_halo(field, (("gx", 1), ("gy", 2)), 3)
        field = lateral(padded, mobility, source, stencil_table, rows, columns)
    stiff = 3.0 * depth * depth
    blocks = lax.axis_size("gz")
    own_index = lax.axis_index("gz")
    inverses = [
        block_inverse(depth, stiff, block == 0, block == blocks - 1) for block in range(blocks)
    ]
    zeros_column = jnp.zeros((depth,), jnp.float32)
    right_spikes = [
        stiff * inverses[block][:, depth - 1] if block < blocks - 1 else zeros_column
        for block in range(blocks)
    ]
    left_spikes = [
        stiff * inverses[block][:, 0] if block > 0 else zeros_column for block in range(blocks)
    ]
    lower_maps = []
    upper_maps = []
    for block in range(blocks):
        left_end = left_spikes[block]
        right_end = right_spikes[block]
        zero_entry = jnp.float32(0.0)
        lower_maps.append(
            jnp.stack(
                [jnp.stack([zero_entry, left_end[0]]), jnp.stack([zero_entry, left_end[depth - 1]])]
            )
        )
        upper_maps.append(
            jnp.stack(
                [
                    jnp.stack([right_end[0], zero_entry]),
                    jnp.stack([right_end[depth - 1], zero_entry]),
                ]
            )
        )
    schur_inverse = []
    carry_maps = []
    for block in range(blocks):
        if block == 0:
            schur = jnp.eye(2, dtype=jnp.float32)
            carry_maps.append(jnp.zeros((2, 2), jnp.float32))
        else:
            carried = times_two(lower_maps[block], schur_inverse[block - 1])
            carry_maps.append(carried)
            schur = jnp.eye(2, dtype=jnp.float32) - times_two(carried, upper_maps[block - 1])
        schur_inverse.append(invert_two(schur))
    own_inverse = jnp.stack(inverses)[own_index]
    flat = field.reshape(depth, rows * columns)
    local_solution = jnp.dot(own_inverse, flat, precision=lax.Precision.HIGHEST).reshape(
        depth, rows, columns
    )
    edge_rows = jnp.stack([local_solution[0], local_solution[depth - 1]])
    own_right = jnp.stack(right_spikes)[own_index]
    own_left = jnp.stack(left_spikes)[own_index]
    every_edge = lax.all_gather(edge_rows[None], "gz", axis=0, tiled=True)
    reduced = []
    for block in range(blocks):
        if block == 0:
            reduced.append(every_edge[0])
        else:
            reduced.append(every_edge[block] + apply_two(carry_maps[block], reduced[block - 1]))
    solved = [None] * blocks
    for block in range(blocks - 1, -1, -1):
        if block == blocks - 1:
            solved[block] = apply_two(schur_inverse[block], reduced[block])
        else:
            solved[block] = apply_two(
                schur_inverse[block],
                reduced[block] + apply_two(upper_maps[block], solved[block + 1]),
            )
    all_solved = jnp.stack(solved)
    next_top = all_solved[jnp.minimum(own_index + 1, blocks - 1), 0]
    prev_bottom = all_solved[jnp.maximum(own_index - 1, 0), 1]
    implicit = (
        local_solution
        + own_right[:, None, None] * next_top[None]
        + own_left[:, None, None] * prev_bottom[None]
    )
    return 2.0 * implicit - field


def solution(mesh):
    in_specs = (
        P("gz", "gx", "gy"),
        P("gz", "gx", "gy"),
        P("gz", "gx", "gy"),
        P(),
        P("gz", "gx", "gy"),
        P(),
        P(),
        P(),
    )
    out_specs = P("gz", "gx", "gy")
    return jax.shard_map(local, mesh=mesh, in_specs=in_specs, out_specs=out_specs, check_vma=False)
```

profile of v0, /device:TPU:1, one launch (start us, length us, event | category | flops | bytes accessed | tf_op | source)
XLA Modules:
  0.0 239.0 jit_solution(2703609094737433852)
XLA Ops:
  0.0 1.4 fusion.566
  1.5 7.4 %collective-permute-start.1 = (f32[64,3,256]{2,0,1:T(8,128)S(1)}, f32[64,3,256]{2,0,1:T(8,128)S(1)}, u32[]{:S(2)}, u32[]{:S(2)}) collective-permute-start(f32[64,3,256]{2,0,1:T(8,128)S(1)} %copy.426), channel_id=1, source_target_pairs={{16,0},{32,16},{48,32},{64,48},{80,64},{96,80},{112,96},{128,112},... | collective-permute-start | bytes 589832 | tf_op jit(solution)/shard_map/ppermute | solution.py:23
  9.0 0.8 add_bitcast_fusion.1
  9.8 0.7 fusion.222
  10.6 0.7 fusion.572
  11.3 0.7 fusion.573
  12.0 0.7 fusion.574
  13.3 0.7 fusion.578
  17.9 0.8 concatenate.195
  22.1 1.4 fusion.240
  23.5 1.2 fusion.244
  24.7 1.4 maximum_bitcast_fusion
  31.3 0.6 maximum_bitcast_fusion.3
  31.9 0.7 maximum_bitcast_fusion.2
  32.6 1.3 fusion.246
  37.4 0.7 fusion.580
  39.5 1.3 fusion.242
  42.6 0.7 maximum_bitcast_fusion.4
  44.2 0.7 fusion.579
  44.9 1.6 constant_dynamic-update-slice_fusion.1
  46.7 0.9 constant_dynamic-update-slice_fusion
  48.3 1.5 fusion.564
  49.8 2.4 %copy.403 = f32[64,38,3]{0,1,2:T(8,128)} copy(f32[64,38,3]{2,1,0:T(8,128)} %get-tuple-element.574) | data formatting | bytes 58368 | tf_op jit(solution)/shard_map/slice | solution.py:21
  52.2 1.3 collective-permute-start.2
  53.5 1.1 copy.406
  54.6 1.4 collective-permute-start.3
  57.3 1.3 copy.404
  58.7 2.4 copy.407
  61.1 3.8 %maximum_maximum_fusion = (f32[64,38,259]{2,1,0:T(8,128)S(1)}, f32[64,38,259]{2,1,0:T(8,128)S(1)}) fusion(f32[64,3,256]{2,1,0:T(4,128)} %copy-done.6, f32[64,32,256]{2,1,0:T(8,128)S(1)} %copy-done, f32[64,3,256]{2,1,0:T(4,128)} %copy-done.5, f32[64,38,3]{2,1,0:T(8,128)S(1)} %copy.404, f32[64,38,3]{2,1,0:T(8,128)} %copy.407), kind=kLoop, calls=%fused_computation | loop fusion | flops 3779328 | bytes 7587840 | tf_op jit(solution)/shard_map/concatenate | solution.py:24
  64.9 60.4 %fusion.149 = (f32[64,32,256]{2,1,0:T(8,128)S(1)}, pred[64,32,256]{2,1,0:T(8,128)(4,1)}, pred[64,32,256]{2,1,0:T(8,128)(4,1)}, pred[64,32,256]{2,1,0:T(8,128)(4,1)}, pred[64,32,256]{2,1,0:T(8,128)(4,1)}) fusion(f32[64,32,256]{2,1,0:T(8,128)} %param.28, f32[64,38,259]{2,1,0:T(8,128)S(1)} %get-tuple-element.573, f32[64,35,256]{2,1,0:T(8,128)} %get-tuple-element.586, ...), kind=kLoop, calls=%fused_computation.213 | loop fusion | flops 92798976 | bytes 107151584 | tf_op jit(solution)/shard_map/add | solution.py:51
  125.4 3.6 %collective-permute-start.5 = (f32[64,3,256]{2,0,1:T(8,128)S(1)}, f32[64,3,256]{2,0,1:T(8,128)S(1)}, u32[]{:S(2)}, u32[]{:S(2)}) collective-permute-start(f32[64,3,256]{2,0,1:T(8,128)S(1)} %copy.410), channel_id=1, source_target_pairs={{16,0},{32,16},{48,32},{64,48},{80,64},{96,80},{112,96},{128,112},... | collective-permute-start | bytes 589832 | tf_op jit(solution)/shard_map/ppermute | solution.py:23
  129.2 0.7 maximum_bitcast_fusion.7
  129.9 1.7 collective-permute-done.5
  131.8 4.0 %collective-permute-done.4 = f32[64,3,256]{2,0,1:T(8,128)S(1)} collective-permute-done((f32[64,3,256]{2,0,1:T(8,128)S(1)}, f32[64,3,256]{2,0,1:T(8,128)S(1)}, u32[]{:S(2)}, u32[]{:S(2)}) %collective-permute-start.4) | collective-permute-done | bytes 196640 | tf_op jit(solution)/shard_map/ppermute | solution.py:20
  136.7 1.5 fusion.563
  138.1 2.4 %copy.413 = f32[64,38,3]{0,1,2:T(8,128)} copy(f32[64,38,3]{2,1,0:T(8,128)} %get-tuple-element.570) | data formatting | bytes 58368 | tf_op jit(solution)/shard_map/slice | solution.py:21
  141.1 1.1 copy.416
  142.2 2.1 collective-permute-start.7
  144.3 0.7 maximum_bitcast_fusion.6
  147.5 1.3 copy.414
  148.9 2.4 copy.417
  151.3 3.8 %maximum_maximum_fusion.1 = (f32[64,38,259]{2,1,0:T(8,128)S(1)}, f32[64,38,259]{2,1,0:T(8,128)S(1)}) fusion(f32[64,3,256]{2,1,0:T(4,128)} %copy-done.3, f32[64,32,256]{2,1,0:T(8,128)S(1)} %get-tuple-element.563, f32[64,3,256]{2,1,0:T(4,128)} %copy-done.4, f32[64,38,3]{2,1,0:T(8,128)S(1)} %copy.414, f32[64,38,3]{2,1,0:T(8,128)} %copy.417), kind=kLoop, calls=%fused_computation.2 | loop fusion | flops 3779328 | bytes 7587840 | tf_op jit(solution)/shard_map/concatenate | solution.py:24
  155.1 59.4 %fusion.16 = f32[64,32,256]{2,1,0:T(8,128)S(1)} fusion(f32[64,32,256]{2,1,0:T(8,128)S(1)} %get-tuple-element.563, f32[64,3,256]{2,1,0:T(4,128)} %copy-done.3, f32[64,3,256]{2,1,0:T(4,128)} %copy-done.4, f32[64,38,259]{2,1,0:T(8,128)S(1)} %get-tuple-element.569, f32[64,38,259]{2,1,0:T(8,128)S(1)} %get-tuple-element.568, f32[]{:T(128)} %bitcast.193, ...), kind=kLoop, calls=%fused_computation.34 | loop fusion | flops 92274688 | bytes 98959584 | tf_op jit(solution)/shard_map/add | solution.py:51
  214.5 1.2 copy.431
  215.8 2.0 fusion.219
  218.0 1.9 copy.432
  220.0 11.5 %all-gather = f32[8,32,256]{2,1,0:T(8,128)S(1)} all-gather(f32[2,32,256]{2,1,0:T(8,128)S(1)} %pad_maximum_fusion.8), channel_id=2, replica_groups=mesh['gx'=16,'gy'=4,'gz'=4] {'gz'}, dimensions={0}, use_global_device_ids=true | all-gather | bytes 327680 | tf_op jit(solution)/shard_map/all_gather | solution.py:150
  235.5 3.4 %fusion.96 = f32[64,32,256]{2,1,0:T(8,128)} fusion(f32[64,32,256]{2,1,0:T(8,128)S(1)} %copy-done.2, f32[8,8,32,256]{3,2,1,0:T(8,128)} %copy.432, f32[32,256]{1,0:T(8,128)S(1)} %bitcast.1909, f32[64]{0:T(128)S(1)} %get-tuple-element.705, f32[32,256]{1,0:T(8,128)S(1)} %bitcast.1910, f32[64]{0:T(128)S(1)} %get-tuple-element.704), kind=kLoop, calls=%fused_computation.115 | loop fusion | flops 3145728 | bytes 6357504 | tf_op jit(solution)/shard_map/sub | solution.py:174
  (148 shorter events, 16.5 us)
Async XLA Ops:
  0.0 44.9 %copy-start = (f32[64,32,256]{2,1,0:T(8,128)S(1)}, f32[64,32,256]{2,1,0:T(8,128)}, u32[]{:S(2)}) copy-start(f32[64,32,256]{2,1,0:T(8,128)} %param.28) | copy-start | bytes 6291460
  0.0 37.4 %copy-start.7 = (f32[4]{0:T(128)S(1)}, f32[4]{0:T(128)}, u32[]{:S(2)}) copy-start(f32[4]{0:T(128)} %param.35) | copy-start | bytes 52
  0.0 44.2 %copy-start.8 = (f32[4]{0:T(128)S(1)}, f32[4]{0:T(128)}, u32[]{:S(2)}) copy-start(f32[4]{0:T(128)} %param.34) | copy-start | bytes 52
  1.5 45.2 %collective-permute-start.1 = (f32[64,3,256]{2,0,1:T(8,128)S(1)}, f32[64,3,256]{2,0,1:T(8,128)S(1)}, u32[]{:S(2)}, u32[]{:S(2)}) collective-permute-start(f32[64,3,256]{2,0,1:T(8,128)S(1)} %copy.426), channel_id=1, source_target_pairs={{16,0},{32,16},{48,32},{64,48},{80,64},{96,80},{112,96},{128,112},... | collective-permute-start | bytes 589832 | tf_op jit(solution)/shard_map/ppermute | solution.py:23
  8.9 37.6 %collective-permute-start = (f32[64,3,256]{2,0,1:T(8,128)S(1)}, f32[64,3,256]{2,0,1:T(8,128)S(1)}, u32[]{:S(2)}, u32[]{:S(2)}) collective-permute-start(f32[64,3,256]{2,0,1:T(8,128)S(1)} %copy.425), channel_id=1, source_target_pairs={{0,16},{16,32},{32,48},{48,64},{64,80},{80,96},{96,112},{112,128},... | collective-permute-start | bytes 589832 | tf_op jit(solution)/shard_map/ppermute | solution.py:20
  24.7 13.5 %copy-start.13 = (f32[1,2]{1,0:T(1,128)}, f32[1,2]{1,0:T(1,128)S(1)}, u32[]{:S(2)}) copy-start(f32[1,2]{1,0:T(1,128)S(1)} %get-tuple-element.699) | copy-start | bytes 28
  24.7 13.7 %copy-start.11 = (f32[1,2]{1,0:T(1,128)}, f32[1,2]{1,0:T(1,128)S(1)}, u32[]{:S(2)}) copy-start(f32[1,2]{1,0:T(1,128)S(1)} %get-tuple-element.698) | copy-start | bytes 28
  26.2 6.4 %copy-start.19 = (f32[2,2]{1,0:T(2,128)}, f32[2,2]{1,0:T(2,128)S(1)}, u32[]{:S(2)}) copy-start(f32[2,2]{1,0:T(2,128)S(1)} %fusion.461) | copy-start | bytes 52
  34.0 12.6 %copy-start.15 = (f32[1,2]{1,0:T(1,128)}, f32[1,2]{1,0:T(1,128)S(1)}, u32[]{:S(2)}) copy-start(f32[1,2]{1,0:T(1,128)S(1)} %get-tuple-element.700) | copy-start | bytes 28
  34.0 12.6 %copy-start.17 = (f32[1,2]{1,0:T(1,128)}, f32[1,2]{1,0:T(1,128)S(1)}, u32[]{:S(2)}) copy-start(f32[1,2]{1,0:T(1,128)S(1)} %get-tuple-element.701) | copy-start | bytes 28
  34.1 4.3 %copy-start.21 = (f32[2,2]{1,0:T(2,128)}, f32[2,2]{1,0:T(2,128)S(1)}, u32[]{:S(2)}) copy-start(f32[2,2]{1,0:T(2,128)S(1)} %fusion.460) | copy-start | bytes 52
  43.3 3.2 %copy-start.9 = (f32[1,2]{1,0:T(1,128)}, f32[1,2]{1,0:T(1,128)S(1)}, u32[]{:S(2)}) copy-start(f32[1,2]{1,0:T(1,128)S(1)} %maximum_bitcast_fusion.4) | copy-start | bytes 28
  43.5 3.1 %copy-start.23 = (f32[2,2]{1,0:T(2,128)}, f32[2,2]{1,0:T(2,128)S(1)}, u32[]{:S(2)}) copy-start(f32[2,2]{1,0:T(2,128)S(1)} %fusion.239) | copy-start | bytes 52
  46.7 1.4 copy-start.5
  47.6 0.7 copy-start.6
  52.2 5.1 %collective-permute-start.2 = (f32[64,38,3]{0,1,2:T(8,128)}, f32[64,38,3]{0,1,2:T(8,128)}, u32[]{:S(2)}, u32[]{:S(2)}) collective-permute-start(f32[64,38,3]{0,1,2:T(8,128)} %copy.403), channel_id=1, source_target_pairs={{0,4},{4,8},{8,12},{12,0},{1,5},{5,9},{9,13},{13,1},{2,6},{6,10},{... | collective-permute-start | bytes 87560 | tf_op jit(solution)/shard_map/ppermute | solution.py:20
  54.6 4.1 %collective-permute-start.3 = (f32[64,38,3]{0,1,2:T(8,128)}, f32[64,38,3]{0,1,2:T(8,128)}, u32[]{:S(2)}, u32[]{:S(2)}) collective-permute-start(f32[64,38,3]{0,1,2:T(8,128)} %copy.406), channel_id=1, source_target_pairs={{4,0},{8,4},{12,8},{0,12},{5,1},{9,5},{13,9},{1,13},{6,2},{10,6},{... | collective-permute-start | bytes 87560 | tf_op jit(solution)/shard_map/ppermute | solution.py:23
  125.4 6.3 %collective-permute-start.5 = (f32[64,3,256]{2,0,1:T(8,128)S(1)}, f32[64,3,256]{2,0,1:T(8,128)S(1)}, u32[]{:S(2)}, u32[]{:S(2)}) collective-permute-start(f32[64,3,256]{2,0,1:T(8,128)S(1)} %copy.410), channel_id=1, source_target_pairs={{16,0},{32,16},{48,32},{64,48},{80,64},{96,80},{112,96},{128,112},... | collective-permute-start | bytes 589832 | tf_op jit(solution)/shard_map/ppermute | solution.py:23
  129.1 6.7 %collective-permute-start.4 = (f32[64,3,256]{2,0,1:T(8,128)S(1)}, f32[64,3,256]{2,0,1:T(8,128)S(1)}, u32[]{:S(2)}, u32[]{:S(2)}) collective-permute-start(f32[64,3,256]{2,0,1:T(8,128)S(1)} %copy.409), channel_id=1, source_target_pairs={{0,16},{16,32},{32,48},{48,64},{64,80},{80,96},{96,112},{112,128},... | collective-permute-start | bytes 589832 | tf_op jit(solution)/shard_map/ppermute | solution.py:20
  131.8 4.6 %copy-start.3 = (f32[64,3,256]{2,1,0:T(4,128)}, f32[64,3,256]{2,1,0:T(4,128)S(1)}, u32[]{:S(2)}) copy-start(f32[64,3,256]{2,1,0:T(4,128)S(1)} %copy.412) | copy-start | bytes 589828
  135.9 0.7 copy-start.4
  140.5 7.0 %collective-permute-start.6 = (f32[64,38,3]{0,1,2:T(8,128)}, f32[64,38,3]{0,1,2:T(8,128)}, u32[]{:S(2)}, u32[]{:S(2)}) collective-permute-start(f32[64,38,3]{0,1,2:T(8,128)} %copy.413), channel_id=1, source_target_pairs={{0,4},{4,8},{8,12},{12,0},{1,5},{5,9},{9,13},{13,1},{2,6},{6,10},{... | collective-permute-start | bytes 87560 | tf_op jit(solution)/shard_map/ppermute | solution.py:20
  142.2 6.7 %collective-permute-start.7 = (f32[64,38,3]{0,1,2:T(8,128)}, f32[64,38,3]{0,1,2:T(8,128)}, u32[]{:S(2)}, u32[]{:S(2)}) collective-permute-start(f32[64,38,3]{0,1,2:T(8,128)} %copy.416), channel_id=1, source_target_pairs={{4,0},{8,4},{12,8},{0,12},{5,1},{9,5},{13,9},{1,13},{6,2},{10,6},{... | collective-permute-start | bytes 87560 | tf_op jit(solution)/shard_map/ppermute | solution.py:23
  214.5 1.3 copy-start.1
  217.9 13.5 %copy-start.20 = (f32[2,2]{1,0:T(2,128)S(1)}, f32[2,2]{1,0:T(2,128)}, u32[]{:S(2)}) copy-start(f32[2,2]{1,0:T(2,128)} %copy-done.19) | copy-start | bytes 52
  218.0 13.9 %copy-start.22 = (f32[2,2]{1,0:T(2,128)S(1)}, f32[2,2]{1,0:T(2,128)}, u32[]{:S(2)}) copy-start(f32[2,2]{1,0:T(2,128)} %copy-done.21) | copy-start | bytes 52
  218.0 14.3 %copy-start.24 = (f32[2,2]{1,0:T(2,128)S(1)}, f32[2,2]{1,0:T(2,128)}, u32[]{:S(2)}) copy-start(f32[2,2]{1,0:T(2,128)} %copy-done.23) | copy-start | bytes 52
  218.0 15.1 %copy-start.16 = (f32[1,2]{1,0:T(1,128)S(1)}, f32[1,2]{1,0:T(1,128)}, u32[]{:S(2)}) copy-start(f32[1,2]{1,0:T(1,128)} %copy-done.15) | copy-start | bytes 28
  218.0 15.1 %copy-start.18 = (f32[1,2]{1,0:T(1,128)S(1)}, f32[1,2]{1,0:T(1,128)}, u32[]{:S(2)}) copy-start(f32[1,2]{1,0:T(1,128)} %copy-done.17) | copy-start | bytes 28
  219.9 13.5 %copy-start.10 = (f32[1,2]{1,0:T(1,128)S(1)}, f32[1,2]{1,0:T(1,128)}, u32[]{:S(2)}) copy-start(f32[1,2]{1,0:T(1,128)} %copy-done.9) | copy-start | bytes 28
  219.9 14.6 %copy-start.12 = (f32[1,2]{1,0:T(1,128)S(1)}, f32[1,2]{1,0:T(1,128)}, u32[]{:S(2)}) copy-start(f32[1,2]{1,0:T(1,128)} %copy-done.11) | copy-start | bytes 28
  219.9 14.6 %copy-start.14 = (f32[1,2]{1,0:T(1,128)S(1)}, f32[1,2]{1,0:T(1,128)}, u32[]{:S(2)}) copy-start(f32[1,2]{1,0:T(1,128)} %copy-done.13) | copy-start | bytes 28
  219.9 15.6 %copy-start.2 = (f32[64,32,256]{2,1,0:T(8,128)S(1)}, f32[64,32,256]{2,1,0:T(8,128)}, u32[]{:S(2)}) copy-start(f32[64,32,256]{2,1,0:T(8,128)} %copy-done.1) | copy-start | bytes 6291460
where the time goes:
time: 241 us; the launch traced here: 239 us
  other arithmetic  147 us (61%)
  local copies, waits for them, and re-layouts  35.5 us (15%)
  starting transfers between devices  16.6 us (7%)
  between operations  15.8 us (7%)
  blocking collectives  11.5 us (5%)
  matrix products  6.42 us (3%)
  waiting for transfers between devices  5.73 us (2%)
    add x2, other arithmetic, lateral(): center + lateral_step * mobility * flux  120 us
    ppermute x4, starting transfers between devices, with_halo(): lax.ppermute(lax.slice_in_dim(block, 0, width, axis=dim), axis, backward)  14.6 us
    all_gather x1, blocking collectives, local(): every_edge = lax.all_gather(edge_rows[None], 'gz', axis=0, tiled=True)  11.5 us
    slice x7, local copies, waits for them, and re-layouts, with_halo(): lax.slice_in_dim(block, block.shape[dim] - width, None, axis=dim)  9.31 us
    concatenate x4, other arithmetic, with_halo(): block = jnp.concatenate([low, block, high], axis=dim)  8.51 us
    unnamed x57, local copies, waits for them, and re-layouts  5.54 us
    another operation x7, other arithmetic, invert_two(): return jnp.stack([top_row, low_row]) / determinant  5.52 us
    ppermute x3, local copies, waits for them, and re-layouts, with_halo(): lax.ppermute(lax.slice_in_dim(block, 0, width, axis=dim), axis, backward)  4.86 us
  transfers between devices with their start and end apart: 8, of which 2 were waited for; matrix products, arithmetic and copies ran while one was open for 14% of the time, Pallas kernels for 0%

commit v1 on v0

v1 whole, which is shorter than its diff:
```python
import functools

import jax
import jax.numpy as jnp
import numpy as np
from jax import lax
from jax.experimental import pallas as pl
from jax.experimental.pallas import tpu as pltpu
from jax.sharding import PartitionSpec as P

DZ, DX, DY = 64, 32, 256
BONDS = 28
INNER = DX - 6
f32, bf16 = jnp.float32, jnp.bfloat16
lateral_step = 0.02
dissolve_step = 0.25

VMEM = pl.BlockSpec(memory_space=pltpu.VMEM)
SMEM = pl.BlockSpec(memory_space=pltpu.SMEM)
HBM = pl.BlockSpec(memory_space=pl.ANY)


def call(kernel, name, out_shape, in_specs, out_specs, scratch=(), aliases=None, flops=0, nbytes=1 << 20):
    return pl.pallas_call(
        kernel,
        name=name,
        out_shape=out_shape,
        in_specs=in_specs,
        out_specs=out_specs,
        scratch_shapes=list(scratch),
        input_output_aliases=aliases or {},
        cost_estimate=pl.CostEstimate(flops=flops, bytes_accessed=nbytes, transcendentals=0),
        compiler_params=pltpu.CompilerParams(vmem_limit_bytes=48 << 20),
    )


def struct(*dims, dtype=f32):
    return jax.ShapeDtypeStruct(dims, dtype)


def lanes():
    return lax.broadcasted_iota(jnp.int32, (DZ, 128), 1)


def add_to_pack(pack, row, x):
    slot = 8 * (x % 16)
    lane = lanes()
    last = pltpu.roll(row[:, 128:], (slot + 3) % 128, 1)
    first = pltpu.roll(row[:, :128], (slot + 4) % 128, 1)
    pack = jnp.where((lane >= slot) & (lane < slot + 3), last, pack)
    return jnp.where((lane >= slot + 4) & (lane < slot + 7), first, pack)


def split(value):
    high = value.astype(bf16)
    return high, (value - high.astype(f32)).astype(bf16)


def edge_window(before, after, x):
    slot = 8 * ((x + 13) % 16)
    lane = lanes()
    window = pltpu.roll(jnp.where(lane >= slot, before, after), (128 - slot) % 128, 1)
    high = window.astype(bf16).astype(f32)
    low = pltpu.roll(window - high, 64, 1)
    return jnp.concatenate([jnp.where(lane < 64, high, low).astype(bf16), high.astype(bf16)], axis=1)


def weights_kernel(offsets, weight, w_ref, table):
    for place in range(49):
        table[place] = jnp.float32(0.0)
    for bond in range(BONDS):
        place = (offsets[2 * bond] + 3) * 7 + offsets[2 * bond + 1] + 3
        table[place] = table[place] + weight[bond]
    diff = lax.broadcasted_iota(jnp.int32, (DY, DY), 0) - lax.broadcasted_iota(jnp.int32, (DY, DY), 1) + 3

    @pl.loop(0, 7)
    def _(first):
        band = jnp.zeros((DY, DY), f32)
        for second in range(7):
            band = jnp.where(diff == second, table[first * 7 + second], band)
        w_ref[first], w_ref[7 + first] = split(band)

    lane = lax.broadcasted_iota(jnp.int32, (128, DY), 0)
    column = lax.broadcasted_iota(jnp.int32, (128, DY), 1)
    place = lane % 8
    which = jnp.where(place < 4, place - column, 255 + place - column)
    which = jnp.where((place == 3) | (place == 7), -1, which)
    which = jnp.where((which >= 0) & (which < 7), which, -100) + 7 * ((lane % 64) // 8)
    edge = jnp.zeros((128, DY), f32)
    for place in range(49):
        edge = jnp.where(which == place, table[place], edge)
    high, low = split(edge)
    w_ref[14, :128, :] = high
    w_ref[14, 128:, :] = jnp.where(lane < 64, low.astype(f32), 0.0).astype(bf16)


def right_side(w_ref):
    bands = [w_ref[a] for a in range(7)]
    return jnp.concatenate(bands + bands + [w_ref[7 + a] for a in range(7)] + [w_ref[14]], axis=0)


def flat(value):
    return value.reshape(value.shape[0] * DZ, DY)


def total_weight(weight):
    total = weight[0]
    for bond in range(1, BONDS):
        total = total + weight[bond]
    return total


def stepped(center, flux, pit, phase, damage, diffusivity, rate, weight_sum):
    def look(table, scale):
        value = jnp.where(phase == 0, table[0] * scale, table[1] * scale)
        return jnp.where(phase < 2, value, jnp.where(phase == 2, table[2] * scale, table[3] * scale))

    mobility = look(diffusivity, lateral_step) * (1.0 + 0.5 * damage.astype(f32))
    source = look(rate, dissolve_step) * pit.astype(f32)
    return center + mobility * (flux - weight_sum * center) + source * (1.0 - center)


def first_kernel(conc, field, pack, up, down, buf, sem, out_sem):
    for x in range(DX):
        pltpu.make_async_copy(conc.at[:, x, :], buf.at[x], sem.at[x // 8]).start()
    for group in range(4):
        for x in range(8 * group, 8 * group + 8):
            pltpu.make_async_copy(conc.at[:, x, :], buf.at[x], sem.at[group]).wait()
        part = pl.ds(8 * group, 8)
        pltpu.make_async_copy(buf.at[part], field.at[part], out_sem.at[group]).start()
        if group % 2 == 0:
            packed = jnp.zeros((DZ, 128), f32)
        for x in range(8 * group, 8 * group + 8):
            packed = add_to_pack(packed, buf[x], x)
        if group % 2:
            pack[group // 2] = packed
    for row in range(3):
        for half in range(2):
            down[2 * row + half] = buf[row, :, 128 * half : 128 * half + 128]
            up[2 * row + half] = buf[DX - 3 + row, :, 128 * half : 128 * half + 128]
    down[6] = jnp.zeros((DZ, 128), f32)
    up[6] = jnp.zeros((DZ, 128), f32)
    for group in range(4):
        part = pl.ds(8 * group, 8)
        pltpu.make_async_copy(buf.at[part], field.at[part], out_sem.at[group]).wait()


def join_kernel(left, right, up_in, down_in, halo, up, down, sem):
    lane = lanes()
    for group in range(2):
        halo[group] = jnp.where(lane % 8 < 4, left[group], right[group])
    copies = [
        pltpu.make_async_copy(halo.at[1], up.at[6], sem.at[0]),
        pltpu.make_async_copy(halo.at[0], down.at[6], sem.at[1]),
    ]
    for copy in copies:
        copy.start()
    for copy in copies:
        copy.wait()


CHUNK = INNER // 2


def inner_kernel(
    last, field, halo, pit, phase, damage, w_ref, weight, diffusivity, rate, sums, out, extra,
    buf, high, low, edges, pv, hv, dv, flux, res, sem, int_sem, out_sem,
):
    def field_copy(group):
        part = pl.ds(8 * group, 8)
        return pltpu.make_async_copy(field.at[part], buf.at[part], sem.at[group])

    def int_copies(chunk):
        for row in range(CHUNK * chunk, CHUNK * chunk + CHUNK):
            for source, target in ((pit, pv), (phase, hv), (damage, dv)):
                yield pltpu.make_async_copy(source.at[:, 3 + row, :], target.at[row], int_sem.at[chunk])

    for group in range(4):
        field_copy(group).start()
    for chunk in range(2):
        for copy in int_copies(chunk):
            copy.start()
    for x in range(3, DX - 3):
        group = (x + 13) // 16 - 1
        edges[x - 3] = edge_window(halo[group], halo[min(group + 1, 1)], x)
    for group in range(4):
        field_copy(group).wait()

        @pl.loop(0, 8)
        def _(row):
            x = 8 * group + row
            high[x], low[x] = split(buf[x])

    weight_sum = total_weight(weight)

    for chunk in range(2):
        row = CHUNK * chunk

        def rows(ref, a):
            return flat(ref[row + a : row + a + CHUNK])

        left = [rows(high, a) for a in range(7)] + [rows(low, a) for a in range(7)]
        left = left + [rows(high, a) for a in range(7)] + [rows(edges, 0)]
        flux[...] = jnp.dot(
            jnp.concatenate(left, axis=1), right_side(w_ref), preferred_element_type=f32
        ).reshape(CHUNK, DZ, DY)
        for copy in int_copies(chunk):
            copy.wait()

        @pl.loop(0, CHUNK)
        def _(i):
            res[row + i] = stepped(
                buf[row + i + 3], flux[i], pv[row + i], hv[row + i], dv[row + i], diffusivity, rate, weight_sum
            )

        part = pl.ds(row, CHUNK)
        pltpu.make_async_copy(res.at[part], out.at[pl.ds(3 + row, CHUNK)], out_sem.at[chunk]).start()
    if last:
        extra[...] = jnp.zeros_like(extra)
        depth_sums(res, sums, extra, 3, INNER, 0)
    else:
        for group in range(2):
            packed = jnp.zeros((DZ, 128), f32)
            for x in range(max(3, 16 * group), min(DX - 3, 16 * group + 16)):
                packed = add_to_pack(packed, res[x - 3], x)
            extra[group] = packed
    for chunk in range(2):
        row = CHUNK * chunk
        pltpu.make_async_copy(
            res.at[pl.ds(row, CHUNK)], out.at[pl.ds(3 + row, CHUNK)], out_sem.at[chunk]
        ).wait()


def depth_sums(res, sums, extra, start, count, first):
    own = lax.axis_index("gz")
    below = jnp.zeros((count, DY), f32)
    above = jnp.zeros((count, DY), f32)
    for z in range(DZ):
        value = res[first : first + count, z, :]
        below = below + sums[own, z] * value
        above = above + sums[own, DZ + z] * value
    extra[0, start : start + count, :] = below
    extra[1, start : start + count, :] = above


def outer_kernel(
    last, field, halo, from_low, from_high, pit, phase, damage, w_ref, weight, diffusivity, rate, sums,
    out_in, extra_in, out, extra, *rest,
):
    if last:
        buf, high, low, edges, pv, hv, dv, res, sem, int_sem, out_sem = rest
    else:
        up, down, buf, high, low, edges, pv, hv, dv, res, sem, int_sem, out_sem = rest
    field_copies = [
        pltpu.make_async_copy(field.at[pl.ds(0, 6)], buf.at[pl.ds(3, 6)], sem.at[0]),
        pltpu.make_async_copy(field.at[pl.ds(DX - 6, 6)], buf.at[pl.ds(9, 6)], sem.at[1]),
    ]
    places = [0, 1, 2, DX - 3, DX - 2, DX - 1]
    int_copies = [
        pltpu.make_async_copy(source.at[:, x, :], target.at[row], int_sem.at[0])
        for row, x in enumerate(places)
        for source, target in ((pit, pv), (phase, hv), (damage, dv))
    ]
    for copy in field_copies + int_copies:
        copy.start()
    groups = [from_low[6], halo[0], halo[1], from_high[6]]
    for row, x in enumerate(places):
        group = (x + 13) // 16
        edges[row] = edge_window(groups[group], groups[min(group + 1, 3)], x)
    for row in range(3):
        for half in range(2):
            part = slice(128 * half, 128 * half + 128)
            buf[row, :, part] = from_low[2 * row + half]
            buf[15 + row, :, part] = from_high[2 * row + half]
    for copy in field_copies:
        copy.wait()

    @pl.loop(0, 18)
    def _(row):
        high[row], low[row] = split(buf[row])

    weight_sum = total_weight(weight)

    def rows(ref, a):
        return jnp.concatenate([flat(ref[a : a + 3]), flat(ref[9 + a : 12 + a])], axis=0)

    left = [rows(high, a) for a in range(7)] + [rows(low, a) for a in range(7)]
    left = left + [rows(high, a) for a in range(7)] + [flat(edges[...])]
    res[...] = jnp.dot(
        jnp.concatenate(left, axis=1), right_side(w_ref), preferred_element_type=f32
    ).reshape(6, DZ, DY)
    for copy in int_copies:
        copy.wait()

    for row in range(6):
        center = buf[3 + row] if row < 3 else buf[9 + row]
        res[row] = stepped(center, res[row], pv[row], hv[row], dv[row], diffusivity, rate, weight_sum)
    out_copies = [
        pltpu.make_async_copy(res.at[pl.ds(0, 3)], out.at[pl.ds(0, 3)], out_sem.at[0]),
        pltpu.make_async_copy(res.at[pl.ds(3, 3)], out.at[pl.ds(DX - 3, 3)], out_sem.at[1]),
    ]
    for copy in out_copies:
        copy.start()
    if last:
        extra[...] = extra_in[...]
        depth_sums(res, sums, extra, 0, 3, 0)
        depth_sums(res, sums, extra, DX - 3, 3, 3)
    else:
        packed = [extra_in[0], extra_in[1]]
        for row, x in enumerate(places):
            packed[x // 16] = add_to_pack(packed[x // 16], res[row], x)
        for group in range(2):
            extra[group] = packed[group]
        for row in range(3):
            for half in range(2):
                part = slice(128 * half, 128 * half + 128)
                down[2 * row + half] = res[row, :, part]
                up[2 * row + half] = res[3 + row, :, part]
        down[6] = jnp.zeros((DZ, 128), f32)
        up[6] = jnp.zeros((DZ, 128), f32)
    for copy in out_copies:
        copy.wait()


def depth_tables(blocks):
    stiff = 3.0 * DZ * DZ
    count = DZ * blocks
    diagonal = np.full(count, 1.0 + 2.0 * stiff)
    diagonal[0] = diagonal[-1] = 1.0 + stiff
    fore = diagonal.copy()
    for i in range(1, count):
        fore[i] = diagonal[i] - stiff * stiff / fore[i - 1]
    back = diagonal.copy()
    for i in range(count - 2, -1, -1):
        back[i] = diagonal[i] - stiff * stiff / back[i + 1]
    sums = np.zeros((blocks, 2 * DZ))
    solve = np.zeros((blocks, 2 * DZ + 2 * blocks))
    for block in range(blocks):
        start, end = block * DZ, block * DZ + DZ - 1
        for z in range(DZ):
            sums[block, z] = np.prod(stiff / fore[start + z : end])
            sums[block, DZ + z] = np.prod(stiff / back[start + 1 : start + z + 1])
            solve[block, z] = stiff / fore[start + z - 1] if start + z else 0.0
            solve[block, DZ + z] = 1.0 / fore[start + z]
        if block < blocks - 1:
            solve[block, 2 * DZ - 1] = 1.0 / (fore[end] - stiff * stiff / back[end + 1])
        for other in range(blocks):
            if other < block:
                solve[block, 2 * DZ + other] = np.prod(stiff / fore[other * DZ + DZ - 1 : start])
            if other > block:
                solve[block, 2 * DZ + blocks + other] = np.prod(stiff / back[end + 1 : other * DZ + 1])
    return jnp.asarray(sums, f32), jnp.asarray(solve, f32)


def depth_kernel(blocks, field, every, solve, out, buf, sweep, sem, out_sem):
    parts = [pl.ds(8 * group, 8) for group in range(4)]
    for group in range(4):
        pltpu.make_async_copy(field.at[parts[group]], buf.at[parts[group]], sem.at[group]).start()
    own = lax.axis_index("gz")
    stiff = 3.0 * DZ * DZ
    above = jnp.zeros((DX, DY), f32)
    below = jnp.zeros((DX, DY), f32)
    for block in range(blocks):
        above = above + solve[own, 2 * DZ + block] * every[block, 0]
        below = below + solve[own, 2 * DZ + blocks + block] * every[block, 1]
    for group in range(4):
        pltpu.make_async_copy(field.at[parts[group]], buf.at[parts[group]], sem.at[group]).wait()
    value = above
    for z in range(DZ):
        carried = value if z == 0 else solve[own, z] * value
        value = buf[:, z, :] + carried
        sweep[z] = value
    value = (value + below) * solve[own, 2 * DZ - 1]
    for z in range(DZ - 1, -1, -1):
        if z < DZ - 1:
            value = (sweep[z] + stiff * value) * solve[own, DZ + z]
        sweep[z] = 2.0 * value - buf[:, z, :]
        if z % 16 == 0:
            part = pl.ds(z, 16)
            pltpu.make_async_copy(sweep.at[part], out.at[part], out_sem.at[z // 16]).start()
    for z in range(0, DZ, 16):
        part = pl.ds(z, 16)
        pltpu.make_async_copy(sweep.at[part], out.at[part], out_sem.at[z // 16]).wait()


def shift(value, axis, step):
    count = lax.axis_size(axis)
    return lax.ppermute(value, axis, [(i, (i + step) % count) for i in range(count)])


def local(conc, pit, phase, offsets, damage, weight, diffusivity, rate):
    blocks = lax.axis_size("gz")
    sums, solve = depth_tables(blocks)
    sem = pltpu.SemaphoreType.DMA
    slab = struct(7, DZ, 128)
    whole = struct(DX, DZ, DY)
    field, pack, up, down = call(
        first_kernel, "first", (whole, struct(2, DZ, 128), slab, slab),
        [HBM], (HBM, VMEM, VMEM, VMEM),
        [pltpu.VMEM((DX, DZ, DY), f32), sem((4,)), sem((4,))], nbytes=4 << 20,
    )(conc)
    w = call(
        weights_kernel, "weights", struct(15, DY, DY, dtype=bf16), [SMEM, SMEM], VMEM, [pltpu.SMEM((64,), f32)],
    )(offsets.reshape(2 * BONDS), weight)
    for substep in range(2):
        last = substep == 1
        left, right = shift(pack, "gy", 1), shift(pack, "gy", -1)
        halo, up, down = call(
            join_kernel, "join", (struct(2, DZ, 128), slab, slab),
            [VMEM, VMEM, HBM, HBM], (VMEM, HBM, HBM), [sem((2,))], {2: 1, 3: 2},
        )(left, right, up, down)
        from_low, from_high = shift(up, "gx", 1), shift(down, "gx", -1)
        extra = struct(2, DX, DY) if last else struct(2, DZ, 128)
        out, more = call(
            functools.partial(inner_kernel, last), f"inner{substep}", (whole, extra),
            [HBM, VMEM, HBM, HBM, HBM, VMEM, SMEM, SMEM, SMEM, SMEM], (HBM, VMEM),
            [
                pltpu.VMEM((DX, DZ, DY), f32), pltpu.VMEM((DX, DZ, DY), bf16), pltpu.VMEM((DX, DZ, DY), bf16),
                pltpu.VMEM((INNER, DZ, DY), bf16),
                pltpu.VMEM((INNER, DZ, DY), jnp.int32), pltpu.VMEM((INNER, DZ, DY), jnp.int32),
                pltpu.VMEM((INNER, DZ, DY), jnp.int32),
                pltpu.VMEM((CHUNK, DZ, DY), f32), pltpu.VMEM((INNER, DZ, DY), f32),
                sem((4,)), sem((2,)), sem((2,)),
            ],
            flops=2 * INNER * DZ * DY * 5632, nbytes=12 << 20,
        )(field, halo, pit, phase, damage, w, weight, diffusivity, rate, sums)
        outs = call(
            functools.partial(outer_kernel, last), f"outer{substep}",
            (whole, extra) + (() if last else (slab, slab)),
            [HBM, VMEM, VMEM, VMEM, HBM, HBM, HBM, VMEM, SMEM, SMEM, SMEM, SMEM, HBM, VMEM],
            (HBM, VMEM) + (() if last else (VMEM, VMEM)),
            [
                pltpu.VMEM((18, DZ, DY), f32), pltpu.VMEM((18, DZ, DY), bf16), pltpu.VMEM((18, DZ, DY), bf16),
                pltpu.VMEM((6, DZ, DY), bf16),
                pltpu.VMEM((6, DZ, DY), jnp.int32), pltpu.VMEM((6, DZ, DY), jnp.int32),
                pltpu.VMEM((6, DZ, DY), jnp.int32), pltpu.VMEM((6, DZ, DY), f32),
                sem((2,)), sem((1,)), sem((2,)),
            ],
            {12: 0}, flops=2 * 6 * DZ * DY * 5632, nbytes=6 << 20,
        )(field, halo, from_low, from_high, pit, phase, damage, w, weight, diffusivity, rate, sums, out, more)
        if last:
            field, ends = outs
        else:
            field, pack, up, down = outs
    every = lax.all_gather(ends, "gz", axis=0)
    return call(
        functools.partial(depth_kernel, blocks), "depth", struct(DZ, DX, DY),
        [HBM, VMEM, SMEM], HBM,
        [pltpu.VMEM((DX, DZ, DY), f32), pltpu.VMEM((DZ, DX, DY), f32), sem((4,)), sem((4,))],
        nbytes=6 << 20,
    )(field, every, solve)


def solution(mesh):
    block = P("gz", "gx", "gy")
    in_specs = (block, block, block, P(), block, P(), P(), P())
    return jax.shard_map(local, mesh=mesh, in_specs=in_specs, out_specs=block, check_vma=False)
```

time: 241 us -> 83.2 us (0.35)
  other arithmetic: 147 us -> 0 us
  Pallas kernels: 0 us -> 46.6 us
  local copies, waits for them, and re-layouts: 35.5 us -> 4.44 us
  between operations: 15.8 us -> 0.35 us
  matrix products: 6.42 us -> 0 us
    add x3 -> x0, other arithmetic: 121 us -> none  [the longest x2 120 us: lateral(): center + lateral_step * mobility * flux]
    pallas_call x0 -> x9, Pallas kernels: none -> 46.6 us  [the longest x2 29.7 us: local(): call(functools.partial(inner_kernel, last), f'inner{substep}', (whole, ex...]
    slice x27 -> x0, local copies, waits for them, and re-layouts: 20 us -> none  [the longest x7 9.31 us: with_halo(): lax.slice_in_dim(block, block.shape[dim] - width, None, axis=dim)]
    another operation x14 -> x0, other arithmetic: 10.9 us -> none  [the longest x7 5.52 us: invert_two(): return jnp.stack([top_row, low_row]) / determinant]
    concatenate x4 -> x0, other arithmetic: 8.51 us -> none  [with_halo(): block = jnp.concatenate([low, block, high], axis=dim)]
    ppermute x7 -> x0, local copies, waits for them, and re-layouts: 7.81 us -> none  [the longest x3 4.86 us: with_halo(): lax.ppermute(lax.slice_in_dim(block, 0, width, axis=dim), axis, backward)]
    dot_general x17 -> x0, matrix products: 6.42 us -> none  [the longest x10 3.66 us: apply_two(): return jnp.tensordot(matrix, rows, axes=1, precision=lax.Precision.HIGHEST)]
    sub x4 -> x0, other arithmetic: 4.18 us -> none  [the longest x1 3.44 us: local(): return 2.0 * implicit - field]
  transfers between devices with their start and end apart: 8 -> 8, of which waited for: 2 -> 3; matrix products, arithmetic and copies ran while one was open for 14% -> 0% of each run, Pallas kernels for 0% -> 38%
where the time goes in v1:
time: 83.2 us; the launch traced here: 83.1 us
  Pallas kernels  46.6 us (56%)
  starting transfers between devices  15.5 us (19%)
  blocking collectives  10.6 us (13%)
  waiting for transfers between devices  5.56 us (7%)
  local copies, waits for them, and re-layouts  4.44 us (5%)
    pallas_call x2, Pallas kernels, local(): call(functools.partial(inner_kernel, last), f'inner{substep}', (whole, ex...  29.7 us
    ppermute x8, starting transfers between devices, shift(): lax.ppermute(value, axis, [(i, (i + step) % count) for i in range(count)])  15.5 us
    all_gather x1, blocking collectives, local(): every = lax.all_gather(ends, 'gz', axis=0)  10.6 us
    pallas_call x2, Pallas kernels, local(): call(functools.partial(outer_kernel, last), f'outer{substep}', (whole, ex...  8.55 us
    ppermute x8, waiting for transfers between devices, shift(): lax.ppermute(value, axis, [(i, (i + step) % count) for i in range(count)])  5.56 us
    unnamed x19, local copies, waits for them, and re-layouts  4.34 us
    pallas_call x1, Pallas kernels, local(): call(functools.partial(depth_kernel, blocks), 'depth', struct(DZ, DX, DY)...  3.52 us
    pallas_call x1, Pallas kernels, local(): call(first_kernel, 'first', (whole, struct(2, DZ, 128), slab, slab), [HBM...  2.52 us
  transfers between devices with their start and end apart: 8, of which 3 were waited for; matrix products, arithmetic and copies ran while one was open for 0% of the time, Pallas kernels for 38%

profile of v1, /device:TPU:1, one launch (start us, length us, event | category | flops | bytes accessed | tf_op | source)
XLA Modules:
  0.0 83.1 jit_solution(11016412425858973566)
XLA Ops:
  0.0 0.0 copy-start.1
  0.0 1.6 %copy-done.1 = f32[64,32,256]{2,1,0:T(8,128)S(1)} copy-done((f32[64,32,256]{2,1,0:T(8,128)S(1)}, f32[64,32,256]{2,1,0:T(8,128)}, u32[]{:S(2)}) %copy-start.1) | copy-done | bytes 2097176
  1.6 0.0 copy-start.8
  1.6 0.0 copy-start.4
  1.6 0.0 copy-start.3
  1.6 0.0 copy-start.6
  1.6 0.0 copy-start.7
  1.6 2.5 %first.1 = (f32[32,64,256]{2,1,0:T(8,128)S(1)}, f32[2,64,128]{2,1,0:T(8,128)S(1)}, f32[7,64,128]{2,1,0:T(8,128)S(1)}, f32[7,64,128]{2,1,0:T(8,128)S(1)}) custom-call(f32[64,32,256]{2,1,0:T(8,128)S(1)} %copy-done.1), custom_call_target="tpu_custom_call" | custom-call | bytes 4194304 | tf_op jit(solution)/shard_map/first/pallas_call | solution.py:397
  4.1 0.0 copy-start.2
  4.1 1.3 %copy-done.2 = f32[32,64,256]{2,1,0:T(8,128)} copy-done((f32[32,64,256]{2,1,0:T(8,128)}, f32[32,64,256]{2,1,0:T(8,128)S(1)}, u32[]{:S(2)}) %copy-start.2) | copy-done | bytes 2097176
  5.5 3.6 %collective-permute-start.1 = (f32[2,64,128]{2,1,0:T(8,128)S(1)}, f32[2,64,128]{2,1,0:T(8,128)S(1)}, u32[]{:S(2)}, u32[]{:S(2)}) collective-permute-start(f32[2,64,128]{2,1,0:T(8,128)S(1)} %get-tuple-element.26), channel_id=1, source_target_pairs={{0,12},{4,0},{8,4},{12,8},{1,13},{5,1},{9,5},{13,9},{2,14},{6,2},{... | collective-permute-start | bytes 196616 | tf_op jit(solution)/shard_map/ppermute | solution.py:388
  9.0 0.0 collective-permute-start
  9.0 0.0 copy-done.8
  9.0 0.1 copy.19
  9.1 0.1 reshape.3.offsets
  9.2 0.0 copy-done.4
  9.2 2.1 %weights.1.w_ref = bf16[15,256,256]{2,1,0:T(8,128)(2,1)S(1)} custom-call(s32[56]{0:T(128)S(1)} %reshape.3.offsets, f32[28]{0:T(128)S(1)} %copy-done.4), custom_call_target="tpu_custom_call" | custom-call | bytes 1048576 | tf_op jit(solution)/shard_map/weights/pallas_call | solution.py:402
  11.3 0.0 collective-permute-done.1.right
  11.3 2.0 %collective-permute-done.left = f32[2,64,128]{2,1,0:T(8,128)S(1)} collective-permute-done((f32[2,64,128]{2,1,0:T(8,128)S(1)}, f32[2,64,128]{2,1,0:T(8,128)S(1)}, u32[]{:S(2)}, u32[]{:S(2)}) %collective-permute-start) | collective-permute-done | bytes 65568 | tf_op jit(solution)/shard_map/ppermute | solution.py:388
  13.3 0.1 join.2
  13.5 1.7 %collective-permute-start.2 = (f32[7,64,128]{2,1,0:T(8,128)S(1)}, f32[7,64,128]{2,1,0:T(8,128)S(1)}, u32[]{:S(2)}, u32[]{:S(2)}) collective-permute-start(f32[7,64,128]{2,1,0:T(8,128)S(1)} %get-tuple-element.30), channel_id=1, source_target_pairs={{0,16},{16,32},{32,48},{48,64},{64,80},{80,96},{96,112},{112,128},... | collective-permute-start | bytes 688136 | tf_op jit(solution)/shard_map/ppermute | solution.py:388
  15.2 5.1 %collective-permute-start.3 = (f32[7,64,128]{2,1,0:T(8,128)S(1)}, f32[7,64,128]{2,1,0:T(8,128)S(1)}, u32[]{:S(2)}, u32[]{:S(2)}) collective-permute-start(f32[7,64,128]{2,1,0:T(8,128)S(1)} %get-tuple-element.31), channel_id=1, source_target_pairs={{0,240},{16,0},{32,16},{48,32},{64,48},{80,64},{96,80},{112,96},{1... | collective-permute-start | bytes 688136 | tf_op jit(solution)/shard_map/ppermute | solution.py:388
  20.3 0.0 copy-done.3
  20.3 0.0 copy-done.6
  20.3 0.0 copy-done.7
  20.3 14.6 %inner0.1 = (f32[32,64,256]{2,1,0:T(8,128)S(1)}, f32[2,64,128]{2,1,0:T(8,128)S(1)}) custom-call(f32[32,64,256]{2,1,0:T(8,128)} %copy-done.2, f32[2,64,128]{2,1,0:T(8,128)S(1)} %get-tuple-element.29.halo, s32[64,32,256]{2,1,0:T(8,128)} %pit.7, s32[64,32,256]{2,1,0:T(8,128)} %phase.7, s32[64,32,256]{2,1,0:T(8,128)} %damage.7, ...), custom_call_target="tpu_custom_call" | custom-call | flops 4798283776 | bytes 12582912 | tf_op jit(solution)/shard_map/inner0/pallas_call | solution.py:414
  34.9 0.0 collective-permute-done.2.from_low
  34.9 0.0 collective-permute-done.3.from_high
  35.0 4.2 %outer0.1 = (f32[32,64,256]{2,1,0:T(8,128)S(1)}, f32[2,64,128]{2,1,0:T(8,128)S(1)}, f32[7,64,128]{2,1,0:T(8,128)S(1)}, f32[7,64,128]{2,1,0:T(8,128)S(1)}) custom-call(f32[32,64,256]{2,1,0:T(8,128)} %copy-done.2, f32[2,64,128]{2,1,0:T(8,128)S(1)} %get-tuple-element.29.halo, ...), custom_call_target="tpu_custom_call", output_to_operand_aliasing={{0}: (12, {})} | custom-call | flops 1107296256 | bytes 6291456 | tf_op jit(solution)/shard_map/outer0/pallas_call | solution.py:427
  39.2 0.0 copy-start
  39.2 1.3 %copy-done = f32[32,64,256]{2,1,0:T(8,128)} copy-done((f32[32,64,256]{2,1,0:T(8,128)}, f32[32,64,256]{2,1,0:T(8,128)S(1)}, u32[]{:S(2)}) %copy-start) | copy-done | bytes 2097176
  40.5 0.7 collective-permute-start.5
  41.2 0.8 collective-permute-start.4
  42.0 1.6 %collective-permute-done.5.right = f32[2,64,128]{2,1,0:T(8,128)S(1)} collective-permute-done((f32[2,64,128]{2,1,0:T(8,128)S(1)}, f32[2,64,128]{2,1,0:T(8,128)S(1)}, u32[]{:S(2)}, u32[]{:S(2)}) %collective-permute-start.5) | collective-permute-done | bytes 65568 | tf_op jit(solution)/shard_map/ppermute | solution.py:388
  43.6 1.9 %collective-permute-done.4.left = f32[2,64,128]{2,1,0:T(8,128)S(1)} collective-permute-done((f32[2,64,128]{2,1,0:T(8,128)S(1)}, f32[2,64,128]{2,1,0:T(8,128)S(1)}, u32[]{:S(2)}, u32[]{:S(2)}) %collective-permute-start.4) | collective-permute-done | bytes 65568 | tf_op jit(solution)/shard_map/ppermute | solution.py:388
  45.5 0.1 join.3
  45.6 0.1 collective-permute-start.6
  45.7 3.6 %collective-permute-start.7 = (f32[7,64,128]{2,1,0:T(8,128)S(1)}, f32[7,64,128]{2,1,0:T(8,128)S(1)}, u32[]{:S(2)}, u32[]{:S(2)}) collective-permute-start(f32[7,64,128]{2,1,0:T(8,128)S(1)} %get-tuple-element.40), channel_id=1, source_target_pairs={{0,240},{16,0},{32,16},{48,32},{64,48},{80,64},{96,80},{112,96},{1... | collective-permute-start | bytes 688136 | tf_op jit(solution)/shard_map/ppermute | solution.py:388
  49.3 15.1 %inner1.1 = (f32[32,64,256]{2,1,0:T(8,128)S(1)}, f32[2,32,256]{2,1,0:T(8,128)S(1)}) custom-call(f32[32,64,256]{2,1,0:T(8,128)} %copy-done, f32[2,64,128]{2,1,0:T(8,128)S(1)} %get-tuple-element.38.halo, s32[64,32,256]{2,1,0:T(8,128)} %pit.7, s32[64,32,256]{2,1,0:T(8,128)} %phase.7, s32[64,32,256]{2,1,0:T(8,128)} %damage.7, ...), custom_call_target="tpu_custom_call" | custom-call | flops 4798283776 | bytes 12582912 | tf_op jit(solution)/shard_map/inner1/pallas_call | solution.py:414
  64.4 0.0 collective-permute-done.6.from_low
  64.4 0.0 collective-permute-done.7.from_high
  64.4 0.0 copy-start.5
  64.4 4.3 %outer1.1 = (f32[32,64,256]{2,1,0:T(8,128)S(1)}, f32[2,32,256]{2,1,0:T(8,128)S(1)}) custom-call(f32[32,64,256]{2,1,0:T(8,128)} %copy-done, f32[2,64,128]{2,1,0:T(8,128)S(1)} %get-tuple-element.38.halo, f32[7,64,128]{2,1,0:T(8,128)S(1)} %collective-permute-done.6.from_low, ...), custom_call_target="tpu_custom_call", output_to_operand_aliasing={{0}: (12, {})} | custom-call | flops 1107296256 | bytes 6291456 | tf_op jit(solution)/shard_map/outer1/pallas_call | solution.py:427
  68.8 10.6 %all-gather = f32[8,32,256]{2,1,0:T(8,128)S(1)} all-gather(f32[2,32,256]{2,1,0:T(8,128)S(1)} %get-tuple-element.44), channel_id=2, replica_groups=mesh['gx'=16,'gy'=4,'gz'=4] {'gz'}, dimensions={0}, use_global_device_ids=true | all-gather | bytes 327680 | tf_op jit(solution)/shard_map/all_gather | solution.py:445
  79.4 0.0 copy-done.5
  79.4 3.5 %depth.1 = f32[64,32,256]{2,1,0:T(8,128)} custom-call(f32[32,64,256]{2,1,0:T(8,128)S(1)} %get-tuple-element.43.field, f32[4,2,32,256]{3,2,1,0:T(8,128)S(1)} %bitcast.1, f32[4,136]{1,0:T(4,128)S(1)} %copy-done.5), custom_call_target="tpu_custom_call" | custom-call | bytes 6291456 | tf_op jit(solution)/shard_map/depth/pallas_call | solution.py:446
Async XLA Ops:
  0.0 1.6 %copy-start.1 = (f32[64,32,256]{2,1,0:T(8,128)S(1)}, f32[64,32,256]{2,1,0:T(8,128)}, u32[]{:S(2)}) copy-start(f32[64,32,256]{2,1,0:T(8,128)} %conc.1) | copy-start | bytes 6291460
  1.6 7.4 %copy-start.8 = (s32[28,2]{0,1:T(2,128)S(1)}, s32[28,2]{0,1:T(2,128)}, u32[]{:S(2)}) copy-start(s32[28,2]{0,1:T(2,128)} %param.13) | copy-start | bytes 676
  1.6 7.6 %copy-start.4 = (f32[28]{0:T(128)S(1)}, f32[28]{0:T(128)}, u32[]{:S(2)}) copy-start(f32[28]{0:T(128)} %weight.9) | copy-start | bytes 340
  1.6 18.7 %copy-start.3 = (f32[4,128]{1,0:T(4,128)S(1)}, f32[4,128]{1,0:T(4,128)}, u32[]{:S(2)}) copy-start(f32[4,128]{1,0:T(4,128)} %constant.4.clone.sums) | copy-start | bytes 6148
  1.6 18.7 %copy-start.6 = (f32[4]{0:T(128)S(1)}, f32[4]{0:T(128)}, u32[]{:S(2)}) copy-start(f32[4]{0:T(128)} %diffusivity.7) | copy-start | bytes 52
  1.6 18.7 %copy-start.7 = (f32[4]{0:T(128)S(1)}, f32[4]{0:T(128)}, u32[]{:S(2)}) copy-start(f32[4]{0:T(128)} %rate.7) | copy-start | bytes 52
  4.1 1.3 %copy-start.2 = (f32[32,64,256]{2,1,0:T(8,128)}, f32[32,64,256]{2,1,0:T(8,128)S(1)}, u32[]{:S(2)}) copy-start(f32[32,64,256]{2,1,0:T(8,128)S(1)} %get-tuple-element.25.field) | copy-start | bytes 6291460
  5.5 5.8 %collective-permute-start.1 = (f32[2,64,128]{2,1,0:T(8,128)S(1)}, f32[2,64,128]{2,1,0:T(8,128)S(1)}, u32[]{:S(2)}, u32[]{:S(2)}) collective-permute-start(f32[2,64,128]{2,1,0:T(8,128)S(1)} %get-tuple-element.26), channel_id=1, source_target_pairs={{0,12},{4,0},{8,4},{12,8},{1,13},{5,1},{9,5},{13,9},{2,14},{6,2},{... | collective-permute-start | bytes 196616 | tf_op jit(solution)/shard_map/ppermute | solution.py:388
  9.0 4.3 %collective-permute-start = (f32[2,64,128]{2,1,0:T(8,128)S(1)}, f32[2,64,128]{2,1,0:T(8,128)S(1)}, u32[]{:S(2)}, u32[]{:S(2)}) collective-permute-start(f32[2,64,128]{2,1,0:T(8,128)S(1)} %get-tuple-element.26), channel_id=1, source_target_pairs={{0,4},{4,8},{8,12},{12,0},{1,5},{5,9},{9,13},{13,1},{2,6},{6,10},{... | collective-permute-start | bytes 196616 | tf_op jit(solution)/shard_map/ppermute | solution.py:388
  13.5 21.5 %collective-permute-start.2 = (f32[7,64,128]{2,1,0:T(8,128)S(1)}, f32[7,64,128]{2,1,0:T(8,128)S(1)}, u32[]{:S(2)}, u32[]{:S(2)}) collective-permute-start(f32[7,64,128]{2,1,0:T(8,128)S(1)} %get-tuple-element.30), channel_id=1, source_target_pairs={{0,16},{16,32},{32,48},{48,64},{64,80},{80,96},{96,112},{112,128},... | collective-permute-start | bytes 688136 | tf_op jit(solution)/shard_map/ppermute | solution.py:388
  15.2 19.8 %collective-permute-start.3 = (f32[7,64,128]{2,1,0:T(8,128)S(1)}, f32[7,64,128]{2,1,0:T(8,128)S(1)}, u32[]{:S(2)}, u32[]{:S(2)}) collective-permute-start(f32[7,64,128]{2,1,0:T(8,128)S(1)} %get-tuple-element.31), channel_id=1, source_target_pairs={{0,240},{16,0},{32,16},{48,32},{64,48},{80,64},{96,80},{112,96},{1... | collective-permute-start | bytes 688136 | tf_op jit(solution)/shard_map/ppermute | solution.py:388
  39.2 1.3 %copy-start = (f32[32,64,256]{2,1,0:T(8,128)}, f32[32,64,256]{2,1,0:T(8,128)S(1)}, u32[]{:S(2)}) copy-start(f32[32,64,256]{2,1,0:T(8,128)S(1)} %get-tuple-element.34.field) | copy-start | bytes 6291460
  40.5 3.1 %collective-permute-start.5 = (f32[2,64,128]{2,1,0:T(8,128)S(1)}, f32[2,64,128]{2,1,0:T(8,128)S(1)}, u32[]{:S(2)}, u32[]{:S(2)}) collective-permute-start(f32[2,64,128]{2,1,0:T(8,128)S(1)} %get-tuple-element.35), channel_id=1, source_target_pairs={{0,12},{4,0},{8,4},{12,8},{1,13},{5,1},{9,5},{13,9},{2,14},{6,2},{... | collective-permute-start | bytes 196616 | tf_op jit(solution)/shard_map/ppermute | solution.py:388
  41.2 4.3 %collective-permute-start.4 = (f32[2,64,128]{2,1,0:T(8,128)S(1)}, f32[2,64,128]{2,1,0:T(8,128)S(1)}, u32[]{:S(2)}, u32[]{:S(2)}) collective-permute-start(f32[2,64,128]{2,1,0:T(8,128)S(1)} %get-tuple-element.35), channel_id=1, source_target_pairs={{0,4},{4,8},{8,12},{12,0},{1,5},{5,9},{9,13},{13,1},{2,6},{6,10},{... | collective-permute-start | bytes 196616 | tf_op jit(solution)/shard_map/ppermute | solution.py:388
  45.6 18.8 %collective-permute-start.6 = (f32[7,64,128]{2,1,0:T(8,128)S(1)}, f32[7,64,128]{2,1,0:T(8,128)S(1)}, u32[]{:S(2)}, u32[]{:S(2)}) collective-permute-start(f32[7,64,128]{2,1,0:T(8,128)S(1)} %get-tuple-element.39), channel_id=1, source_target_pairs={{0,16},{16,32},{32,48},{48,64},{64,80},{80,96},{96,112},{112,128},... | collective-permute-start | bytes 688136 | tf_op jit(solution)/shard_map/ppermute | solution.py:388
  45.7 18.7 %collective-permute-start.7 = (f32[7,64,128]{2,1,0:T(8,128)S(1)}, f32[7,64,128]{2,1,0:T(8,128)S(1)}, u32[]{:S(2)}, u32[]{:S(2)}) collective-permute-start(f32[7,64,128]{2,1,0:T(8,128)S(1)} %get-tuple-element.40), channel_id=1, source_target_pairs={{0,240},{16,0},{32,16},{48,32},{64,48},{80,64},{96,80},{112,96},{1... | collective-permute-start | bytes 688136 | tf_op jit(solution)/shard_map/ppermute | solution.py:388
  64.4 15.0 %copy-start.5 = (f32[4,136]{1,0:T(4,128)S(1)}, f32[4,136]{1,0:T(4,128)}, u32[]{:S(2)}) copy-start(f32[4,136]{1,0:T(4,128)} %constant.5.clone.solve) | copy-start | bytes 6532

commit v2 on v1

v2 whole, which is shorter than its diff:
```python
import functools

import jax
import jax.numpy as jnp
import numpy as np
from jax import lax
from jax.experimental import pallas as pl
from jax.experimental.pallas import tpu as pltpu
from jax.sharding import PartitionSpec as P

DZ, DX, DY = 64, 32, 256
BONDS = 28
INNER = DX - 6
OUTER = [0, 1, 2, DX - 3, DX - 2, DX - 1]
f32, bf16 = jnp.float32, jnp.bfloat16
lateral_step = 0.02
dissolve_step = 0.25

VMEM = pl.BlockSpec(memory_space=pltpu.VMEM)
SMEM = pl.BlockSpec(memory_space=pltpu.SMEM)
HBM = pl.BlockSpec(memory_space=pltpu.HBM)
SEM = pltpu.SemaphoreType.DMA


def call(kernel, name, out_shape, in_specs, out_specs, scratch=(), flops=0, nbytes=1 << 20, limit=16):
    return pl.pallas_call(
        kernel,
        name=name,
        out_shape=out_shape,
        in_specs=in_specs,
        out_specs=out_specs,
        scratch_shapes=list(scratch),
        cost_estimate=pl.CostEstimate(flops=flops, bytes_accessed=nbytes, transcendentals=0),
        compiler_params=pltpu.CompilerParams(vmem_limit_bytes=limit << 20),
    )


def struct(*dims, dtype=f32):
    return jax.ShapeDtypeStruct(dims, dtype)


PARTS = tuple(struct(n, DZ, DY, dtype=t) for t in (f32, bf16, bf16) for n in (INNER, 6))
PACK = struct(2, DZ, 128)
SLABS = struct(7, DZ, 128)
WHOLE = struct(DX, DZ, DY)


def lanes():
    return lax.broadcasted_iota(jnp.int32, (DZ, 128), 1)


def add_to_pack(pack, row, x):
    slot = 8 * (x % 16)
    lane = lanes()
    last = pltpu.roll(row[:, 128:], (slot + 3) % 128, 1)
    first = pltpu.roll(row[:, :128], (slot + 4) % 128, 1)
    pack = jnp.where((lane >= slot) & (lane < slot + 3), last, pack)
    return jnp.where((lane >= slot + 4) & (lane < slot + 7), first, pack)


def split(value):
    high = value.astype(bf16)
    return high, (value - high.astype(f32)).astype(bf16)


def edge_window(before, after, x):
    slot = 8 * ((x + 13) % 16)
    lane = lanes()
    window = pltpu.roll(jnp.where(lane >= slot, before, after), (128 - slot) % 128, 1)
    high = window.astype(bf16).astype(f32)
    low = pltpu.roll(window - high, 64, 1)
    return jnp.concatenate([jnp.where(lane < 64, high, low).astype(bf16), high.astype(bf16)], axis=1)


def total_weight(weight):
    total = weight[0]
    for bond in range(1, BONDS):
        total = total + weight[bond]
    return total


def prepare_kernel(offsets, weight, diffusivity, rate, pit, phase, damage, w_ref, move, gain, table, pv, hv, dv, sem):
    def copies(group):
        return [
            pltpu.make_async_copy(source.at[:, x, :], target.at[x], sem.at[group])
            for x in range(8 * group, 8 * group + 8)
            for source, target in ((pit, pv), (phase, hv), (damage, dv))
        ]

    for group in range(4):
        for copy in copies(group):
            copy.start()
    for place in range(49):
        table[place] = jnp.float32(0.0)
    for bond in range(BONDS):
        place = (offsets[0, bond] + 3) * 7 + offsets[1, bond] + 3
        table[place] = table[place] + weight[bond]
    diff = lax.broadcasted_iota(jnp.int32, (DY, DY), 0) - lax.broadcasted_iota(jnp.int32, (DY, DY), 1) + 3

    @pl.loop(0, 7)
    def _(first):
        band = jnp.zeros((DY, DY), f32)
        for second in range(7):
            band = jnp.where(diff == second, table[first * 7 + second], band)
        w_ref[first], w_ref[7 + first] = split(band)

    lane = lax.broadcasted_iota(jnp.int32, (128, DY), 0)
    column = lax.broadcasted_iota(jnp.int32, (128, DY), 1)
    place = lane % 8
    which = jnp.where(place < 4, place - column, 255 + place - column)
    which = jnp.where((place == 3) | (place == 7), -1, which)
    which = jnp.where((which >= 0) & (which < 7), which, -100) + 7 * ((lane % 64) // 8)
    edge = jnp.zeros((128, DY), f32)
    for place in range(49):
        edge = jnp.where(which == place, table[place], edge)
    high, low = split(edge)
    w_ref[14, :128, :] = high
    w_ref[14, 128:, :] = jnp.where(lane < 64, low.astype(f32), 0.0).astype(bf16)

    def look(ids, values, scale):
        value = jnp.where(ids == 0, values[0] * scale, values[1] * scale)
        return jnp.where(ids < 2, value, jnp.where(ids == 2, values[2] * scale, values[3] * scale))

    for group in range(4):
        for copy in copies(group):
            copy.wait()

        @pl.loop(8 * group, 8 * group + 8)
        def _(x):
            ids = hv[x]
            move[x] = look(ids, diffusivity, lateral_step) * (1.0 + 0.5 * dv[x].astype(f32))
            gain[x] = look(ids, rate, dissolve_step) * pv[x].astype(f32)


def right_side(w_ref):
    bands = [w_ref[a] for a in range(7)]
    return jnp.concatenate(bands + bands + [w_ref[7 + a] for a in range(7)] + [w_ref[14]], axis=0)


def flat(value):
    return value.reshape(value.shape[0] * DZ, DY)


def stepped(center, flux, move, gain, weight_sum):
    return center + move * (flux - weight_sum * center) + gain * (1.0 - center)


def first_kernel(conc, mid, end, mid_high, end_high, mid_low, end_low, pack, up, down, buf, sem):
    for x in range(DX):
        pltpu.make_async_copy(conc.at[:, x, :], buf.at[x], sem.at[x // 8]).start()
    for group in range(4):
        for x in range(8 * group, 8 * group + 8):
            pltpu.make_async_copy(conc.at[:, x, :], buf.at[x], sem.at[group]).wait()
        if group % 2 == 0:
            packed = jnp.zeros((DZ, 128), f32)
        for x in range(8 * group, 8 * group + 8):
            row = buf[x]
            high, low = split(row)
            if x in OUTER:
                place = OUTER.index(x)
                end[place], end_high[place], end_low[place] = row, high, low
            else:
                mid[x - 3], mid_high[x - 3], mid_low[x - 3] = row, high, low
            packed = add_to_pack(packed, row, x)
        if group % 2:
            pack[group // 2] = packed
    fill_slabs(lambda row: buf[OUTER[row]], up, down)


def fill_slabs(row_of, up, down):
    for row in range(3):
        for half in range(2):
            part = slice(128 * half, 128 * half + 128)
            down[2 * row + half] = row_of(row)[:, part]
            up[2 * row + half] = row_of(3 + row)[:, part]
    down[6] = jnp.zeros((DZ, 128), f32)
    up[6] = jnp.zeros((DZ, 128), f32)


def join_kernel(left, right, up_in, down_in, halo, up, down):
    lane = lanes()
    for group in range(2):
        halo[group] = jnp.where(lane % 8 < 4, left[group], right[group])
    for slab in range(6):
        up[slab] = up_in[slab]
        down[slab] = down_in[slab]
    up[6] = halo[1]
    down[6] = halo[0]


CHUNK = INNER // 2


def row_range(mid, end, start, count):
    pieces = []
    stop = start + count
    if start < 3:
        pieces.append(end[start : min(stop, 3)])
    if stop > 3 and start < DX - 3:
        pieces.append(mid[max(start, 3) - 3 : min(stop, DX - 3) - 3])
    if stop > DX - 3:
        pieces.append(end[max(start, DX - 3) - DX + 6 : stop - DX + 6])
    pieces = [flat(piece) for piece in pieces]
    return pieces[0] if len(pieces) == 1 else jnp.concatenate(pieces, axis=0)


def inner_kernel(
    last, mid, mid_high, end_high, mid_low, end_low, halo, move, gain, w_ref, weight, sums,
    out, out_high, out_low, extra, edges,
):
    for x in range(3, DX - 3):
        group = (x + 13) // 16 - 1
        edges[x - 3] = edge_window(halo[group], halo[min(group + 1, 1)], x)
    weight_sum = total_weight(weight)
    packed = [jnp.zeros((DZ, 128), f32)] * 2
    for chunk in range(2):
        start = CHUNK * chunk
        highs = [row_range(mid_high, end_high, start + a, CHUNK) for a in range(7)]
        lows = [row_range(mid_low, end_low, start + a, CHUNK) for a in range(7)]
        left = highs + lows + highs + [flat(edges[start : start + CHUNK])]
        flux = jnp.dot(jnp.concatenate(left, axis=1), right_side(w_ref), preferred_element_type=f32)
        for i in range(CHUNK):
            row, x = start + i, start + i + 3
            new = stepped(mid[row], flux[DZ * i : DZ * i + DZ], move[x], gain[x], weight_sum)
            out[row] = new
            if not last:
                out_high[row], out_low[row] = split(new)
                packed[x // 16] = add_to_pack(packed[x // 16], new, x)
    if last:
        extra[...] = jnp.zeros_like(extra)
        depth_sums(out, sums, extra, 3, INNER, 0)
    else:
        for group in range(2):
            extra[group] = packed[group]


def depth_sums(rows, sums, extra, start, count, first):
    own = lax.axis_index("gz")
    below = jnp.zeros((count, DY), f32)
    above = jnp.zeros((count, DY), f32)
    for z in range(DZ):
        value = rows[first : first + count, z, :]
        below = below + sums[own, z] * value
        above = above + sums[own, DZ + z] * value
    extra[0, start : start + count, :] = below
    extra[1, start : start + count, :] = above


def outer_kernel(
    last, end, mid_high, end_high, mid_low, end_low, halo, from_low, from_high, move, gain, w_ref, weight, sums,
    extra_in, out, *rest,
):
    if last:
        (extra,) = rest
    else:
        out_high, out_low, extra, up, down = rest
    groups = [from_low[6], halo[0], halo[1], from_high[6]]
    edges = []
    for x in OUTER:
        group = (x + 13) // 16
        edges.append(edge_window(groups[group], groups[min(group + 1, 3)], x))

    def halo_rows(slabs):
        rows = [split(jnp.concatenate([slabs[2 * row], slabs[2 * row + 1]], axis=1)) for row in range(3)]
        return [row[0] for row in rows], [row[1] for row in rows]

    low_halo, high_halo = halo_rows(from_low), halo_rows(from_high)

    def taps(which, mid_part, end_part):
        top = low_halo[which] + [end_part[i] for i in range(3)] + [mid_part[i] for i in range(3)]
        bottom = [mid_part[INNER - 3 + i] for i in range(3)] + [end_part[3 + i] for i in range(3)]
        bottom = bottom + high_halo[which]
        return [jnp.concatenate(top[a : a + 3] + bottom[a : a + 3], axis=0) for a in range(7)]

    highs, lows = taps(0, mid_high, end_high), taps(1, mid_low, end_low)
    left = highs + lows + highs + [jnp.concatenate(edges, axis=0)]
    flux = jnp.dot(jnp.concatenate(left, axis=1), right_side(w_ref), preferred_element_type=f32)
    weight_sum = total_weight(weight)
    packed = [extra_in[0], extra_in[1]]
    for row, x in enumerate(OUTER):
        new = stepped(end[row], flux[DZ * row : DZ * row + DZ], move[x], gain[x], weight_sum)
        out[row] = new
        if not last:
            out_high[row], out_low[row] = split(new)
            packed[x // 16] = add_to_pack(packed[x // 16], new, x)
    if last:
        extra[...] = extra_in[...]
        depth_sums(out, sums, extra, 0, 3, 0)
        depth_sums(out, sums, extra, DX - 3, 3, 3)
    else:
        for group in range(2):
            extra[group] = packed[group]
        fill_slabs(lambda row: out[row], up, down)


def depth_tables(blocks):
    stiff = 3.0 * DZ * DZ
    count = DZ * blocks
    diagonal = np.full(count, 1.0 + 2.0 * stiff)
    diagonal[0] = diagonal[-1] = 1.0 + stiff
    fore = diagonal.copy()
    for i in range(1, count):
        fore[i] = diagonal[i] - stiff * stiff / fore[i - 1]
    back = diagonal.copy()
    for i in range(count - 2, -1, -1):
        back[i] = diagonal[i] - stiff * stiff / back[i + 1]
    sums = np.zeros((blocks, 2 * DZ))
    solve = np.zeros((blocks, 2 * DZ + 2 * blocks))
    for block in range(blocks):
        start, end = block * DZ, block * DZ + DZ - 1
        for z in range(DZ):
            sums[block, z] = np.prod(stiff / fore[start + z : end])
            sums[block, DZ + z] = np.prod(stiff / back[start + 1 : start + z + 1])
            solve[block, z] = stiff / fore[start + z - 1] if start + z else 0.0
            solve[block, DZ + z] = 1.0 / fore[start + z]
        if block < blocks - 1:
            solve[block, 2 * DZ - 1] = 1.0 / (fore[end] - stiff * stiff / back[end + 1])
        for other in range(blocks):
            if other < block:
                solve[block, 2 * DZ + other] = np.prod(stiff / fore[other * DZ + DZ - 1 : start])
            if other > block:
                solve[block, 2 * DZ + blocks + other] = np.prod(stiff / back[end + 1 : other * DZ + 1])
    return jnp.asarray(sums, f32), jnp.asarray(solve, f32)


def depth_kernel(blocks, mid, end, every, solve, out, buf, sweep, out_sem):
    for row, x in enumerate(OUTER):
        buf[:, x, :] = end[row]
    for row in range(INNER):
        buf[:, 3 + row, :] = mid[row]
    own = lax.axis_index("gz")
    stiff = 3.0 * DZ * DZ
    above = jnp.zeros((DX, DY), f32)
    below = jnp.zeros((DX, DY), f32)
    for block in range(blocks):
        above = above + solve[own, 2 * DZ + block] * every[block, 0]
        below = below + solve[own, 2 * DZ + blocks + block] * every[block, 1]
    value = above
    for z in range(DZ):
        carried = value if z == 0 else solve[own, z] * value
        value = buf[z] + carried
        sweep[z] = value
    value = (value + below) * solve[own, 2 * DZ - 1]
    for z in range(DZ - 1, -1, -1):
        if z < DZ - 1:
            value = (sweep[z] + stiff * value) * solve[own, DZ + z]
        sweep[z] = 2.0 * value - buf[z]
        if z % 16 == 0:
            part = pl.ds(z, 16)
            pltpu.make_async_copy(sweep.at[part], out.at[part], out_sem.at[z // 16]).start()
    for z in range(0, DZ, 16):
        part = pl.ds(z, 16)
        pltpu.make_async_copy(sweep.at[part], out.at[part], out_sem.at[z // 16]).wait()


def shift(value, axis, step):
    count = lax.axis_size(axis)
    return lax.ppermute(value, axis, [(i, (i + step) % count) for i in range(count)])


def local(conc, pit, phase, offsets, damage, weight, diffusivity, rate):
    blocks = lax.axis_size("gz")
    sums, solve = depth_tables(blocks)
    *parts, pack, up, down = call(
        first_kernel, "first", PARTS + (PACK, SLABS, SLABS), [HBM], (VMEM,) * 9,
        [pltpu.VMEM((DX, DZ, DY), f32), SEM((4,))], nbytes=4 << 20, limit=50,
    )(conc)
    w, move, gain = call(
        prepare_kernel, "prepare", (struct(15, DY, DY, dtype=bf16), WHOLE, WHOLE),
        [SMEM] * 4 + [HBM] * 3, (VMEM,) * 3,
        [pltpu.SMEM((64,), f32)] + [pltpu.VMEM((DX, DZ, DY), jnp.int32)] * 3 + [SEM((4,))],
        nbytes=8 << 20, limit=47,
    )(offsets.T, weight, diffusivity, rate, pit, phase, damage)
    for substep in range(2):
        last = substep == 1
        left, right = shift(pack, "gy", 1), shift(pack, "gy", -1)
        halo, up, down = call(
            join_kernel, "join", (PACK, SLABS, SLABS), [VMEM] * 4, (VMEM,) * 3,
        )(left, right, up, down)
        from_low, from_high = shift(up, "gx", 1), shift(down, "gx", -1)
        mid, end, mid_high, end_high, mid_low, end_low = parts
        extra = struct(2, DX, DY) if last else PACK
        tiny = struct(1, 16, 128, dtype=bf16)
        inner_split = (tiny, tiny) if last else (PARTS[2], PARTS[4])
        new_mid, new_mid_high, new_mid_low, more = call(
            functools.partial(inner_kernel, last), f"inner{substep}", (PARTS[0],) + inner_split + (extra,),
            [VMEM] * 9 + [SMEM] * 2, (VMEM,) * 4, [pltpu.VMEM((INNER, DZ, DY), bf16)],
            flops=2 * INNER * DZ * DY * 5632, nbytes=12 << 20,
        )(mid, mid_high, end_high, mid_low, end_low, halo, move, gain, w, weight, sums)
        outs = call(
            functools.partial(outer_kernel, last), f"outer{substep}",
            (PARTS[1],) + ((extra,) if last else (PARTS[3], PARTS[5], PACK, SLABS, SLABS)),
            [VMEM] * 11 + [SMEM] * 2 + [VMEM], (VMEM,) * (2 if last else 6),
            flops=2 * 6 * DZ * DY * 5632, nbytes=6 << 20,
        )(end, mid_high, end_high, mid_low, end_low, halo, from_low, from_high, move, gain, w, weight, sums, more)
        if last:
            new_end, ends = outs
        else:
            new_end, new_end_high, new_end_low, pack, up, down = outs
            parts = [new_mid, new_end, new_mid_high, new_end_high, new_mid_low, new_end_low]
    every = lax.all_gather(ends, "gz", axis=0)
    return call(
        functools.partial(depth_kernel, blocks), "depth", struct(DZ, DX, DY),
        [VMEM, VMEM, VMEM, SMEM], HBM,
        [pltpu.VMEM((DZ, DX, DY), f32), pltpu.VMEM((DZ, DX, DY), f32), SEM((4,))], nbytes=6 << 20,
    )(new_mid, new_end, every, solve)


def solution(mesh):
    block = P("gz", "gx", "gy")
    in_specs = (block, block, block, P(), block, P(), P(), P())
    return jax.shard_map(local, mesh=mesh, in_specs=in_specs, out_specs=block, check_vma=False)
```

time: 83.2 us -> 61.3 us (0.74)
  Pallas kernels: 46.6 us -> 28.9 us
  local copies, waits for them, and re-layouts: 4.44 us -> 0.04 us
  starting transfers between devices: 15.5 us -> 16.9 us
  waiting for transfers between devices: 5.56 us -> 4.34 us
    pallas_call x8, Pallas kernels: 43.1 us -> 25.6 us  [the longest x2 13.4 us: local(): call(functools.partial(inner_kernel, last), f'inner{substep}', (PARTS[0],...]
    unnamed x19 -> x14, local copies, waits for them, and re-layouts: 4.34 us -> 0.04 us
    ppermute x8, starting transfers between devices: 15.5 us -> 16.9 us  [shift(): lax.ppermute(value, axis, [(i, (i + step) % count) for i in range(count)])]
    ppermute x8, waiting for transfers between devices: 5.56 us -> 4.34 us  [shift(): lax.ppermute(value, axis, [(i, (i + step) % count) for i in range(count)])]
  transfers between devices with their start and end apart: 8 -> 8, of which waited for: 3 -> 2; matrix products, arithmetic and copies ran while one was open for 0% -> 0% of each run, Pallas kernels for 38% -> 30%
where the time goes in v2:
time: 61.3 us; the launch traced here: 61.1 us
  Pallas kernels  28.9 us (47%)
  starting transfers between devices  16.9 us (28%)
  blocking collectives  10.6 us (17%)
  waiting for transfers between devices  4.34 us (7%)
    ppermute x8, starting transfers between devices, shift(): lax.ppermute(value, axis, [(i, (i + step) % count) for i in range(count)])  16.9 us
    pallas_call x2, Pallas kernels, local(): call(functools.partial(inner_kernel, last), f'inner{substep}', (PARTS[0],...  13.4 us
    all_gather x1, blocking collectives, local(): every = lax.all_gather(ends, 'gz', axis=0)  10.6 us
    pallas_call x1, Pallas kernels, local(): call(prepare_kernel, 'prepare', (struct(15, DY, DY, dtype=bf16), WHOLE, W...  4.62 us
    ppermute x8, waiting for transfers between devices, shift(): lax.ppermute(value, axis, [(i, (i + step) % count) for i in range(count)])  4.34 us
    pallas_call x2, Pallas kernels, local(): call(functools.partial(outer_kernel, last), f'outer{substep}', (PARTS[1],...  4.24 us
    pallas_call x1, Pallas kernels, local(): call(functools.partial(depth_kernel, blocks), 'depth', struct(DZ, DX, DY)...  3.33 us
    pallas_call x1, Pallas kernels, local(): call(first_kernel, 'first', PARTS + (PACK, SLABS, SLABS), [HBM], (VMEM,)...  3.24 us
  transfers between devices with their start and end apart: 8, of which 2 were waited for; matrix products, arithmetic and copies ran while one was open for 0% of the time, Pallas kernels for 30%

profile of v2, /device:TPU:1, one launch (start us, length us, event | category | flops | bytes accessed | tf_op | source)
XLA Modules:
  0.0 61.1 jit_solution(8986193900726732682)
XLA Ops:
  0.0 0.0 copy-start.1
  0.0 0.0 copy-start.5
  0.0 0.0 copy-start.4
  0.0 0.0 copy-start.3
  0.0 3.2 %first.1 = (f32[26,64,256]{2,1,0:T(8,128)}, f32[6,64,256]{2,1,0:T(8,128)S(1)}, bf16[26,64,256]{2,1,0:T(8,128)(2,1)S(1)}, bf16[6,64,256]{2,1,0:T(8,128)(2,1)S(1)}...) custom-call(f32[64,32,256]{2,1,0:T(8,128)} %conc.1), custom_call_target="tpu_custom_call" | custom-call | bytes 4194304 | tf_op jit(solution)/shard_map/first/pallas_call | solution.py:364
  3.3 3.6 %collective-permute-start.1 = (f32[2,64,128]{2,1,0:T(8,128)S(1)}, f32[2,64,128]{2,1,0:T(8,128)S(1)}, u32[]{:S(2)}, u32[]{:S(2)}) collective-permute-start(f32[2,64,128]{2,1,0:T(8,128)S(1)} %get-tuple-element.42), channel_id=1, source_target_pairs={{0,12},{4,0},{8,4},{12,8},{1,13},{5,1},{9,5},{13,9},{2,14},{6,2},{... | collective-permute-start | bytes 196616 | tf_op jit(solution)/shard_map/ppermute | solution.py:358
  6.9 0.0 collective-permute-start
  6.9 0.0 copy-done.1
  6.9 0.0 copy-done.5
  6.9 0.0 copy-done.4
  6.9 0.0 copy-done.3
  6.9 0.0 copy-start
  6.9 0.0 copy-start.6
  6.9 4.6 %prepare.1 = (bf16[15,256,256]{2,1,0:T(8,128)(2,1)S(1)}, f32[32,64,256]{2,1,0:T(8,128)S(1)}, f32[32,64,256]{2,1,0:T(8,128)S(1)}) custom-call(s32[2,28]{1,0:T(2,128)S(1)} %bitcast.3, f32[28]{0:T(128)S(1)} %copy-done.1, f32[4]{0:T(128)S(1)} %copy-done.4, f32[4]{0:T(128)S(1)} %copy-done.5, s32[64,32,256]{2,1,0:T(8,128)} %pit.1, s32[64,32,256]{2,1,0:T(8,128)} %phase.1, ...), custom_call_target="tpu_custom_call" | custom-call | bytes 8388608 | tf_op jit(solution)/shard_map/prepare/pallas_call | solution.py:368
  11.6 0.0 collective-permute-done.1.right
  11.6 0.0 collective-permute-done.left
  11.7 1.7 %collective-permute-start.2 = (f32[7,64,128]{2,1,0:T(8,128)S(1)}, f32[7,64,128]{2,1,0:T(8,128)S(1)}, u32[]{:S(2)}, u32[]{:S(2)}) collective-permute-start(f32[7,64,128]{2,1,0:T(8,128)S(1)} %get-tuple-element.52), channel_id=1, source_target_pairs={{0,16},{16,32},{32,48},{48,64},{64,80},{80,96},{96,112},{112,128},... | collective-permute-start | bytes 688136 | tf_op jit(solution)/shard_map/ppermute | solution.py:358
  13.4 5.0 %collective-permute-start.3 = (f32[7,64,128]{2,1,0:T(8,128)S(1)}, f32[7,64,128]{2,1,0:T(8,128)S(1)}, u32[]{:S(2)}, u32[]{:S(2)}) collective-permute-start(f32[7,64,128]{2,1,0:T(8,128)S(1)} %get-tuple-element.53), channel_id=1, source_target_pairs={{0,240},{16,0},{32,16},{48,32},{64,48},{80,64},{96,80},{112,96},{1... | collective-permute-start | bytes 688136 | tf_op jit(solution)/shard_map/ppermute | solution.py:358
  18.3 0.0 copy-done
  18.3 0.0 copy-done.6
  18.3 6.3 %inner0.1 = (f32[26,64,256]{2,1,0:T(8,128)S(1)}, bf16[26,64,256]{2,1,0:T(8,128)(2,1)S(1)}, bf16[26,64,256]{2,1,0:T(8,128)(2,1)S(1)}, f32[2,64,128]{2,1,0:T(8,128)S(1)}) custom-call(f32[26,64,256]{2,1,0:T(8,128)S(1)} %copy-done.6, bf16[26,64,256]{2,1,0:T(8,128)(2,1)S(1)} %get-tuple-element.38.mid_high, bf16[6,64,256]{2,1,0:T(8,128)(2,1)S(1)} %get-tuple-element.39.end_high, ...), custom_call_target="tpu_custom_call" | custom-call | flops 4798283776 | bytes 12582912 | tf_op jit(solution)/shard_map/inner0/pallas_call | solution.py:385
  24.6 0.0 collective-permute-done.2.from_low
  24.6 0.0 collective-permute-done.3.from_high
  24.6 2.0 %outer0.1 = (f32[6,64,256]{2,1,0:T(8,128)S(1)}, bf16[6,64,256]{2,1,0:T(8,128)(2,1)S(1)}, bf16[6,64,256]{2,1,0:T(8,128)(2,1)S(1)}, f32[2,64,128]{2,1,0:T(8,128)S(...) custom-call(f32[6,64,256]{2,1,0:T(8,128)S(1)} %get-tuple-element.51.end, ...), custom_call_target="tpu_custom_call" | custom-call | flops 1107296256 | bytes 6291456 | tf_op jit(solution)/shard_map/outer0/pallas_call | solution.py:390
  26.6 2.7 %collective-permute-start.5 = (f32[2,64,128]{2,1,0:T(8,128)S(1)}, f32[2,64,128]{2,1,0:T(8,128)S(1)}, u32[]{:S(2)}, u32[]{:S(2)}) collective-permute-start(f32[2,64,128]{2,1,0:T(8,128)S(1)} %get-tuple-element.58), channel_id=1, source_target_pairs={{0,12},{4,0},{8,4},{12,8},{1,13},{5,1},{9,5},{13,9},{2,14},{6,2},{... | collective-permute-start | bytes 196616 | tf_op jit(solution)/shard_map/ppermute | solution.py:358
  29.4 0.0 collective-permute-start.4
  29.4 1.3 %collective-permute-done.5.right = f32[2,64,128]{2,1,0:T(8,128)S(1)} collective-permute-done((f32[2,64,128]{2,1,0:T(8,128)S(1)}, f32[2,64,128]{2,1,0:T(8,128)S(1)}, u32[]{:S(2)}, u32[]{:S(2)}) %collective-permute-start.5) | collective-permute-done | bytes 65568 | tf_op jit(solution)/shard_map/ppermute | solution.py:358
  30.7 3.0 %collective-permute-done.4.left = f32[2,64,128]{2,1,0:T(8,128)S(1)} collective-permute-done((f32[2,64,128]{2,1,0:T(8,128)S(1)}, f32[2,64,128]{2,1,0:T(8,128)S(1)}, u32[]{:S(2)}, u32[]{:S(2)}) %collective-permute-start.4) | collective-permute-done | bytes 65568 | tf_op jit(solution)/shard_map/ppermute | solution.py:358
  33.7 0.3 collective-permute-start.6
  34.0 3.6 %collective-permute-start.7 = (f32[7,64,128]{2,1,0:T(8,128)S(1)}, f32[7,64,128]{2,1,0:T(8,128)S(1)}, u32[]{:S(2)}, u32[]{:S(2)}) collective-permute-start(f32[7,64,128]{2,1,0:T(8,128)S(1)} %get-tuple-element.65), channel_id=1, source_target_pairs={{0,240},{16,0},{32,16},{48,32},{64,48},{80,64},{96,80},{112,96},{1... | collective-permute-start | bytes 688136 | tf_op jit(solution)/shard_map/ppermute | solution.py:358
  37.6 7.1 %inner1.1 = (f32[26,64,256]{2,1,0:T(8,128)S(1)}, bf16[1,16,128]{2,1,0:T(8,128)(2,1)}, bf16[1,16,128]{2,1,0:T(8,128)(2,1)}, f32[2,32,256]{2,1,0:T(8,128)S(1)}) custom-call(f32[26,64,256]{2,1,0:T(8,128)S(1)} %get-tuple-element.49.mid, bf16[26,64,256]{2,1,0:T(8,128)(2,1)S(1)} %get-tuple-element.50.mid_high, bf16[6,64,256]{2,1,0:T(8,128)(2,1)S(1)} %get-tuple-element.55.end_high, ...), custom_call_target="tpu_custom_call" | custom-call | flops 4798283776 | bytes 12582912 | tf_op jit(solution)/shard_map/inner1/pallas_call | solution.py:385
  44.7 0.0 collective-permute-done.6.from_low
  44.7 0.0 collective-permute-done.7.from_high
  44.7 0.0 copy-start.2
  44.7 2.3 %outer1.1 = (f32[6,64,256]{2,1,0:T(8,128)S(1)}, f32[2,32,256]{2,1,0:T(8,128)S(1)}) custom-call(f32[6,64,256]{2,1,0:T(8,128)S(1)} %get-tuple-element.63.end, bf16[26,64,256]{2,1,0:T(8,128)(2,1)S(1)} %get-tuple-element.50.mid_high, bf16[6,64,256]{2,1,0:T(8,128)(2,1)S(1)} %get-tuple-element.55.end_high, bf16[26,64,256]{2,1,0:T(8,128)(2,1)S(1)} %get-tuple-element.56.mid_low, ...), custom_call_target="tpu_custom_call" | custom-call | flops 1107296256 | bytes 6291456 | tf_op jit(solution)/shard_map/outer1/pallas_call | solution.py:390
  47.0 10.6 %all-gather = f32[8,32,256]{2,1,0:T(8,128)S(1)} all-gather(f32[2,32,256]{2,1,0:T(8,128)S(1)} %get-tuple-element.68), channel_id=2, replica_groups=mesh['gx'=16,'gy'=4,'gz'=4] {'gz'}, dimensions={0}, use_global_device_ids=true | all-gather | bytes 327680 | tf_op jit(solution)/shard_map/all_gather | solution.py:401
  57.6 0.0 copy-done.2
  57.6 3.3 %depth.1 = f32[64,32,256]{2,1,0:T(8,128)} custom-call(f32[26,64,256]{2,1,0:T(8,128)S(1)} %get-tuple-element.62.mid, f32[6,64,256]{2,1,0:T(8,128)S(1)} %get-tuple-element.67.end, f32[4,2,32,256]{3,2,1,0:T(8,128)S(1)} %bitcast.2, f32[4,136]{1,0:T(4,128)S(1)} %copy-done.2), custom_call_target="tpu_custom_call" | custom-call | bytes 6291456 | tf_op jit(solution)/shard_map/depth/pallas_call | solution.py:402
  (2 shorter events, 0.1 us)
Async XLA Ops:
  0.0 6.9 %copy-start.1 = (f32[28]{0:T(128)S(1)}, f32[28]{0:T(128)}, u32[]{:S(2)}) copy-start(f32[28]{0:T(128)} %weight.9) | copy-start | bytes 340
  0.0 6.9 %copy-start.5 = (f32[4]{0:T(128)S(1)}, f32[4]{0:T(128)}, u32[]{:S(2)}) copy-start(f32[4]{0:T(128)} %rate.1) | copy-start | bytes 52
  0.0 6.9 %copy-start.4 = (f32[4]{0:T(128)S(1)}, f32[4]{0:T(128)}, u32[]{:S(2)}) copy-start(f32[4]{0:T(128)} %diffusivity.1) | copy-start | bytes 52
  0.0 6.9 %copy-start.3 = (s32[28,2]{0,1:T(2,128)S(1)}, s32[28,2]{0,1:T(2,128)}, u32[]{:S(2)}) copy-start(s32[28,2]{0,1:T(2,128)} %param.13) | copy-start | bytes 676
  3.3 8.3 %collective-permute-start.1 = (f32[2,64,128]{2,1,0:T(8,128)S(1)}, f32[2,64,128]{2,1,0:T(8,128)S(1)}, u32[]{:S(2)}, u32[]{:S(2)}) collective-permute-start(f32[2,64,128]{2,1,0:T(8,128)S(1)} %get-tuple-element.42), channel_id=1, source_target_pairs={{0,12},{4,0},{8,4},{12,8},{1,13},{5,1},{9,5},{13,9},{2,14},{6,2},{... | collective-permute-start | bytes 196616 | tf_op jit(solution)/shard_map/ppermute | solution.py:358
  6.9 4.7 %collective-permute-start = (f32[2,64,128]{2,1,0:T(8,128)S(1)}, f32[2,64,128]{2,1,0:T(8,128)S(1)}, u32[]{:S(2)}, u32[]{:S(2)}) collective-permute-start(f32[2,64,128]{2,1,0:T(8,128)S(1)} %get-tuple-element.42), channel_id=1, source_target_pairs={{0,4},{4,8},{8,12},{12,0},{1,5},{5,9},{9,13},{13,1},{2,6},{6,10},{... | collective-permute-start | bytes 196616 | tf_op jit(solution)/shard_map/ppermute | solution.py:358
  6.9 11.4 %copy-start = (f32[4,128]{1,0:T(4,128)S(1)}, f32[4,128]{1,0:T(4,128)}, u32[]{:S(2)}) copy-start(f32[4,128]{1,0:T(4,128)} %constant.4.clone.sums) | copy-start | bytes 6148
  6.9 11.4 %copy-start.6 = (f32[26,64,256]{2,1,0:T(8,128)S(1)}, f32[26,64,256]{2,1,0:T(8,128)}, u32[]{:S(2)}) copy-start(f32[26,64,256]{2,1,0:T(8,128)} %get-tuple-element.37.mid) | copy-start | bytes 5111812
  11.7 13.0 %collective-permute-start.2 = (f32[7,64,128]{2,1,0:T(8,128)S(1)}, f32[7,64,128]{2,1,0:T(8,128)S(1)}, u32[]{:S(2)}, u32[]{:S(2)}) collective-permute-start(f32[7,64,128]{2,1,0:T(8,128)S(1)} %get-tuple-element.52), channel_id=1, source_target_pairs={{0,16},{16,32},{32,48},{48,64},{64,80},{80,96},{96,112},{112,128},... | collective-permute-start | bytes 688136 | tf_op jit(solution)/shard_map/ppermute | solution.py:358
  13.4 11.3 %collective-permute-start.3 = (f32[7,64,128]{2,1,0:T(8,128)S(1)}, f32[7,64,128]{2,1,0:T(8,128)S(1)}, u32[]{:S(2)}, u32[]{:S(2)}) collective-permute-start(f32[7,64,128]{2,1,0:T(8,128)S(1)} %get-tuple-element.53), channel_id=1, source_target_pairs={{0,240},{16,0},{32,16},{48,32},{64,48},{80,64},{96,80},{112,96},{1... | collective-permute-start | bytes 688136 | tf_op jit(solution)/shard_map/ppermute | solution.py:358
  26.6 4.1 %collective-permute-start.5 = (f32[2,64,128]{2,1,0:T(8,128)S(1)}, f32[2,64,128]{2,1,0:T(8,128)S(1)}, u32[]{:S(2)}, u32[]{:S(2)}) collective-permute-start(f32[2,64,128]{2,1,0:T(8,128)S(1)} %get-tuple-element.58), channel_id=1, source_target_pairs={{0,12},{4,0},{8,4},{12,8},{1,13},{5,1},{9,5},{13,9},{2,14},{6,2},{... | collective-permute-start | bytes 196616 | tf_op jit(solution)/shard_map/ppermute | solution.py:358
  29.4 4.3 %collective-permute-start.4 = (f32[2,64,128]{2,1,0:T(8,128)S(1)}, f32[2,64,128]{2,1,0:T(8,128)S(1)}, u32[]{:S(2)}, u32[]{:S(2)}) collective-permute-start(f32[2,64,128]{2,1,0:T(8,128)S(1)} %get-tuple-element.58), channel_id=1, source_target_pairs={{0,4},{4,8},{8,12},{12,0},{1,5},{5,9},{9,13},{13,1},{2,6},{6,10},{... | collective-permute-start | bytes 196616 | tf_op jit(solution)/shard_map/ppermute | solution.py:358
  33.7 11.0 %collective-permute-start.6 = (f32[7,64,128]{2,1,0:T(8,128)S(1)}, f32[7,64,128]{2,1,0:T(8,128)S(1)}, u32[]{:S(2)}, u32[]{:S(2)}) collective-permute-start(f32[7,64,128]{2,1,0:T(8,128)S(1)} %get-tuple-element.64), channel_id=1, source_target_pairs={{0,16},{16,32},{32,48},{48,64},{64,80},{80,96},{96,112},{112,128},... | collective-permute-start | bytes 688136 | tf_op jit(solution)/shard_map/ppermute | solution.py:358
  34.0 10.7 %collective-permute-start.7 = (f32[7,64,128]{2,1,0:T(8,128)S(1)}, f32[7,64,128]{2,1,0:T(8,128)S(1)}, u32[]{:S(2)}, u32[]{:S(2)}) collective-permute-start(f32[7,64,128]{2,1,0:T(8,128)S(1)} %get-tuple-element.65), channel_id=1, source_target_pairs={{0,240},{16,0},{32,16},{48,32},{64,48},{80,64},{96,80},{112,96},{1... | collective-permute-start | bytes 688136 | tf_op jit(solution)/shard_map/ppermute | solution.py:358
  44.7 12.9 %copy-start.2 = (f32[4,136]{1,0:T(4,128)S(1)}, f32[4,136]{1,0:T(4,128)}, u32[]{:S(2)}) copy-start(f32[4,136]{1,0:T(4,128)} %constant.5.clone.solve) | copy-start | bytes 6532

commit v3 on v2

--- a/solution.py
+++ b/solution.py
@@ -49,13 +49,14 @@
     return lax.broadcasted_iota(jnp.int32, (DZ, 128), 1)
 
 
-def add_to_pack(pack, row, x):
-    slot = 8 * (x % 16)
+def at_lanes(pack, row, source, target, count):
     lane = lanes()
-    last = pltpu.roll(row[:, 128:], (slot + 3) % 128, 1)
-    first = pltpu.roll(row[:, :128], (slot + 4) % 128, 1)
-    pack = jnp.where((lane >= slot) & (lane < slot + 3), last, pack)
-    return jnp.where((lane >= slot + 4) & (lane < slot + 7), first, pack)
+    moved = pltpu.roll(row, (target - source) % 128, 1)
+    return jnp.where((lane >= target) & (lane < target + count), moved, pack)
+
+
+def two_sides(left, right):
+    return jnp.where(lanes() % 8 < 4, left, right)
 
 
 def split(value):
@@ -79,7 +80,7 @@
     return total
 
 
-def prepare_kernel(offsets, weight, diffusivity, rate, pit, phase, damage, w_ref, move, gain, table, pv, hv, dv, sem):
+def prepare_kernel(offsets, weight, diffusivity, rate, pit, phase, damage, w_ref, move, gain, table, to_high, to_low, pv, hv, dv, sem):
     def copies(group):
         return [
             pltpu.make_async_copy(source.at[:, x, :], target.at[x], sem.at[group])
@@ -131,6 +132,17 @@
             move[x] = look(ids, diffusivity, lateral_step) * (1.0 + 0.5 * dv[x].astype(f32))
             gain[x] = look(ids, rate, dissolve_step) * pv[x].astype(f32)
 
+        if group % 2 == 0:
+            high, low = jnp.zeros((DZ, 128), f32), jnp.zeros((DZ, 128), f32)
+        for x in range(8 * group, 8 * group + 8):
+            slot = 8 * (x % 16)
+            high = at_lanes(high, move[x, :, 128:], 125, slot, 3)
+            high = at_lanes(high, gain[x, :, 128:], 125, slot + 4, 3)
+            low = at_lanes(low, gain[x, :, :128], 0, slot, 3)
+            low = at_lanes(low, move[x, :, :128], 0, slot + 4, 3)
+        if group % 2:
+            to_high[group // 2], to_low[group // 2] = high, low
+
 
 def right_side(w_ref):
     bands = [w_ref[a] for a in range(7)]
@@ -145,14 +157,14 @@
     return center + move * (flux - weight_sum * center) + gain * (1.0 - center)
 
 
-def first_kernel(conc, mid, end, mid_high, end_high, mid_low, end_low, pack, up, down, buf, sem):
+def first_kernel(conc, mid, end, mid_high, end_high, mid_low, end_low, lasts, firsts, up, down, buf, sem):
     for x in range(DX):
         pltpu.make_async_copy(conc.at[:, x, :], buf.at[x], sem.at[x // 8]).start()
     for group in range(4):
         for x in range(8 * group, 8 * group + 8):
             pltpu.make_async_copy(conc.at[:, x, :], buf.at[x], sem.at[group]).wait()
         if group % 2 == 0:
-            packed = jnp.zeros((DZ, 128), f32)
+            high_side, low_side = jnp.zeros((DZ, 128), f32), jnp.zeros((DZ, 128), f32)
         for x in range(8 * group, 8 * group + 8):
             row = buf[x]
             high, low = split(row)
@@ -161,10 +173,14 @@
                 end[place], end_high[place], end_low[place] = row, high, low
             else:
                 mid[x - 3], mid_high[x - 3], mid_low[x - 3] = row, high, low
-            packed = add_to_pack(packed, row, x)
+            slot = 8 * (x % 16)
+            high_side = at_lanes(high_side, row[:, 128:], 122, slot, 6)
+            low_side = at_lanes(low_side, row[:, :128], 0, slot, 6)
         if group % 2:
-            pack[group // 2] = packed
+            lasts[group // 2], firsts[group // 2] = high_side, low_side
     fill_slabs(lambda row: buf[OUTER[row]], up, down)
+    down[6] = jnp.zeros((DZ, 128), f32)
+    up[6] = jnp.zeros((DZ, 128), f32)
 
 
 def fill_slabs(row_of, up, down):
@@ -173,19 +189,67 @@
             part = slice(128 * half, 128 * half + 128)
             down[2 * row + half] = row_of(row)[:, part]
             up[2 * row + half] = row_of(3 + row)[:, part]
-    down[6] = jnp.zeros((DZ, 128), f32)
-    up[6] = jnp.zeros((DZ, 128), f32)
-
-
-def join_kernel(left, right, up_in, down_in, halo, up, down):
-    lane = lanes()
+
+
+def join_kernel(left, right, lasts, firsts, up_in, down_in, strips, up, down):
     for group in range(2):
-        halo[group] = jnp.where(lane % 8 < 4, left[group], right[group])
+        strips[0, group] = two_sides(left[group], pltpu.roll(lasts[group], 1, 1))
+        strips[1, group] = two_sides(pltpu.roll(left[group], 125, 1), pltpu.roll(right[group], 4, 1))
+        strips[2, group] = two_sides(firsts[group], pltpu.roll(right[group], 1, 1))
     for slab in range(6):
         up[slab] = up_in[slab]
         down[slab] = down_in[slab]
-    up[6] = halo[1]
-    down[6] = halo[0]
+    lane = lanes()
+    up[6] = jnp.where(
+        lane >= 104, strips[1, 1],
+        jnp.where(lane >= 72, pltpu.roll(strips[0, 1], 96, 1), pltpu.roll(strips[2, 1], 64, 1)),
+    )
+    down[6] = jnp.where(
+        lane < 32, strips[1, 0],
+        jnp.where(lane < 64, pltpu.roll(strips[0, 0], 32, 1), pltpu.roll(strips[2, 0], 64, 1)),
+    )
+
+
+def strip_taps(table, first, second, third):
+    place = lanes() % 4
+
+    def moved(value, step):
+        return pltpu.roll(value, step % 128, 1)
+
+    columns = [
+        first,
+        jnp.where(place < 2, moved(first, -1), moved(second, 2)),
+        jnp.where(place < 1, moved(first, -2), moved(second, 1)),
+        second,
+        jnp.where(place < 2, moved(second, -1), moved(third, 2)),
+        jnp.where(place < 1, moved(second, -2), moved(third, 1)),
+        third,
+    ]
+    sums = []
+    for a in range(7):
+        total = table[7 * a] * columns[0]
+        for second_index in range(1, 7):
+            total = total + table[7 * a + second_index] * columns[second_index]
+        sums.append(total)
+    return sums
+
+
+def strip_flux(taps, group):
+    lane = lanes()
+    total = jnp.zeros((DZ, 128), f32)
+    zero = jnp.zeros((DZ, 128), f32)
+    for a in range(7):
+        step = 8 * (a - 3)
+        own, after, before = (
+            zero if taps[g] is None else taps[g][a] for g in (group, (group + 1) % 3, (group + 2) % 3)
+        )
+        if step == 0:
+            total = total + own
+        elif step > 0:
+            total = total + pltpu.roll(jnp.where(lane >= step, own, after), 128 - step, 1)
+        else:
+            total = total + pltpu.roll(jnp.where(lane < 128 + step, own, before), -step, 1)
+    return total
 
 
 CHUNK = INNER // 2
@@ -205,14 +269,14 @@
 
 
 def inner_kernel(
-    last, mid, mid_high, end_high, mid_low, end_low, halo, move, gain, w_ref, weight, sums,
+    last, mid, mid_high, end_high, mid_low, end_low, strips, move, gain, w_ref, weight, sums, table,
     out, out_high, out_low, extra, edges,
 ):
+    halo = strips.at[0 if last else 1]
     for x in range(3, DX - 3):
         group = (x + 13) // 16 - 1
         edges[x - 3] = edge_window(halo[group], halo[min(group + 1, 1)], x)
     weight_sum = total_weight(weight)
-    packed = [jnp.zeros((DZ, 128), f32)] * 2
     for chunk in range(2):
         start = CHUNK * chunk
         highs = [row_range(mid_high, end_high, start + a, CHUNK) for a in range(7)]
@@ -225,13 +289,13 @@
             out[row] = new
             if not last:
                 out_high[row], out_low[row] = split(new)
-                packed[x // 16] = add_to_pack(packed[x // 16], new, x)
     if last:
         extra[...] = jnp.zeros_like(extra)
         depth_sums(out, sums, extra, 3, INNER, 0)
     else:
+        taps = [strip_taps(table, strips[0, g], strips[1, g], strips[2, g]) for g in range(2)] + [None]
         for group in range(2):
-            extra[group] = packed[group]
+            extra[group] = strip_flux(taps, group)
 
 
 def depth_sums(rows, sums, extra, start, count, first):
@@ -247,13 +311,14 @@
 
 
 def outer_kernel(
-    last, end, mid_high, end_high, mid_low, end_low, halo, from_low, from_high, move, gain, w_ref, weight, sums,
-    extra_in, out, *rest,
+    last, end, mid_high, end_high, mid_low, end_low, strips, from_low, from_high, move, gain, w_ref, weight, sums,
+    extra_in, *rest,
 ):
     if last:
-        (extra,) = rest
+        out, extra = rest
     else:
-        out_high, out_low, extra, up, down = rest
+        table, coefs_left, coefs_right, out, out_high, out_low, extra, up, down = rest
+    halo = strips.at[0 if last else 1]
     groups = [from_low[6], halo[0], halo[1], from_high[6]]
     edges = []
     for x in OUTER:
@@ -276,21 +341,34 @@
     left = highs + lows + highs + [jnp.concatenate(edges, axis=0)]
     flux = jnp.dot(jnp.concatenate(left, axis=1), right_side(w_ref), preferred_element_type=f32)
     weight_sum = total_weight(weight)
-    packed = [extra_in[0], extra_in[1]]
     for row, x in enumerate(OUTER):
         new = stepped(end[row], flux[DZ * row : DZ * row + DZ], move[x], gain[x], weight_sum)
         out[row] = new
         if not last:
             out_high[row], out_low[row] = split(new)
-            packed[x // 16] = add_to_pack(packed[x // 16], new, x)
     if last:
         extra[...] = extra_in[...]
         depth_sums(out, sums, extra, 0, 3, 0)
         depth_sums(out, sums, extra, DX - 3, 3, 3)
     else:
+        fill_slabs(lambda row: out[row], up, down)
+        lane = lanes()
+        low, high = from_low[6], from_high[6]
+        beyond = [
+            jnp.where(lane < 64, pltpu.roll(high, 96, 1), pltpu.roll(low, 32, 1)),
+            jnp.where(lane < 64, high, low),
+            jnp.where(lane < 64, pltpu.roll(high, 64, 1), pltpu.roll(low, 64, 1)),
+        ]
+        taps = [None, None, strip_taps(table, *beyond)]
         for group in range(2):
-            extra[group] = packed[group]
-        fill_slabs(lambda row: out[row], up, down)
+            flux = extra_in[group] + strip_flux(taps, group)
+            left, right = coefs_left[group], coefs_right[group]
+            extra[0, group] = stepped(
+                halo[group], flux, two_sides(left, right),
+                two_sides(pltpu.roll(left, 124, 1), pltpu.roll(right, 4, 1)), weight_sum,
+            )
+        up[6] = extra[0, 1]
+        down[6] = extra[0, 0]
 
 
 def depth_tables(blocks):
@@ -361,42 +439,48 @@
 def local(conc, pit, phase, offsets, damage, weight, diffusivity, rate):
     blocks = lax.axis_size("gz")
     sums, solve = depth_tables(blocks)
-    *parts, pack, up, down = call(
-        first_kernel, "first", PARTS + (PACK, SLABS, SLABS), [HBM], (VMEM,) * 9,
+    *parts, lasts, firsts, up, down = call(
+        first_kernel, "first", PARTS + (PACK, PACK, SLABS, SLABS), [HBM], (VMEM,) * 10,
         [pltpu.VMEM((DX, DZ, DY), f32), SEM((4,))], nbytes=4 << 20, limit=50,
     )(conc)
-    w, move, gain = call(
-        prepare_kernel, "prepare", (struct(15, DY, DY, dtype=bf16), WHOLE, WHOLE),
-        [SMEM] * 4 + [HBM] * 3, (VMEM,) * 3,
-        [pltpu.SMEM((64,), f32)] + [pltpu.VMEM((DX, DZ, DY), jnp.int32)] * 3 + [SEM((4,))],
+    left, right = shift(lasts, "gy", 1), shift(firsts, "gy", -1)
+    w, move, gain, table, to_high, to_low = call(
+        prepare_kernel, "prepare", (struct(15, DY, DY, dtype=bf16), WHOLE, WHOLE, struct(64), PACK, PACK),
+        [SMEM] * 4 + [HBM] * 3, (VMEM, VMEM, VMEM, SMEM, VMEM, VMEM),
+        [pltpu.VMEM((DX, DZ, DY), jnp.int32)] * 3 + [SEM((4,))],
         nbytes=8 << 20, limit=47,
     )(offsets.T, weight, diffusivity, rate, pit, phase, damage)
+    strips, up, down = call(
+        join_kernel, "join", (struct(3, 2, DZ, 128), SLABS, SLABS), [VMEM] * 6, (VMEM,) * 3,
+    )(left, right, lasts, firsts, up, down)
     for substep in range(2):
         last = substep == 1
-        left, right = shift(pack, "gy", 1), shift(pack, "gy", -1)
-        halo, up, down = call(
-            join_kernel, "join", (PACK, SLABS, SLABS), [VMEM] * 4, (VMEM,) * 3,
-        )(left, right, up, down)
         from_low, from_high = shift(up, "gx", 1), shift(down, "gx", -1)
+        if not last:
+            to_high, to_low, up, down = lax.optimization_barrier((to_high, to_low, up, down))
+            coefs = [shift(to_high, "gy", 1), shift(to_low, "gy", -1)]
         mid, end, mid_high, end_high, mid_low, end_low = parts
-        extra = struct(2, DX, DY) if last else PACK
         tiny = struct(1, 16, 128, dtype=bf16)
         inner_split = (tiny, tiny) if last else (PARTS[2], PARTS[4])
         new_mid, new_mid_high, new_mid_low, more = call(
-            functools.partial(inner_kernel, last), f"inner{substep}", (PARTS[0],) + inner_split + (extra,),
-            [VMEM] * 9 + [SMEM] * 2, (VMEM,) * 4, [pltpu.VMEM((INNER, DZ, DY), bf16)],
+            functools.partial(inner_kernel, last), f"inner{substep}",
+            (PARTS[0],) + inner_split + ((struct(2, DX, DY) if last else PACK),),
+            [VMEM] * 9 + [SMEM] * 3, (VMEM,) * 4, [pltpu.VMEM((INNER, DZ, DY), bf16)],
             flops=2 * INNER * DZ * DY * 5632, nbytes=12 << 20,
-        )(mid, mid_high, end_high, mid_low, end_low, halo, move, gain, w, weight, sums)
-        outs = call(
-            functools.partial(outer_kernel, last), f"outer{substep}",
-            (PARTS[1],) + ((extra,) if last else (PARTS[3], PARTS[5], PACK, SLABS, SLABS)),
-            [VMEM] * 11 + [SMEM] * 2 + [VMEM], (VMEM,) * (2 if last else 6),
-            flops=2 * 6 * DZ * DY * 5632, nbytes=6 << 20,
-        )(end, mid_high, end_high, mid_low, end_low, halo, from_low, from_high, move, gain, w, weight, sums, more)
+        )(mid, mid_high, end_high, mid_low, end_low, strips, move, gain, w, weight, sums, table)
+        args = (end, mid_high, end_high, mid_low, end_low, strips, from_low, from_high, move, gain, w, weight, sums, more)
+        specs = [VMEM] * 11 + [SMEM] * 2 + [VMEM]
+        cost = dict(flops=2 * 6 * DZ * DY * 5632, nbytes=6 << 20)
         if last:
-            new_end, ends = outs
+            new_end, ends = call(
+                functools.partial(outer_kernel, last), "outer1", (PARTS[1], struct(2, DX, DY)), specs, (VMEM,) * 2, **cost
+            )(*args)
         else:
-            new_end, new_end_high, new_end_low, pack, up, down = outs
+            new_end, new_end_high, new_end_low, strips, up, down = call(
+                functools.partial(outer_kernel, last), "outer0",
+                (PARTS[1], PARTS[3], PARTS[5], struct(1, 2, DZ, 128), SLABS, SLABS),
+                specs + [SMEM, VMEM, VMEM], (VMEM,) * 6, **cost,
+            )(*args, table, *coefs)
             parts = [new_mid, new_end, new_mid_high, new_end_high, new_mid_low, new_end_low]
     every = lax.all_gather(ends, "gz", axis=0)
     return call(

time: 61.3 us -> 57 us (0.930)
  waiting for transfers between devices: 4.34 us -> 0.02 us
  Pallas kernels: 28.9 us -> 30.1 us
  blocking collectives: 10.6 us -> 9.62 us
    ppermute x8, waiting for transfers between devices: 4.34 us -> 0.02 us  [shift(): lax.ppermute(value, axis, [(i, (i + step) % count) for i in range(count)])]
    pallas_call x1, Pallas kernels: 4.62 us -> 5.88 us  [local(): call(prepare_kernel, 'prepare', (struct(15, DY, DY, dtype=bf16), WHOLE, W...]
    all_gather x1, blocking collectives: 10.6 us -> 9.62 us  [local(): every = lax.all_gather(ends, 'gz', axis=0)]
    pallas_call x5 -> x4, Pallas kernels: 7.55 us -> 7.66 us  [the longest x1 3.24 us: local(): call(first_kernel, 'first', PARTS + (PACK, PACK, SLABS, SLABS), [HBM], (V...]
  transfers between devices with their start and end apart: 8 -> 8, of which waited for: 2 -> 0; matrix products, arithmetic and copies ran while one was open for 0% -> 0% of each run, Pallas kernels for 30% -> 34%
where the time goes in v3:
time: 57 us; the launch traced here: 56.8 us
  Pallas kernels  30.1 us (53%)
  starting transfers between devices  16.7 us (29%)
  blocking collectives  9.62 us (17%)
    ppermute x8, starting transfers between devices, shift(): lax.ppermute(value, axis, [(i, (i + step) % count) for i in range(count)])  16.7 us
    pallas_call x2, Pallas kernels, local(): call(functools.partial(inner_kernel, last), f'inner{substep}', (PARTS[0],...  13.2 us
    all_gather x1, blocking collectives, local(): every = lax.all_gather(ends, 'gz', axis=0)  9.62 us
    pallas_call x1, Pallas kernels, local(): call(prepare_kernel, 'prepare', (struct(15, DY, DY, dtype=bf16), WHOLE, W...  5.88 us
    pallas_call x1, Pallas kernels, local(): call(functools.partial(depth_kernel, blocks), 'depth', struct(DZ, DX, DY)...  3.33 us
    pallas_call x1, Pallas kernels, local(): call(first_kernel, 'first', PARTS + (PACK, PACK, SLABS, SLABS), [HBM], (V...  3.24 us
    pallas_call x1, Pallas kernels, local(): call(functools.partial(outer_kernel, last), 'outer1', (PARTS[1], struct(2...  2.25 us
    pallas_call x1, Pallas kernels, local(): call(functools.partial(outer_kernel, last), 'outer0', (PARTS[1], PARTS[3]...  1.98 us
  transfers between devices with their start and end apart: 8, of which 0 were waited for; matrix products, arithmetic and copies ran while one was open for 0% of the time, Pallas kernels for 34%

profile of v3, /device:TPU:1, one launch (start us, length us, event | category | flops | bytes accessed | tf_op | source)
XLA Modules:
  0.0 56.8 jit_solution(13700443190123112640)
XLA Ops:
  0.0 0.0 copy-start.1
  0.0 0.0 copy-start.5
  0.0 0.0 copy-start.4
  0.0 0.0 copy-start.3
  0.0 3.2 %first.1 = (f32[26,64,256]{2,1,0:T(8,128)}, f32[6,64,256]{2,1,0:T(8,128)S(1)}, bf16[26,64,256]{2,1,0:T(8,128)(2,1)S(1)}, bf16[6,64,256]{2,1,0:T(8,128)(2,1)S(1)}...) custom-call(f32[64,32,256]{2,1,0:T(8,128)} %conc.1), custom_call_target="tpu_custom_call" | custom-call | bytes 4194304 | tf_op jit(solution)/shard_map/first/pallas_call | solution.py:442
  3.3 2.2 %collective-permute-start = (f32[2,64,128]{2,1,0:T(8,128)S(1)}, f32[2,64,128]{2,1,0:T(8,128)S(1)}, u32[]{:S(2)}, u32[]{:S(2)}) collective-permute-start(f32[2,64,128]{2,1,0:T(8,128)S(1)} %get-tuple-element.45.lasts), channel_id=1, source_target_pairs={{0,4},{4,8},{8,12},{12,0},{1,5},{5,9},{9,13},{13,1},{2,6},{6,10},{... | collective-permute-start | bytes 196616 | tf_op jit(solution)/shard_map/ppermute | solution.py:436
  5.5 1.5 %collective-permute-start.1 = (f32[2,64,128]{2,1,0:T(8,128)S(1)}, f32[2,64,128]{2,1,0:T(8,128)S(1)}, u32[]{:S(2)}, u32[]{:S(2)}) collective-permute-start(f32[2,64,128]{2,1,0:T(8,128)S(1)} %get-tuple-element.46.firsts), channel_id=1, source_target_pairs={{0,12},{4,0},{8,4},{12,8},{1,13},{5,1},{9,5},{13,9},{2,14},{6,2},{... | collective-permute-start | bytes 196616 | tf_op jit(solution)/shard_map/ppermute | solution.py:436
  7.0 0.0 copy-done.1
  7.0 0.0 copy-done.5
  7.0 0.0 copy-done.4
  7.0 0.0 copy-done.3
  7.0 0.0 copy-start
  7.0 0.0 copy-start.6
  7.0 5.9 %prepare.1 = (bf16[15,256,256]{2,1,0:T(8,128)(2,1)S(1)}, f32[32,64,256]{2,1,0:T(8,128)S(1)}, f32[32,64,256]{2,1,0:T(8,128)S(1)}, f32[64]{0:T(128)S(1)}, f32[2,64...) custom-call(s32[2,28]{1,0:T(2,128)S(1)} %bitcast.3, f32[28]{0:T(128)S(1)} %copy-done.1, f32[4]{0:T(128)S(1)} %copy-done.4, ...), custom_call_target="tpu_custom_call" | custom-call | bytes 8388608 | tf_op jit(solution)/shard_map/prepare/pallas_call | solution.py:447
  12.9 0.0 collective-permute-done.left
  12.9 0.0 collective-permute-done.1.right
  12.9 0.2 join.1
  13.1 1.7 %collective-permute-start.2 = (f32[7,64,128]{2,1,0:T(8,128)S(1)}, f32[7,64,128]{2,1,0:T(8,128)S(1)}, u32[]{:S(2)}, u32[]{:S(2)}) collective-permute-start(f32[7,64,128]{2,1,0:T(8,128)S(1)} %get-tuple-element.57), channel_id=1, source_target_pairs={{0,16},{16,32},{32,48},{48,64},{64,80},{80,96},{96,112},{112,128},... | collective-permute-start | bytes 688136 | tf_op jit(solution)/shard_map/ppermute | solution.py:436
  14.8 5.0 %collective-permute-start.3 = (f32[7,64,128]{2,1,0:T(8,128)S(1)}, f32[7,64,128]{2,1,0:T(8,128)S(1)}, u32[]{:S(2)}, u32[]{:S(2)}) collective-permute-start(f32[7,64,128]{2,1,0:T(8,128)S(1)} %get-tuple-element.58), channel_id=1, source_target_pairs={{0,240},{16,0},{32,16},{48,32},{64,48},{80,64},{96,80},{112,96},{1... | collective-permute-start | bytes 688136 | tf_op jit(solution)/shard_map/ppermute | solution.py:436
  19.8 0.0 collective-permute-start.4
  19.8 2.7 %collective-permute-start.5 = (f32[2,64,128]{2,1,0:T(8,128)S(1)}, f32[2,64,128]{2,1,0:T(8,128)S(1)}, u32[]{:S(2)}, u32[]{:S(2)}) collective-permute-start(f32[2,64,128]{2,1,0:T(8,128)S(1)} %get-tuple-element.63), channel_id=1, source_target_pairs={{0,12},{4,0},{8,4},{12,8},{1,13},{5,1},{9,5},{13,9},{2,14},{6,2},{... | collective-permute-start | bytes 196616 | tf_op jit(solution)/shard_map/ppermute | solution.py:436
  22.5 0.0 copy-done
  22.5 0.0 copy-done.6
  22.5 6.2 %inner0.1 = (f32[26,64,256]{2,1,0:T(8,128)S(1)}, bf16[26,64,256]{2,1,0:T(8,128)(2,1)S(1)}, bf16[26,64,256]{2,1,0:T(8,128)(2,1)S(1)}, f32[2,64,128]{2,1,0:T(8,128)S(1)}) custom-call(f32[26,64,256]{2,1,0:T(8,128)S(1)} %copy-done.6, bf16[26,64,256]{2,1,0:T(8,128)(2,1)S(1)} %get-tuple-element.41.mid_high, bf16[6,64,256]{2,1,0:T(8,128)(2,1)S(1)} %get-tuple-element.42.end_high, ...), custom_call_target="tpu_custom_call" | custom-call | flops 4798283776 | bytes 12582912 | tf_op jit(solution)/shard_map/inner0/pallas_call | solution.py:465
  28.7 0.0 collective-permute-done.4.rest_1_
  28.7 0.0 collective-permute-done.5.rest_2_
  28.7 0.0 collective-permute-done.2.from_low
  28.7 0.0 collective-permute-done.3.from_high
  28.7 2.0 %outer0.1 = (f32[6,64,256]{2,1,0:T(8,128)S(1)}, bf16[6,64,256]{2,1,0:T(8,128)(2,1)S(1)}, bf16[6,64,256]{2,1,0:T(8,128)(2,1)S(1)}, f32[1,2,64,128]{3,2,1,0:T(8,12...) custom-call(f32[6,64,256]{2,1,0:T(8,128)S(1)} %get-tuple-element.56.end, ...), custom_call_target="tpu_custom_call" | custom-call | flops 1107296256 | bytes 6291456 | tf_op jit(solution)/shard_map/outer0/pallas_call | solution.py:479
  30.7 0.1 collective-permute-start.6
  30.8 3.6 %collective-permute-start.7 = (f32[7,64,128]{2,1,0:T(8,128)S(1)}, f32[7,64,128]{2,1,0:T(8,128)S(1)}, u32[]{:S(2)}, u32[]{:S(2)}) collective-permute-start(f32[7,64,128]{2,1,0:T(8,128)S(1)} %get-tuple-element.71), channel_id=1, source_target_pairs={{0,240},{16,0},{32,16},{48,32},{64,48},{80,64},{96,80},{112,96},{1... | collective-permute-start | bytes 688136 | tf_op jit(solution)/shard_map/ppermute | solution.py:436
  34.3 7.0 %inner1.1 = (f32[26,64,256]{2,1,0:T(8,128)S(1)}, bf16[1,16,128]{2,1,0:T(8,128)(2,1)}, bf16[1,16,128]{2,1,0:T(8,128)(2,1)}, f32[2,32,256]{2,1,0:T(8,128)S(1)}) custom-call(f32[26,64,256]{2,1,0:T(8,128)S(1)} %get-tuple-element.54.mid, bf16[26,64,256]{2,1,0:T(8,128)(2,1)S(1)} %get-tuple-element.55.mid_high, bf16[6,64,256]{2,1,0:T(8,128)(2,1)S(1)} %get-tuple-element.64.end_high, ...), custom_call_target="tpu_custom_call" | custom-call | flops 4798283776 | bytes 12582912 | tf_op jit(solution)/shard_map/inner1/pallas_call | solution.py:465
  41.4 0.0 collective-permute-done.6.from_low
  41.4 0.0 collective-permute-done.7.from_high
  41.4 0.0 copy-start.2
  41.4 2.2 %outer1.1 = (f32[6,64,256]{2,1,0:T(8,128)S(1)}, f32[2,32,256]{2,1,0:T(8,128)S(1)}) custom-call(f32[6,64,256]{2,1,0:T(8,128)S(1)} %get-tuple-element.69.end, bf16[26,64,256]{2,1,0:T(8,128)(2,1)S(1)} %get-tuple-element.55.mid_high, bf16[6,64,256]{2,1,0:T(8,128)(2,1)S(1)} %get-tuple-element.64.end_high, bf16[26,64,256]{2,1,0:T(8,128)(2,1)S(1)} %get-tuple-element.65.mid_low, ...), custom_call_target="tpu_custom_call" | custom-call | flops 1107296256 | bytes 6291456 | tf_op jit(solution)/shard_map/outer1/pallas_call | solution.py:475
  43.7 9.6 %all-gather = f32[8,32,256]{2,1,0:T(8,128)S(1)} all-gather(f32[2,32,256]{2,1,0:T(8,128)S(1)} %get-tuple-element.74), channel_id=2, replica_groups=mesh['gx'=16,'gy'=4,'gz'=4] {'gz'}, dimensions={0}, use_global_device_ids=true | all-gather | bytes 327680 | tf_op jit(solution)/shard_map/all_gather | solution.py:485
  53.3 0.0 copy-done.2
  53.3 3.3 %depth.1 = f32[64,32,256]{2,1,0:T(8,128)} custom-call(f32[26,64,256]{2,1,0:T(8,128)S(1)} %get-tuple-element.68.mid, f32[6,64,256]{2,1,0:T(8,128)S(1)} %get-tuple-element.73.end, f32[4,2,32,256]{3,2,1,0:T(8,128)S(1)} %bitcast.2, f32[4,136]{1,0:T(4,128)S(1)} %copy-done.2), custom_call_target="tpu_custom_call" | custom-call | bytes 6291456 | tf_op jit(solution)/shard_map/depth/pallas_call | solution.py:486
Async XLA Ops:
  0.0 7.0 %copy-start.1 = (f32[28]{0:T(128)S(1)}, f32[28]{0:T(128)}, u32[]{:S(2)}) copy-start(f32[28]{0:T(128)} %weight.9) | copy-start | bytes 340
  0.0 7.0 %copy-start.5 = (f32[4]{0:T(128)S(1)}, f32[4]{0:T(128)}, u32[]{:S(2)}) copy-start(f32[4]{0:T(128)} %rate.1) | copy-start | bytes 52
  0.0 7.0 %copy-start.4 = (f32[4]{0:T(128)S(1)}, f32[4]{0:T(128)}, u32[]{:S(2)}) copy-start(f32[4]{0:T(128)} %diffusivity.1) | copy-start | bytes 52
  0.0 7.0 %copy-start.3 = (s32[28,2]{0,1:T(2,128)S(1)}, s32[28,2]{0,1:T(2,128)}, u32[]{:S(2)}) copy-start(s32[28,2]{0,1:T(2,128)} %param.13) | copy-start | bytes 676
  3.3 9.6 %collective-permute-start = (f32[2,64,128]{2,1,0:T(8,128)S(1)}, f32[2,64,128]{2,1,0:T(8,128)S(1)}, u32[]{:S(2)}, u32[]{:S(2)}) collective-permute-start(f32[2,64,128]{2,1,0:T(8,128)S(1)} %get-tuple-element.45.lasts), channel_id=1, source_target_pairs={{0,4},{4,8},{8,12},{12,0},{1,5},{5,9},{9,13},{13,1},{2,6},{6,10},{... | collective-permute-start | bytes 196616 | tf_op jit(solution)/shard_map/ppermute | solution.py:436
  5.5 7.5 %collective-permute-start.1 = (f32[2,64,128]{2,1,0:T(8,128)S(1)}, f32[2,64,128]{2,1,0:T(8,128)S(1)}, u32[]{:S(2)}, u32[]{:S(2)}) collective-permute-start(f32[2,64,128]{2,1,0:T(8,128)S(1)} %get-tuple-element.46.firsts), channel_id=1, source_target_pairs={{0,12},{4,0},{8,4},{12,8},{1,13},{5,1},{9,5},{13,9},{2,14},{6,2},{... | collective-permute-start | bytes 196616 | tf_op jit(solution)/shard_map/ppermute | solution.py:436
  7.0 15.5 %copy-start = (f32[4,128]{1,0:T(4,128)S(1)}, f32[4,128]{1,0:T(4,128)}, u32[]{:S(2)}) copy-start(f32[4,128]{1,0:T(4,128)} %constant.4.clone.sums) | copy-start | bytes 6148
  7.0 15.5 %copy-start.6 = (f32[26,64,256]{2,1,0:T(8,128)S(1)}, f32[26,64,256]{2,1,0:T(8,128)}, u32[]{:S(2)}) copy-start(f32[26,64,256]{2,1,0:T(8,128)} %get-tuple-element.40.mid) | copy-start | bytes 5111812
  13.1 15.6 %collective-permute-start.2 = (f32[7,64,128]{2,1,0:T(8,128)S(1)}, f32[7,64,128]{2,1,0:T(8,128)S(1)}, u32[]{:S(2)}, u32[]{:S(2)}) collective-permute-start(f32[7,64,128]{2,1,0:T(8,128)S(1)} %get-tuple-element.57), channel_id=1, source_target_pairs={{0,16},{16,32},{32,48},{48,64},{64,80},{80,96},{96,112},{112,128},... | collective-permute-start | bytes 688136 | tf_op jit(solution)/shard_map/ppermute | solution.py:436
  14.8 13.8 %collective-permute-start.3 = (f32[7,64,128]{2,1,0:T(8,128)S(1)}, f32[7,64,128]{2,1,0:T(8,128)S(1)}, u32[]{:S(2)}, u32[]{:S(2)}) collective-permute-start(f32[7,64,128]{2,1,0:T(8,128)S(1)} %get-tuple-element.58), channel_id=1, source_target_pairs={{0,240},{16,0},{32,16},{48,32},{64,48},{80,64},{96,80},{112,96},{1... | collective-permute-start | bytes 688136 | tf_op jit(solution)/shard_map/ppermute | solution.py:436
  19.8 8.9 %collective-permute-start.4 = (f32[2,64,128]{2,1,0:T(8,128)S(1)}, f32[2,64,128]{2,1,0:T(8,128)S(1)}, u32[]{:S(2)}, u32[]{:S(2)}) collective-permute-start(f32[2,64,128]{2,1,0:T(8,128)S(1)} %get-tuple-element.62), channel_id=1, source_target_pairs={{0,4},{4,8},{8,12},{12,0},{1,5},{5,9},{9,13},{13,1},{2,6},{6,10},{... | collective-permute-start | bytes 196616 | tf_op jit(solution)/shard_map/ppermute | solution.py:436
  19.8 8.9 %collective-permute-start.5 = (f32[2,64,128]{2,1,0:T(8,128)S(1)}, f32[2,64,128]{2,1,0:T(8,128)S(1)}, u32[]{:S(2)}, u32[]{:S(2)}) collective-permute-start(f32[2,64,128]{2,1,0:T(8,128)S(1)} %get-tuple-element.63), channel_id=1, source_target_pairs={{0,12},{4,0},{8,4},{12,8},{1,13},{5,1},{9,5},{13,9},{2,14},{6,2},{... | collective-permute-start | bytes 196616 | tf_op jit(solution)/shard_map/ppermute | solution.py:436
  30.7 10.7 %collective-permute-start.6 = (f32[7,64,128]{2,1,0:T(8,128)S(1)}, f32[7,64,128]{2,1,0:T(8,128)S(1)}, u32[]{:S(2)}, u32[]{:S(2)}) collective-permute-start(f32[7,64,128]{2,1,0:T(8,128)S(1)} %get-tuple-element.70), channel_id=1, source_target_pairs={{0,16},{16,32},{32,48},{48,64},{64,80},{80,96},{96,112},{112,128},... | collective-permute-start | bytes 688136 | tf_op jit(solution)/shard_map/ppermute | solution.py:436
  30.8 10.6 %collective-permute-start.7 = (f32[7,64,128]{2,1,0:T(8,128)S(1)}, f32[7,64,128]{2,1,0:T(8,128)S(1)}, u32[]{:S(2)}, u32[]{:S(2)}) collective-permute-start(f32[7,64,128]{2,1,0:T(8,128)S(1)} %get-tuple-element.71), channel_id=1, source_target_pairs={{0,240},{16,0},{32,16},{48,32},{64,48},{80,64},{96,80},{112,96},{1... | collective-permute-start | bytes 688136 | tf_op jit(solution)/shard_map/ppermute | solution.py:436
  41.4 11.9 %copy-start.2 = (f32[4,136]{1,0:T(4,128)S(1)}, f32[4,136]{1,0:T(4,128)}, u32[]{:S(2)}) copy-start(f32[4,136]{1,0:T(4,128)} %constant.5.clone.solve) | copy-start | bytes 6532

commit v4 on v3

--- a/solution.py
+++ b/solution.py
@@ -64,6 +64,12 @@
     return high, (value - high.astype(f32)).astype(bf16)
 
 
+def add_middle(pack, row, x):
+    slot = 8 * (x % 16)
+    pack = at_lanes(pack, row[:, :128], 125, slot, 3)
+    return at_lanes(pack, row[:, 128:], 0, slot + 4, 3)
+
+
 def edge_window(before, after, x):
     slot = 8 * ((x + 13) % 16)
     lane = lanes()
@@ -80,7 +86,7 @@
     return total
 
 
-def prepare_kernel(offsets, weight, diffusivity, rate, pit, phase, damage, w_ref, move, gain, table, to_high, to_low, pv, hv, dv, sem):
+def prepare_kernel(offsets, weight, diffusivity, rate, pit, phase, damage, mid, end, w_ref, move, gain, table, to_high, to_low, middle, pv, hv, dv, sem):
     def copies(group):
         return [
             pltpu.make_async_copy(source.at[:, x, :], target.at[x], sem.at[group])
@@ -96,27 +102,38 @@
     for bond in range(BONDS):
         place = (offsets[0, bond] + 3) * 7 + offsets[1, bond] + 3
         table[place] = table[place] + weight[bond]
-    diff = lax.broadcasted_iota(jnp.int32, (DY, DY), 0) - lax.broadcasted_iota(jnp.int32, (DY, DY), 1) + 3
-
-    @pl.loop(0, 7)
-    def _(first):
-        band = jnp.zeros((DY, DY), f32)
+    diff = lax.broadcasted_iota(jnp.int32, (128, 128), 0) - lax.broadcasted_iota(jnp.int32, (128, 128), 1) + 3
+    blank = jnp.zeros((128, 128), bf16)
+    for start in (0, 4):
+        w_ref[start, :128, 128:] = blank
+        w_ref[start + 3, 128:, :128] = blank
+    for first in range(7):
+        band = jnp.zeros((128, 128), f32)
         for second in range(7):
             band = jnp.where(diff == second, table[first * 7 + second], band)
-        w_ref[first], w_ref[7 + first] = split(band)
-
-    lane = lax.broadcasted_iota(jnp.int32, (128, DY), 0)
-    column = lax.broadcasted_iota(jnp.int32, (128, DY), 1)
+        high, low = split(band)
+        for out_row in range(2):
+            row = first + out_row
+            place = (slice(128 * (row % 2), 128 * (row % 2) + 128), slice(128 * out_row, 128 * out_row + 128))
+            w_ref[(row // 2,) + place] = high
+            w_ref[(4 + row // 2,) + place] = low
+    lane = lax.broadcasted_iota(jnp.int32, (64, DY), 0)
+    column = lax.broadcasted_iota(jnp.int32, (64, DY), 1)
     place = lane % 8
-    which = jnp.where(place < 4, place - column, 255 + place - column)
-    which = jnp.where((place == 3) | (place == 7), -1, which)
-    which = jnp.where((which >= 0) & (which < 7), which, -100) + 7 * ((lane % 64) // 8)
-    edge = jnp.zeros((128, DY), f32)
+    first = lane // 8 - column // 128
+    second = jnp.where(place < 4, place, 127 + place) - column % 128
+    good = (place != 3) & (place != 7) & (first >= 0) & (first < 7) & (second >= 0) & (second < 7)
+    which = jnp.where(good, 7 * first + second, -1)
+    edge = jnp.zeros((64, DY), f32)
     for place in range(49):
         edge = jnp.where(which == place, table[place], edge)
     high, low = split(edge)
-    w_ref[14, :128, :] = high
-    w_ref[14, 128:, :] = jnp.where(lane < 64, low.astype(f32), 0.0).astype(bf16)
+    for row, value in enumerate((high, high, low, jnp.zeros((64, DY), bf16))):
+        w_ref[8, 64 * row : 64 * row + 64, :] = value
+    packed = [jnp.zeros((DZ, 128), f32)] * 2
+    for x in range(DX):
+        packed[x // 16] = add_middle(packed[x // 16], end[OUTER.index(x)] if x in OUTER else mid[x - 3], x)
+    middle[0], middle[1] = packed
 
     def look(ids, values, scale):
         value = jnp.where(ids == 0, values[0] * scale, values[1] * scale)
@@ -145,12 +162,24 @@
 
 
 def right_side(w_ref):
-    bands = [w_ref[a] for a in range(7)]
-    return jnp.concatenate(bands + bands + [w_ref[7 + a] for a in range(7)] + [w_ref[14]], axis=0)
-
-
-def flat(value):
-    return value.reshape(value.shape[0] * DZ, DY)
+    high, low = [w_ref[t] for t in range(4)], [w_ref[4 + t] for t in range(4)]
+    return jnp.concatenate(high + high + low + [w_ref[8]], axis=0)
+
+
+def pair_flux(pairs, high_of, low_of, edges, half, w_ref):
+    part = slice(128 * half, 128 * half + 128)
+
+    def side(row_of):
+        return [jnp.concatenate([row_of(x - 3 + i)[:, part] for x in pairs], axis=0) for i in range(8)]
+
+    high, low = side(high_of), side(low_of)
+    left = jnp.concatenate(high + low + high + [edges], axis=1)
+    flux = jnp.dot(left, right_side(w_ref), preferred_element_type=f32)
+
+    def of(place, out_row):
+        return flux[DZ * place : DZ * place + DZ, 128 * out_row : 128 * out_row + 128]
+
+    return of
 
 
 def stepped(center, flux, move, gain, weight_sum):
@@ -252,47 +281,46 @@
     return total
 
 
-CHUNK = INNER // 2
-
-
-def row_range(mid, end, start, count):
-    pieces = []
-    stop = start + count
-    if start < 3:
-        pieces.append(end[start : min(stop, 3)])
-    if stop > 3 and start < DX - 3:
-        pieces.append(mid[max(start, 3) - 3 : min(stop, DX - 3) - 3])
-    if stop > DX - 3:
-        pieces.append(end[max(start, DX - 3) - DX + 6 : stop - DX + 6])
-    pieces = [flat(piece) for piece in pieces]
-    return pieces[0] if len(pieces) == 1 else jnp.concatenate(pieces, axis=0)
-
-
 def inner_kernel(
-    last, mid, mid_high, end_high, mid_low, end_low, strips, move, gain, w_ref, weight, sums, table,
-    out, out_high, out_low, extra, edges,
+    last, mid, mid_high, end_high, mid_low, end_low, strips, middle, move, gain, w_ref, weight, sums, table,
+    out, out_high, out_low, extra, new_middle,
 ):
     halo = strips.at[0 if last else 1]
-    for x in range(3, DX - 3):
-        group = (x + 13) // 16 - 1
-        edges[x - 3] = edge_window(halo[group], halo[min(group + 1, 1)], x)
     weight_sum = total_weight(weight)
-    for chunk in range(2):
-        start = CHUNK * chunk
-        highs = [row_range(mid_high, end_high, start + a, CHUNK) for a in range(7)]
-        lows = [row_range(mid_low, end_low, start + a, CHUNK) for a in range(7)]
-        left = highs + lows + highs + [flat(edges[start : start + CHUNK])]
-        flux = jnp.dot(jnp.concatenate(left, axis=1), right_side(w_ref), preferred_element_type=f32)
-        for i in range(CHUNK):
-            row, x = start + i, start + i + 3
-            new = stepped(mid[row], flux[DZ * i : DZ * i + DZ], move[x], gain[x], weight_sum)
-            out[row] = new
-            if not last:
-                out_high[row], out_low[row] = split(new)
+    pairs = range(3, DX - 3, 2)
+
+    def row_of(mid_part, end_part):
+        return lambda x: end_part[OUTER.index(x)] if x in OUTER else mid_part[x - 3]
+
+    packed = [jnp.zeros((DZ, 128), f32)] * 2
+    for half in range(2):
+        around = [
+            two_sides(halo[g], middle[g]) if half == 0 else two_sides(middle[g], halo[g]) for g in range(2)
+        ]
+        edges = []
+        for x in pairs:
+            group = (x + 13) // 16 - 1
+            edges.append(edge_window(around[group], around[min(group + 1, 1)], x))
+        flux = pair_flux(
+            pairs, row_of(mid_high, end_high), row_of(mid_low, end_low), jnp.concatenate(edges, axis=0), half, w_ref
+        )
+        part = slice(128 * half, 128 * half + 128)
+        for place, first in enumerate(pairs):
+            for out_row in range(2):
+                x = first + out_row
+                row = x - 3
+                new = stepped(mid[row, :, part], flux(place, out_row), move[x, :, part], gain[x, :, part], weight_sum)
+                out[row, :, part] = new
+                if not last:
+                    out_high[row, :, part], out_low[row, :, part] = split(new)
+                    slot = 8 * (x % 16)
+                    source, target = (125, slot) if half == 0 else (0, slot + 4)
+                    packed[x // 16] = at_lanes(packed[x // 16], new, source, target, 3)
     if last:
         extra[...] = jnp.zeros_like(extra)
         depth_sums(out, sums, extra, 3, INNER, 0)
     else:
+        new_middle[0], new_middle[1] = packed
         taps = [strip_taps(table, strips[0, g], strips[1, g], strips[2, g]) for g in range(2)] + [None]
         for group in range(2):
             extra[group] = strip_flux(taps, group)
@@ -311,46 +339,69 @@
 
 
 def outer_kernel(
-    last, end, mid_high, end_high, mid_low, end_low, strips, from_low, from_high, move, gain, w_ref, weight, sums,
-    extra_in, *rest,
+    last, end, mid_high, end_high, mid_low, end_low, strips, middle, from_low, from_high, move, gain, w_ref, weight,
+    sums, extra_in, *rest,
 ):
     if last:
         out, extra = rest
     else:
-        table, coefs_left, coefs_right, out, out_high, out_low, extra, up, down = rest
+        table, coefs_left, coefs_right, middle_in, out, out_high, out_low, extra, up, down, new_middle = rest
     halo = strips.at[0 if last else 1]
-    groups = [from_low[6], halo[0], halo[1], from_high[6]]
-    edges = []
-    for x in OUTER:
-        group = (x + 13) // 16
-        edges.append(edge_window(groups[group], groups[min(group + 1, 3)], x))
+    weight_sum = total_weight(weight)
+    zero = jnp.zeros((DZ, 128), f32)
 
     def halo_rows(slabs):
-        rows = [split(jnp.concatenate([slabs[2 * row], slabs[2 * row + 1]], axis=1)) for row in range(3)]
-        return [row[0] for row in rows], [row[1] for row in rows]
-
-    low_halo, high_halo = halo_rows(from_low), halo_rows(from_high)
-
-    def taps(which, mid_part, end_part):
-        top = low_halo[which] + [end_part[i] for i in range(3)] + [mid_part[i] for i in range(3)]
-        bottom = [mid_part[INNER - 3 + i] for i in range(3)] + [end_part[3 + i] for i in range(3)]
-        bottom = bottom + high_halo[which]
-        return [jnp.concatenate(top[a : a + 3] + bottom[a : a + 3], axis=0) for a in range(7)]
-
-    highs, lows = taps(0, mid_high, end_high), taps(1, mid_low, end_low)
-    left = highs + lows + highs + [jnp.concatenate(edges, axis=0)]
-    flux = jnp.dot(jnp.concatenate(left, axis=1), right_side(w_ref), preferred_element_type=f32)
-    weight_sum = total_weight(weight)
-    for row, x in enumerate(OUTER):
-        new = stepped(end[row], flux[DZ * row : DZ * row + DZ], move[x], gain[x], weight_sum)
-        out[row] = new
-        if not last:
-            out_high[row], out_low[row] = split(new)
+        return [jnp.concatenate([slabs[2 * row], slabs[2 * row + 1]], axis=1) for row in range(3)]
+
+    low_rows, high_rows = halo_rows(from_low), halo_rows(from_high)
+    low_split, high_split = [split(row) for row in low_rows], [split(row) for row in high_rows]
+    low_middle, high_middle = zero, zero
+    for row in range(3):
+        low_middle = add_middle(low_middle, low_rows[row], 13 + row)
+        high_middle = add_middle(high_middle, high_rows[row], row)
+    sides = [from_low[6], halo[0], halo[1], from_high[6]]
+    middles = [low_middle, middle[0], middle[1], high_middle]
+
+    def row_of(which, mid_part, end_part):
+        def of(x):
+            if x < 0:
+                return low_split[x + 3][which]
+            if x >= DX:
+                return high_split[x - DX][which]
+            return end_part[OUTER.index(x)] if x in OUTER else mid_part[x - 3]
+
+        return of
+
+    pairs = [0, 2, DX - 4, DX - 2]
+    packed = [zero, zero] if last else [middle_in[0], middle_in[1]]
+    for half in range(2):
+        around = [two_sides(p, q) if half == 0 else two_sides(q, p) for p, q in zip(sides, middles)]
+        edges = []
+        for x in pairs:
+            group = (x + 13) // 16
+            edges.append(edge_window(around[group], around[min(group + 1, 3)], x))
+        flux = pair_flux(
+            pairs, row_of(0, mid_high, end_high), row_of(1, mid_low, end_low), jnp.concatenate(edges, axis=0), half,
+            w_ref,
+        )
+        part = slice(128 * half, 128 * half + 128)
+        for row, x in enumerate(OUTER):
+            place = [i for i in range(4) if pairs[i] <= x <= pairs[i] + 1][0]
+            new = stepped(
+                end[row, :, part], flux(place, x - pairs[place]), move[x, :, part], gain[x, :, part], weight_sum
+            )
+            out[row, :, part] = new
+            if not last:
+                out_high[row, :, part], out_low[row, :, part] = split(new)
+                slot = 8 * (x % 16)
+                source, target = (125, slot) if half == 0 else (0, slot + 4)
+                packed[x // 16] = at_lanes(packed[x // 16], new, source, target, 3)
     if last:
         extra[...] = extra_in[...]
         depth_sums(out, sums, extra, 0, 3, 0)
         depth_sums(out, sums, extra, DX - 3, 3, 3)
     else:
+        new_middle[0], new_middle[1] = packed
         fill_slabs(lambda row: out[row], up, down)
         lane = lanes()
         low, high = from_low[6], from_high[6]
@@ -371,7 +422,8 @@
         down[6] = extra[0, 0]
 
 
-def depth_tables(blocks):
+def depth_tables():
+    blocks = 4
     stiff = 3.0 * DZ * DZ
     count = DZ * blocks
     diagonal = np.full(count, 1.0 + 2.0 * stiff)
@@ -382,53 +434,97 @@
     back = diagonal.copy()
     for i in range(count - 2, -1, -1):
         back[i] = diagonal[i] - stiff * stiff / back[i + 1]
+
+    def from_above(block, other):
+        return np.prod(stiff / fore[other * DZ + DZ - 1 : block * DZ])
+
+    def from_below(block, other):
+        return np.prod(stiff / back[block * DZ + DZ : other * DZ + 1])
+
     sums = np.zeros((blocks, 2 * DZ))
-    solve = np.zeros((blocks, 2 * DZ + 2 * blocks))
+    solve = np.zeros((blocks, 2 * DZ))
+    reply = np.zeros((blocks, 2 * DZ))
+    mix = np.zeros((blocks, 8))
     for block in range(blocks):
         start, end = block * DZ, block * DZ + DZ - 1
+        pivots = fore[start : end + 1].copy()
+        if block < blocks - 1:
+            pivots[-1] = fore[end] - stiff * stiff / back[end + 1]
         for z in range(DZ):
             sums[block, z] = np.prod(stiff / fore[start + z : end])
             sums[block, DZ + z] = np.prod(stiff / back[start + 1 : start + z + 1])
-            solve[block, z] = stiff / fore[start + z - 1] if start + z else 0.0
-            solve[block, DZ + z] = 1.0 / fore[start + z]
-        if block < blocks - 1:
-            solve[block, 2 * DZ - 1] = 1.0 / (fore[end] - stiff * stiff / back[end + 1])
-        for other in range(blocks):
-            if other < block:
-                solve[block, 2 * DZ + other] = np.prod(stiff / fore[other * DZ + DZ - 1 : start])
-            if other > block:
-                solve[block, 2 * DZ + blocks + other] = np.prod(stiff / back[end + 1 : other * DZ + 1])
-    return jnp.asarray(sums, f32), jnp.asarray(solve, f32)
-
-
-def depth_kernel(blocks, mid, end, every, solve, out, buf, sweep, out_sem):
+            solve[block, z] = stiff / fore[start + z - 1] if z else 0.0
+            solve[block, DZ + z] = 1.0 / pivots[z]
+        for side, place in ((0, 0), (1, DZ - 1)):
+            value = np.zeros(DZ)
+            value[place] = 1.0
+            for z in range(1, DZ):
+                value[z] += solve[block, z] * value[z - 1]
+            value[-1] /= pivots[-1]
+            for z in range(DZ - 2, -1, -1):
+                value[z] = (value[z] + stiff * value[z + 1]) / pivots[z]
+            reply[block, side * DZ : side * DZ + DZ] = 2.0 * value
+        partner = block ^ 1
+        if block < 2:
+            near, far = (1.0, from_above(3, 0) / from_above(3, 1))
+            mix[block, 0:2] = (far, near) if block == 0 else (near, far)
+            mix[block, 7] = from_below(block, 2)
+        else:
+            near, far = (1.0, from_below(0, 3) / from_below(0, 2))
+            mix[block, 2:4] = (near, far) if block == 2 else (far, near)
+            mix[block, 5] = from_above(block, 1)
+        if partner < block:
+            mix[block, 4] = from_above(block, partner)
+        else:
+            mix[block, 6] = from_below(block, partner)
+    return [jnp.asarray(table, f32) for table in (sums, solve, reply, mix)]
+
+
+def mix_kernel(own_sums, partner_sums, mix, send, near):
+    own = lax.axis_index("gz")
+    send[...] = (
+        mix[own, 0] * own_sums[0] + mix[own, 1] * partner_sums[0]
+        + mix[own, 2] * own_sums[1] + mix[own, 3] * partner_sums[1]
+    )
+    near[0] = mix[own, 4] * partner_sums[0]
+    near[1] = mix[own, 6] * partner_sums[1]
+
+
+def sweep_kernel(mid, end, solve, sweep, buf):
     for row, x in enumerate(OUTER):
         buf[:, x, :] = end[row]
     for row in range(INNER):
         buf[:, 3 + row, :] = mid[row]
     own = lax.axis_index("gz")
     stiff = 3.0 * DZ * DZ
-    above = jnp.zeros((DX, DY), f32)
-    below = jnp.zeros((DX, DY), f32)
-    for block in range(blocks):
-        above = above + solve[own, 2 * DZ + block] * every[block, 0]
-        below = below + solve[own, 2 * DZ + blocks + block] * every[block, 1]
-    value = above
-    for z in range(DZ):
-        carried = value if z == 0 else solve[own, z] * value
-        value = buf[z] + carried
+    value = buf[0]
+    sweep[0] = value
+    for z in range(1, DZ):
+        value = buf[z] + solve[own, z] * value
         sweep[z] = value
-    value = (value + below) * solve[own, 2 * DZ - 1]
+    value = value * solve[own, 2 * DZ - 1]
     for z in range(DZ - 1, -1, -1):
         if z < DZ - 1:
             value = (sweep[z] + stiff * value) * solve[own, DZ + z]
         sweep[z] = 2.0 * value - buf[z]
-        if z % 16 == 0:
-            part = pl.ds(z, 16)
-            pltpu.make_async_copy(sweep.at[part], out.at[part], out_sem.at[z // 16]).start()
-    for z in range(0, DZ, 16):
+
+
+def finish_kernel(swept, near, far, mix, reply, out, buf, out_sem):
+    own = lax.axis_index("gz")
+    above = near[0] + mix[own, 5] * far[...]
+    below = near[1] + mix[own, 7] * far[...]
+    parts = range(0, DZ, 16)
+
+    def copy(z):
         part = pl.ds(z, 16)
-        pltpu.make_async_copy(sweep.at[part], out.at[part], out_sem.at[z // 16]).wait()
+        return pltpu.make_async_copy(buf.at[part], out.at[part], out_sem.at[z // 16])
+
+    for start in parts:
+        for z in range(start, start + 16):
+            buf[z] = swept[z] + reply[own, z] * above + reply[own, DZ + z] * below
+        copy(start).start()
+    for start in parts:
+        copy(start).wait()
 
 
 def shift(value, axis, step):
@@ -437,19 +533,18 @@
 
 
 def local(conc, pit, phase, offsets, damage, weight, diffusivity, rate):
-    blocks = lax.axis_size("gz")
-    sums, solve = depth_tables(blocks)
+    sums, solve, reply, mix = depth_tables()
     *parts, lasts, firsts, up, down = call(
         first_kernel, "first", PARTS + (PACK, PACK, SLABS, SLABS), [HBM], (VMEM,) * 10,
-        [pltpu.VMEM((DX, DZ, DY), f32), SEM((4,))], nbytes=4 << 20, limit=50,
+        [pltpu.VMEM((DX, DZ, DY), f32), SEM((4,))], nbytes=4 << 20, limit=48,
     )(conc)
     left, right = shift(lasts, "gy", 1), shift(firsts, "gy", -1)
-    w, move, gain, table, to_high, to_low = call(
-        prepare_kernel, "prepare", (struct(15, DY, DY, dtype=bf16), WHOLE, WHOLE, struct(64), PACK, PACK),
-        [SMEM] * 4 + [HBM] * 3, (VMEM, VMEM, VMEM, SMEM, VMEM, VMEM),
+    w, move, gain, table, to_high, to_low, middle = call(
+        prepare_kernel, "prepare", (struct(9, DY, DY, dtype=bf16), WHOLE, WHOLE, struct(64), PACK, PACK, PACK),
+        [SMEM] * 4 + [HBM] * 3 + [VMEM] * 2, (VMEM, VMEM, VMEM, SMEM, VMEM, VMEM, VMEM),
         [pltpu.VMEM((DX, DZ, DY), jnp.int32)] * 3 + [SEM((4,))],
-        nbytes=8 << 20, limit=47,
-    )(offsets.T, weight, diffusivity, rate, pit, phase, damage)
+        nbytes=8 << 20, limit=45,
+    )(offsets.T, weight, diffusivity, rate, pit, phase, damage, parts[0], parts[1])
     strips, up, down = call(
         join_kernel, "join", (struct(3, 2, DZ, 128), SLABS, SLABS), [VMEM] * 6, (VMEM,) * 3,
     )(left, right, lasts, firsts, up, down)
@@ -462,32 +557,40 @@
         mid, end, mid_high, end_high, mid_low, end_low = parts
         tiny = struct(1, 16, 128, dtype=bf16)
         inner_split = (tiny, tiny) if last else (PARTS[2], PARTS[4])
-        new_mid, new_mid_high, new_mid_low, more = call(
+        new_mid, new_mid_high, new_mid_low, more, more_middle = call(
             functools.partial(inner_kernel, last), f"inner{substep}",
-            (PARTS[0],) + inner_split + ((struct(2, DX, DY) if last else PACK),),
-            [VMEM] * 9 + [SMEM] * 3, (VMEM,) * 4, [pltpu.VMEM((INNER, DZ, DY), bf16)],
-            flops=2 * INNER * DZ * DY * 5632, nbytes=12 << 20,
-        )(mid, mid_high, end_high, mid_low, end_low, strips, move, gain, w, weight, sums, table)
-        args = (end, mid_high, end_high, mid_low, end_low, strips, from_low, from_high, move, gain, w, weight, sums, more)
-        specs = [VMEM] * 11 + [SMEM] * 2 + [VMEM]
-        cost = dict(flops=2 * 6 * DZ * DY * 5632, nbytes=6 << 20)
+            (PARTS[0],) + inner_split + ((struct(2, DX, DY) if last else PACK), struct(1, 8, 128) if last else PACK),
+            [VMEM] * 10 + [SMEM] * 3, (VMEM,) * 5, flops=2 * INNER * DZ * DY * 3328, nbytes=12 << 20,
+        )(mid, mid_high, end_high, mid_low, end_low, strips, middle, move, gain, w, weight, sums, table)
+        args = (end, mid_high, end_high, mid_low, end_low, strips, middle, from_low, from_high, move, gain, w, weight)
+        args = args + (sums, more)
+        specs = [VMEM] * 12 + [SMEM] * 2 + [VMEM]
+        cost = dict(flops=2 * 8 * DZ * DY * 3328, nbytes=6 << 20)
         if last:
             new_end, ends = call(
                 functools.partial(outer_kernel, last), "outer1", (PARTS[1], struct(2, DX, DY)), specs, (VMEM,) * 2, **cost
             )(*args)
         else:
-            new_end, new_end_high, new_end_low, strips, up, down = call(
+            new_end, new_end_high, new_end_low, strips, up, down, middle = call(
                 functools.partial(outer_kernel, last), "outer0",
-                (PARTS[1], PARTS[3], PARTS[5], struct(1, 2, DZ, 128), SLABS, SLABS),
-                specs + [SMEM, VMEM, VMEM], (VMEM,) * 6, **cost,
-            )(*args, table, *coefs)
+                (PARTS[1], PARTS[3], PARTS[5], struct(1, 2, DZ, 128), SLABS, SLABS, PACK),
+                specs + [SMEM, VMEM, VMEM, VMEM], (VMEM,) * 7, **cost,
+            )(*args, table, *coefs, more_middle)
             parts = [new_mid, new_end, new_mid_high, new_end_high, new_mid_low, new_end_low]
-    every = lax.all_gather(ends, "gz", axis=0)
+    partner = lax.ppermute(ends, "gz", [(0, 1), (1, 0), (2, 3), (3, 2)])
+    send, near = call(
+        mix_kernel, "mix", (struct(DX, DY), struct(2, DX, DY)), [VMEM, VMEM, SMEM], (VMEM,) * 2,
+    )(ends, partner, mix)
+    send, new_mid, new_end = lax.optimization_barrier((send, new_mid, new_end))
+    far = lax.ppermute(send, "gz", [(0, 2), (2, 0), (1, 3), (3, 1)])
+    swept = call(
+        sweep_kernel, "sweep", struct(DZ, DX, DY), [VMEM, VMEM, SMEM], VMEM, [pltpu.VMEM((DZ, DX, DY), f32)],
+        flops=20 << 20, nbytes=4 << 20,
+    )(new_mid, new_end, solve)
     return call(
-        functools.partial(depth_kernel, blocks), "depth", struct(DZ, DX, DY),
-        [VMEM, VMEM, VMEM, SMEM], HBM,
-        [pltpu.VMEM((DZ, DX, DY), f32), pltpu.VMEM((DZ, DX, DY), f32), SEM((4,))], nbytes=6 << 20,
-    )(new_mid, new_end, every, solve)
+        finish_kernel, "finish", struct(DZ, DX, DY), [VMEM, VMEM, VMEM, SMEM, SMEM], HBM,
+        [pltpu.VMEM((DZ, DX, DY), f32), SEM((4,))], nbytes=6 << 20,
+    )(swept, near, far, mix, reply)
 
 
 def solution(mesh):

time: 57 us -> 49.4 us (0.87)
  blocking collectives: 9.62 us -> 0 us
  starting transfers between devices: 16.7 us -> 21.8 us
  Pallas kernels: 30.1 us -> 26.1 us
  waiting for transfers between devices: 0.02 us -> 0.93 us
    all_gather x1 -> x0, blocking collectives: 9.62 us -> none  [local(): every = lax.all_gather(ends, 'gz', axis=0)]
    ppermute x0 -> x2, starting transfers between devices: none -> 5.12 us  [the longest x1 2.58 us: local(): partner = lax.ppermute(ends, 'gz', [(0, 1), (1, 0), (2, 3), (3, 2)])]
    pallas_call x2, Pallas kernels: 13.2 us -> 9.46 us  [local(): call(functools.partial(inner_kernel, last), f'inner{substep}', (PARTS[0],...]
    pallas_call x2 -> x4, Pallas kernels: 9.2 us -> 10.4 us  [the longest x1 5.57 us: local(): call(prepare_kernel, 'prepare', (struct(9, DY, DY, dtype=bf16), WHOLE, WH...]
    pallas_call x1, Pallas kernels: 3.24 us -> 2.17 us  [local(): call(first_kernel, 'first', PARTS + (PACK, PACK, SLABS, SLABS), [HBM], (V...]
    ppermute x0 -> x2, waiting for transfers between devices: none -> 0.9 us  [the longest x1 0.9 us: local(): partner = lax.ppermute(ends, 'gz', [(0, 1), (1, 0), (2, 3), (3, 2)])]
  transfers between devices with their start and end apart: 8 -> 10, of which waited for: 0 -> 1; matrix products, arithmetic and copies ran while one was open for 0% -> 0% of each run, Pallas kernels for 34% -> 35%
where the time goes in v4:
time: 49.4 us; the launch traced here: 49.3 us
  Pallas kernels  26.1 us (53%)
  starting transfers between devices  21.8 us (44%)
  waiting for transfers between devices  0.93 us (2%)
    ppermute x8, starting transfers between devices, shift(): lax.ppermute(value, axis, [(i, (i + step) % count) for i in range(count)])  16.7 us
    pallas_call x2, Pallas kernels, local(): call(functools.partial(inner_kernel, last), f'inner{substep}', (PARTS[0],...  9.46 us
    pallas_call x1, Pallas kernels, local(): call(prepare_kernel, 'prepare', (struct(9, DY, DY, dtype=bf16), WHOLE, WH...  5.57 us
    ppermute x1, starting transfers between devices, local(): partner = lax.ppermute(ends, 'gz', [(0, 1), (1, 0), (2, 3), (3, 2)])  2.58 us
    ppermute x1, starting transfers between devices, local(): far = lax.ppermute(send, 'gz', [(0, 2), (2, 0), (1, 3), (3, 1)])  2.54 us
    pallas_call x1, Pallas kernels, local(): call(sweep_kernel, 'sweep', struct(DZ, DX, DY), [VMEM, VMEM, SMEM], VMEM,...  2.22 us
    pallas_call x1, Pallas kernels, local(): call(first_kernel, 'first', PARTS + (PACK, PACK, SLABS, SLABS), [HBM], (V...  2.17 us
    pallas_call x1, Pallas kernels, local(): call(finish_kernel, 'finish', struct(DZ, DX, DY), [VMEM, VMEM, VMEM, SMEM...  2.03 us
  transfers between devices with their start and end apart: 10, of which 1 were waited for; matrix products, arithmetic and copies ran while one was open for 0% of the time, Pallas kernels for 35%

profile of v4, /device:TPU:1, one launch (start us, length us, event | category | flops | bytes accessed | tf_op | source)
XLA Modules:
  0.0 49.3 jit_solution(11331366466212304653)
XLA Ops:
  0.0 0.0 copy-start.2
  0.0 0.0 copy-start.7
  0.0 0.0 copy-start.6
  0.0 0.0 copy-start.5
  0.0 2.2 %first.1 = (f32[26,64,256]{2,1,0:T(8,128)S(1)}, f32[6,64,256]{2,1,0:T(8,128)S(1)}, bf16[26,64,256]{2,1,0:T(8,128)(2,1)S(1)}, bf16[6,64,256]{2,1,0:T(8,128)(2,1)S...) custom-call(f32[64,32,256]{2,1,0:T(8,128)} %conc.1), custom_call_target="tpu_custom_call" | custom-call | bytes 4194304 | tf_op jit(solution)/shard_map/first/pallas_call | solution.py:537
  2.2 2.2 %collective-permute-start = (f32[2,64,128]{2,1,0:T(8,128)S(1)}, f32[2,64,128]{2,1,0:T(8,128)S(1)}, u32[]{:S(2)}, u32[]{:S(2)}) collective-permute-start(f32[2,64,128]{2,1,0:T(8,128)S(1)} %get-tuple-element.53.lasts), channel_id=1, source_target_pairs={{0,4},{4,8},{8,12},{12,0},{1,5},{5,9},{9,13},{13,1},{2,6},{6,10},{... | collective-permute-start | bytes 196616 | tf_op jit(solution)/shard_map/ppermute | solution.py:532
  4.4 1.5 %collective-permute-start.1 = (f32[2,64,128]{2,1,0:T(8,128)S(1)}, f32[2,64,128]{2,1,0:T(8,128)S(1)}, u32[]{:S(2)}, u32[]{:S(2)}) collective-permute-start(f32[2,64,128]{2,1,0:T(8,128)S(1)} %get-tuple-element.54.firsts), channel_id=1, source_target_pairs={{0,12},{4,0},{8,4},{12,8},{1,13},{5,1},{9,5},{13,9},{2,14},{6,2},{... | collective-permute-start | bytes 196616 | tf_op jit(solution)/shard_map/ppermute | solution.py:532
  5.9 0.0 copy-done.2
  5.9 0.0 copy-done.7
  5.9 0.0 copy-done.6
  5.9 0.0 copy-done.5
  5.9 0.0 copy-start.1
  5.9 5.6 %prepare.1 = (bf16[9,256,256]{2,1,0:T(8,128)(2,1)S(1)}, f32[32,64,256]{2,1,0:T(8,128)S(1)}, f32[32,64,256]{2,1,0:T(8,128)S(1)}, f32[64]{0:T(128)S(1)}, f32[2,64,...) custom-call(s32[2,28]{1,0:T(2,128)S(1)} %bitcast.1, f32[28]{0:T(128)S(1)} %copy-done.2, ...), custom_call_target="tpu_custom_call" | custom-call | bytes 8388608 | tf_op jit(solution)/shard_map/prepare/pallas_call | solution.py:542
  11.5 0.0 collective-permute-done.left
  11.5 0.0 collective-permute-done.1.right
  11.5 0.2 join.1
  11.8 1.7 %collective-permute-start.2 = (f32[7,64,128]{2,1,0:T(8,128)S(1)}, f32[7,64,128]{2,1,0:T(8,128)S(1)}, u32[]{:S(2)}, u32[]{:S(2)}) collective-permute-start(f32[7,64,128]{2,1,0:T(8,128)S(1)} %get-tuple-element.60), channel_id=1, source_target_pairs={{0,16},{16,32},{32,48},{48,64},{64,80},{80,96},{96,112},{112,128},... | collective-permute-start | bytes 688136 | tf_op jit(solution)/shard_map/ppermute | solution.py:532
  13.5 5.0 %collective-permute-start.3 = (f32[7,64,128]{2,1,0:T(8,128)S(1)}, f32[7,64,128]{2,1,0:T(8,128)S(1)}, u32[]{:S(2)}, u32[]{:S(2)}) collective-permute-start(f32[7,64,128]{2,1,0:T(8,128)S(1)} %get-tuple-element.61), channel_id=1, source_target_pairs={{0,240},{16,0},{32,16},{48,32},{64,48},{80,64},{96,80},{112,96},{1... | collective-permute-start | bytes 688136 | tf_op jit(solution)/shard_map/ppermute | solution.py:532
  18.4 0.0 collective-permute-start.4
  18.4 2.7 %collective-permute-start.5 = (f32[2,64,128]{2,1,0:T(8,128)S(1)}, f32[2,64,128]{2,1,0:T(8,128)S(1)}, u32[]{:S(2)}, u32[]{:S(2)}) collective-permute-start(f32[2,64,128]{2,1,0:T(8,128)S(1)} %get-tuple-element.70), channel_id=1, source_target_pairs={{0,12},{4,0},{8,4},{12,8},{1,13},{5,1},{9,5},{13,9},{2,14},{6,2},{... | collective-permute-start | bytes 196616 | tf_op jit(solution)/shard_map/ppermute | solution.py:532
  21.1 0.0 copy-done.1
  21.1 4.4 %inner0.1 = (f32[26,64,256]{2,1,0:T(8,128)S(1)}, bf16[26,64,256]{2,1,0:T(8,128)(2,1)S(1)}, bf16[26,64,256]{2,1,0:T(8,128)(2,1)S(1)}, f32[2,64,128]{2,1,0:T(8,128)S(1)}, f32[2,64,128]{2,1,0:T(8,128)S(1)}) custom-call(f32[26,64,256]{2,1,0:T(8,128)S(1)} %get-tuple-element.58.mid, bf16[26,64,256]{2,1,0:T(8,128)(2,1)S(1)} %get-tuple-element.49.mid_high, ...), custom_call_target="tpu_custom_call" | custom-call | flops 2835349504 | bytes 12582912 | tf_op jit(solution)/shard_map/inner0/pallas_call | solution.py:560
  25.5 0.0 collective-permute-done.4.rest_1_
  25.5 0.0 collective-permute-done.5.rest_2_
  25.5 0.0 collective-permute-done.2.from_low
  25.5 0.0 collective-permute-done.3.from_high
  25.5 1.9 %outer0.1 = (f32[6,64,256]{2,1,0:T(8,128)S(1)}, bf16[6,64,256]{2,1,0:T(8,128)(2,1)S(1)}, bf16[6,64,256]{2,1,0:T(8,128)(2,1)S(1)}, f32[1,2,64,128]{3,2,1,0:T(8,12...) custom-call(f32[6,64,256]{2,1,0:T(8,128)S(1)} %get-tuple-element.48.end, ...), custom_call_target="tpu_custom_call" | custom-call | flops 872415232 | bytes 6291456 | tf_op jit(solution)/shard_map/outer0/pallas_call | solution.py:574
  27.4 0.1 collective-permute-start.6
  27.5 3.6 %collective-permute-start.7 = (f32[7,64,128]{2,1,0:T(8,128)S(1)}, f32[7,64,128]{2,1,0:T(8,128)S(1)}, u32[]{:S(2)}, u32[]{:S(2)}) collective-permute-start(f32[7,64,128]{2,1,0:T(8,128)S(1)} %get-tuple-element.80), channel_id=1, source_target_pairs={{0,240},{16,0},{32,16},{48,32},{64,48},{80,64},{96,80},{112,96},{1... | collective-permute-start | bytes 688136 | tf_op jit(solution)/shard_map/ppermute | solution.py:532
  31.0 5.1 %inner1.1 = (f32[26,64,256]{2,1,0:T(8,128)S(1)}, bf16[1,16,128]{2,1,0:T(8,128)(2,1)}, bf16[1,16,128]{2,1,0:T(8,128)(2,1)}, f32[2,32,256]{2,1,0:T(8,128)S(1)}, f32[1,8,128]{2,1,0:T(8,128)}) custom-call(f32[26,64,256]{2,1,0:T(8,128)S(1)} %get-tuple-element.81.mid, bf16[26,64,256]{2,1,0:T(8,128)(2,1)S(1)} %get-tuple-element.73.mid_high, ...), custom_call_target="tpu_custom_call" | custom-call | flops 2835349504 | bytes 12582912 | tf_op jit(solution)/shard_map/inner1/pallas_call | solution.py:560
  36.1 0.0 collective-permute-done.6.from_low
  36.1 0.0 collective-permute-done.7.from_high
  36.2 0.0 copy-start
  36.2 0.0 copy-start.4
  36.2 2.0 %outer1.1 = (f32[6,64,256]{2,1,0:T(8,128)S(1)}, f32[2,32,256]{2,1,0:T(8,128)S(1)}) custom-call(f32[6,64,256]{2,1,0:T(8,128)S(1)} %get-tuple-element.72.end, bf16[26,64,256]{2,1,0:T(8,128)(2,1)S(1)} %get-tuple-element.73.mid_high, bf16[6,64,256]{2,1,0:T(8,128)(2,1)S(1)} %get-tuple-element.74.end_high, bf16[26,64,256]{2,1,0:T(8,128)(2,1)S(1)} %get-tuple-element.75.mid_low, ...), custom_call_target="tpu_custom_call" | custom-call | flops 872415232 | bytes 6291456 | tf_op jit(solution)/shard_map/outer1/pallas_call | solution.py:570
  38.2 2.6 %collective-permute-start.8 = (f32[2,32,256]{2,1,0:T(8,128)S(1)}, f32[2,32,256]{2,1,0:T(8,128)S(1)}, u32[]{:S(2)}, u32[]{:S(2)}) collective-permute-start(f32[2,32,256]{2,1,0:T(8,128)S(1)} %get-tuple-element.83.own_sums), channel_id=1, source_target_pairs={{0,1},{1,0},{2,3},{3,2},{4,5},{5,4},{6,7},{7,6},{8,9},{9,8},{10,11... | collective-permute-start | bytes 196616 | tf_op jit(solution)/shard_map/ppermute | solution.py:580
  40.7 0.9 %collective-permute-done.8.partner_sums = f32[2,32,256]{2,1,0:T(8,128)S(1)} collective-permute-done((f32[2,32,256]{2,1,0:T(8,128)S(1)}, f32[2,32,256]{2,1,0:T(8,128)S(1)}, u32[]{:S(2)}, u32[]{:S(2)}) %collective-permute-start.8) | collective-permute-done | bytes 65568 | tf_op jit(solution)/shard_map/ppermute | solution.py:580
  41.7 0.0 copy-done
  41.7 0.6 %mix.3 = (f32[32,256]{1,0:T(8,128)S(1)}, f32[2,32,256]{2,1,0:T(8,128)S(1)}) custom-call(f32[2,32,256]{2,1,0:T(8,128)S(1)} %get-tuple-element.83.own_sums, f32[2,32,256]{2,1,0:T(8,128)S(1)} %collective-permute-done.8.partner_sums, f32[4,8]{1,0:T(4,128)S(1)} %copy-done), custom_call_target="tpu_custom_call" | custom-call | bytes 1048576 | tf_op jit(solution)/shard_map/mix/pallas_call | solution.py:581
  42.3 0.0 copy-start.3
  42.3 2.5 %collective-permute-start.9 = (f32[32,256]{1,0:T(8,128)S(1)}, f32[32,256]{1,0:T(8,128)S(1)}, u32[]{:S(2)}, u32[]{:S(2)}) collective-permute-start(f32[32,256]{1,0:T(8,128)S(1)} %get-tuple-element.90), channel_id=1, source_target_pairs={{0,2},{2,0},{1,3},{3,1},{4,6},{6,4},{5,7},{7,5},{8,10},{10,8},{9,1... | collective-permute-start | bytes 98312 | tf_op jit(solution)/shard_map/ppermute | solution.py:585
  44.8 0.0 copy-done.4
  44.8 2.2 %sweep.1.swept = f32[64,32,256]{2,1,0:T(8,128)S(1)} custom-call(f32[26,64,256]{2,1,0:T(8,128)S(1)} %get-tuple-element.87.mid, f32[6,64,256]{2,1,0:T(8,128)S(1)} %get-tuple-element.88.end, f32[4,128]{1,0:T(4,128)S(1)} %copy-done.4), custom_call_target="tpu_custom_call" | custom-call | flops 20971520 | bytes 4194304 | tf_op jit(solution)/shard_map/sweep/pallas_call | solution.py:586
  47.0 0.0 collective-permute-done.9.far
  47.1 0.0 copy-done.3
  47.1 2.0 %finish.1 = f32[64,32,256]{2,1,0:T(8,128)} custom-call(f32[64,32,256]{2,1,0:T(8,128)S(1)} %sweep.1.swept, f32[2,32,256]{2,1,0:T(8,128)S(1)} %get-tuple-element.89.near, f32[32,256]{1,0:T(8,128)S(1)} %collective-permute-done.9.far, f32[4,8]{1,0:T(4,128)S(1)} %copy-done, f32[4,128]{1,0:T(4,128)S(1)} %copy-done.3), custom_call_target="tpu_custom_call" | custom-call | bytes 6291456 | tf_op jit(solution)/shard_map/finish/pallas_call | solution.py:590
Async XLA Ops:
  0.0 5.9 %copy-start.2 = (f32[28]{0:T(128)S(1)}, f32[28]{0:T(128)}, u32[]{:S(2)}) copy-start(f32[28]{0:T(128)} %weight.9) | copy-start | bytes 340
  0.0 5.9 %copy-start.7 = (f32[4]{0:T(128)S(1)}, f32[4]{0:T(128)}, u32[]{:S(2)}) copy-start(f32[4]{0:T(128)} %rate.1) | copy-start | bytes 52
  0.0 5.9 %copy-start.6 = (f32[4]{0:T(128)S(1)}, f32[4]{0:T(128)}, u32[]{:S(2)}) copy-start(f32[4]{0:T(128)} %diffusivity.1) | copy-start | bytes 52
  0.0 5.9 %copy-start.5 = (s32[28,2]{0,1:T(2,128)S(1)}, s32[28,2]{0,1:T(2,128)}, u32[]{:S(2)}) copy-start(s32[28,2]{0,1:T(2,128)} %param.15) | copy-start | bytes 676
  2.2 9.3 %collective-permute-start = (f32[2,64,128]{2,1,0:T(8,128)S(1)}, f32[2,64,128]{2,1,0:T(8,128)S(1)}, u32[]{:S(2)}, u32[]{:S(2)}) collective-permute-start(f32[2,64,128]{2,1,0:T(8,128)S(1)} %get-tuple-element.53.lasts), channel_id=1, source_target_pairs={{0,4},{4,8},{8,12},{12,0},{1,5},{5,9},{9,13},{13,1},{2,6},{6,10},{... | collective-permute-start | bytes 196616 | tf_op jit(solution)/shard_map/ppermute | solution.py:532
  4.4 7.1 %collective-permute-start.1 = (f32[2,64,128]{2,1,0:T(8,128)S(1)}, f32[2,64,128]{2,1,0:T(8,128)S(1)}, u32[]{:S(2)}, u32[]{:S(2)}) collective-permute-start(f32[2,64,128]{2,1,0:T(8,128)S(1)} %get-tuple-element.54.firsts), channel_id=1, source_target_pairs={{0,12},{4,0},{8,4},{12,8},{1,13},{5,1},{9,5},{13,9},{2,14},{6,2},{... | collective-permute-start | bytes 196616 | tf_op jit(solution)/shard_map/ppermute | solution.py:532
  5.9 15.2 %copy-start.1 = (f32[4,128]{1,0:T(4,128)S(1)}, f32[4,128]{1,0:T(4,128)}, u32[]{:S(2)}) copy-start(f32[4,128]{1,0:T(4,128)} %constant.8.clone.sums) | copy-start | bytes 6148
  11.8 13.7 %collective-permute-start.2 = (f32[7,64,128]{2,1,0:T(8,128)S(1)}, f32[7,64,128]{2,1,0:T(8,128)S(1)}, u32[]{:S(2)}, u32[]{:S(2)}) collective-permute-start(f32[7,64,128]{2,1,0:T(8,128)S(1)} %get-tuple-element.60), channel_id=1, source_target_pairs={{0,16},{16,32},{32,48},{48,64},{64,80},{80,96},{96,112},{112,128},... | collective-permute-start | bytes 688136 | tf_op jit(solution)/shard_map/ppermute | solution.py:532
  13.5 12.0 %collective-permute-start.3 = (f32[7,64,128]{2,1,0:T(8,128)S(1)}, f32[7,64,128]{2,1,0:T(8,128)S(1)}, u32[]{:S(2)}, u32[]{:S(2)}) collective-permute-start(f32[7,64,128]{2,1,0:T(8,128)S(1)} %get-tuple-element.61), channel_id=1, source_target_pairs={{0,240},{16,0},{32,16},{48,32},{64,48},{80,64},{96,80},{112,96},{1... | collective-permute-start | bytes 688136 | tf_op jit(solution)/shard_map/ppermute | solution.py:532
  18.4 7.1 %collective-permute-start.4 = (f32[2,64,128]{2,1,0:T(8,128)S(1)}, f32[2,64,128]{2,1,0:T(8,128)S(1)}, u32[]{:S(2)}, u32[]{:S(2)}) collective-permute-start(f32[2,64,128]{2,1,0:T(8,128)S(1)} %get-tuple-element.69), channel_id=1, source_target_pairs={{0,4},{4,8},{8,12},{12,0},{1,5},{5,9},{9,13},{13,1},{2,6},{6,10},{... | collective-permute-start | bytes 196616 | tf_op jit(solution)/shard_map/ppermute | solution.py:532
  18.4 7.1 %collective-permute-start.5 = (f32[2,64,128]{2,1,0:T(8,128)S(1)}, f32[2,64,128]{2,1,0:T(8,128)S(1)}, u32[]{:S(2)}, u32[]{:S(2)}) collective-permute-start(f32[2,64,128]{2,1,0:T(8,128)S(1)} %get-tuple-element.70), channel_id=1, source_target_pairs={{0,12},{4,0},{8,4},{12,8},{1,13},{5,1},{9,5},{13,9},{2,14},{6,2},{... | collective-permute-start | bytes 196616 | tf_op jit(solution)/shard_map/ppermute | solution.py:532
  27.4 8.8 %collective-permute-start.6 = (f32[7,64,128]{2,1,0:T(8,128)S(1)}, f32[7,64,128]{2,1,0:T(8,128)S(1)}, u32[]{:S(2)}, u32[]{:S(2)}) collective-permute-start(f32[7,64,128]{2,1,0:T(8,128)S(1)} %get-tuple-element.79), channel_id=1, source_target_pairs={{0,16},{16,32},{32,48},{48,64},{64,80},{80,96},{96,112},{112,128},... | collective-permute-start | bytes 688136 | tf_op jit(solution)/shard_map/ppermute | solution.py:532
  27.5 8.7 %collective-permute-start.7 = (f32[7,64,128]{2,1,0:T(8,128)S(1)}, f32[7,64,128]{2,1,0:T(8,128)S(1)}, u32[]{:S(2)}, u32[]{:S(2)}) collective-permute-start(f32[7,64,128]{2,1,0:T(8,128)S(1)} %get-tuple-element.80), channel_id=1, source_target_pairs={{0,240},{16,0},{32,16},{48,32},{64,48},{80,64},{96,80},{112,96},{1... | collective-permute-start | bytes 688136 | tf_op jit(solution)/shard_map/ppermute | solution.py:532
  36.2 5.5 %copy-start = (f32[4,8]{1,0:T(4,128)S(1)}, f32[4,8]{1,0:T(4,128)}, u32[]{:S(2)}) copy-start(f32[4,8]{1,0:T(4,128)} %constant.11.clone.mix) | copy-start | bytes 388
  36.2 8.6 %copy-start.4 = (f32[4,128]{1,0:T(4,128)S(1)}, f32[4,128]{1,0:T(4,128)}, u32[]{:S(2)}) copy-start(f32[4,128]{1,0:T(4,128)} %constant.9.clone.solve) | copy-start | bytes 6148
  38.2 3.5 %collective-permute-start.8 = (f32[2,32,256]{2,1,0:T(8,128)S(1)}, f32[2,32,256]{2,1,0:T(8,128)S(1)}, u32[]{:S(2)}, u32[]{:S(2)}) collective-permute-start(f32[2,32,256]{2,1,0:T(8,128)S(1)} %get-tuple-element.83.own_sums), channel_id=1, source_target_pairs={{0,1},{1,0},{2,3},{3,2},{4,5},{5,4},{6,7},{7,6},{8,9},{9,8},{10,11... | collective-permute-start | bytes 196616 | tf_op jit(solution)/shard_map/ppermute | solution.py:580
  42.3 4.8 %copy-start.3 = (f32[4,128]{1,0:T(4,128)S(1)}, f32[4,128]{1,0:T(4,128)}, u32[]{:S(2)}) copy-start(f32[4,128]{1,0:T(4,128)} %constant.10.clone.reply) | copy-start | bytes 6148
  42.3 4.8 %collective-permute-start.9 = (f32[32,256]{1,0:T(8,128)S(1)}, f32[32,256]{1,0:T(8,128)S(1)}, u32[]{:S(2)}, u32[]{:S(2)}) collective-permute-start(f32[32,256]{1,0:T(8,128)S(1)} %get-tuple-element.90), channel_id=1, source_target_pairs={{0,2},{2,0},{1,3},{3,1},{4,6},{6,4},{5,7},{7,5},{8,10},{10,8},{9,1... | collective-permute-start | bytes 98312 | tf_op jit(solution)/shard_map/ppermute | solution.py:585

commit v5 on v4

--- a/solution.py
+++ b/solution.py
@@ -19,6 +19,7 @@
 VMEM = pl.BlockSpec(memory_space=pltpu.VMEM)
 SMEM = pl.BlockSpec(memory_space=pltpu.SMEM)
 HBM = pl.BlockSpec(memory_space=pltpu.HBM)
+ANY = pl.BlockSpec(memory_space=pl.ANY)
 SEM = pltpu.SemaphoreType.DMA
 
 
@@ -59,6 +60,11 @@
     return jnp.where(lanes() % 8 < 4, left, right)
 
 
+def by_parity(axis, first, second):
+    even = lanes() < jnp.where(lax.axis_index(axis) % 2 == 0, 128, 0)
+    return jnp.where(even, first, second), jnp.where(even, second, first)
+
+
 def split(value):
     high = value.astype(bf16)
     return high, (value - high.astype(f32)).astype(bf16)
@@ -86,7 +92,11 @@
     return total
 
 
-def prepare_kernel(offsets, weight, diffusivity, rate, pit, phase, damage, mid, end, w_ref, move, gain, table, to_high, to_low, middle, pv, hv, dv, sem):
+def prepare_kernel(
+    offsets_in, weight_in, diffusivity_in, rate_in, pit, phase, damage, mid, end,
+    w_ref, move, gain, table_rows, to_high, to_low, middle,
+    pv, hv, dv, offsets, weight, diffusivity, rate, table, sem, scalar_sem,
+):
     def copies(group):
         return [
             pltpu.make_async_copy(source.at[:, x, :], target.at[x], sem.at[group])
@@ -94,14 +104,27 @@
             for source, target in ((pit, pv), (phase, hv), (damage, dv))
         ]
 
+    scalar_copies = [
+        pltpu.make_async_copy(source, target, scalar_sem.at[i])
+        for i, (source, target) in enumerate(
+            ((offsets_in, offsets), (weight_in, weight), (diffusivity_in, diffusivity), (rate_in, rate))
+        )
+    ]
+    for copy in scalar_copies:
+        copy.start()
     for group in range(4):
         for copy in copies(group):
             copy.start()
+    for copy in scalar_copies:
+        copy.wait()
     for place in range(49):
         table[place] = jnp.float32(0.0)
     for bond in range(BONDS):
         place = (offsets[0, bond] + 3) * 7 + offsets[1, bond] + 3
         table[place] = table[place] + weight[bond]
+    for place in range(49):
+        table_rows[place : place + 1, :] = jnp.full((1, 128), table[place], f32)
+    table_rows[49:50, :] = jnp.full((1, 128), total_weight(weight), f32)
     diff = lax.broadcasted_iota(jnp.int32, (128, 128), 0) - lax.broadcasted_iota(jnp.int32, (128, 128), 1) + 3
     blank = jnp.zeros((128, 128), bf16)
     for start in (0, 4):
@@ -158,7 +181,7 @@
             low = at_lanes(low, gain[x, :, :128], 0, slot, 3)
             low = at_lanes(low, move[x, :, :128], 0, slot + 4, 3)
         if group % 2:
-            to_high[group // 2], to_low[group // 2] = high, low
+            to_high[group // 2], to_low[group // 2] = by_parity("gy", high, low)
 
 
 def right_side(w_ref):
@@ -206,7 +229,7 @@
             high_side = at_lanes(high_side, row[:, 128:], 122, slot, 6)
             low_side = at_lanes(low_side, row[:, :128], 0, slot, 6)
         if group % 2:
-            lasts[group // 2], firsts[group // 2] = high_side, low_side
+            lasts[group // 2], firsts[group // 2] = by_parity("gy", high_side, low_side)
     fill_slabs(lambda row: buf[OUTER[row]], up, down)
     down[6] = jnp.zeros((DZ, 128), f32)
     up[6] = jnp.zeros((DZ, 128), f32)
@@ -216,27 +239,29 @@
     for row in range(3):
         for half in range(2):
             part = slice(128 * half, 128 * half + 128)
-            down[2 * row + half] = row_of(row)[:, part]
-            up[2 * row + half] = row_of(3 + row)[:, part]
-
-
-def join_kernel(left, right, lasts, firsts, up_in, down_in, strips, up, down):
+            up[2 * row + half], down[2 * row + half] = by_parity("gx", row_of(3 + row)[:, part], row_of(row)[:, part])
+
+
+def join_kernel(y_first, y_second, own_first, own_second, up_in, down_in, strips, up, down):
     for group in range(2):
-        strips[0, group] = two_sides(left[group], pltpu.roll(lasts[group], 1, 1))
-        strips[1, group] = two_sides(pltpu.roll(left[group], 125, 1), pltpu.roll(right[group], 4, 1))
-        strips[2, group] = two_sides(firsts[group], pltpu.roll(right[group], 1, 1))
+        right, left = by_parity("gy", y_first[group], y_second[group])
+        lasts, firsts = by_parity("gy", own_first[group], own_second[group])
+        strips[0, group] = two_sides(left, pltpu.roll(lasts, 1, 1))
+        strips[1, group] = two_sides(pltpu.roll(left, 125, 1), pltpu.roll(right, 4, 1))
+        strips[2, group] = two_sides(firsts, pltpu.roll(right, 1, 1))
     for slab in range(6):
         up[slab] = up_in[slab]
         down[slab] = down_in[slab]
     lane = lanes()
-    up[6] = jnp.where(
+    to_next = jnp.where(
         lane >= 104, strips[1, 1],
         jnp.where(lane >= 72, pltpu.roll(strips[0, 1], 96, 1), pltpu.roll(strips[2, 1], 64, 1)),
     )
-    down[6] = jnp.where(
+    to_last = jnp.where(
         lane < 32, strips[1, 0],
         jnp.where(lane < 64, pltpu.roll(strips[0, 0], 32, 1), pltpu.roll(strips[2, 0], 64, 1)),
     )
+    up[6], down[6] = by_parity("gx", to_next, to_last)
 
 
 def strip_taps(table, first, second, third):
@@ -256,9 +281,10 @@
     ]
     sums = []
     for a in range(7):
-        total = table[7 * a] * columns[0]
+        total = table[7 * a : 7 * a + 1, :] * columns[0]
         for second_index in range(1, 7):
-            total = total + table[7 * a + second_index] * columns[second_index]
+            place = 7 * a + second_index
+            total = total + table[place : place + 1, :] * columns[second_index]
         sums.append(total)
     return sums
 
@@ -282,11 +308,11 @@
 
 
 def inner_kernel(
-    last, mid, mid_high, end_high, mid_low, end_low, strips, middle, move, gain, w_ref, weight, sums, table,
+    last, mid, mid_high, end_high, mid_low, end_low, strips, middle, move, gain, w_ref, sums, table,
     out, out_high, out_low, extra, new_middle,
 ):
     halo = strips.at[0 if last else 1]
-    weight_sum = total_weight(weight)
+    weight_sum = table[49:50, :]
     pairs = range(3, DX - 3, 2)
 
     def row_of(mid_part, end_part):
@@ -328,31 +354,34 @@
 
 def depth_sums(rows, sums, extra, start, count, first):
     own = lax.axis_index("gz")
-    below = jnp.zeros((count, DY), f32)
-    above = jnp.zeros((count, DY), f32)
-    for z in range(DZ):
-        value = rows[first : first + count, z, :]
-        below = below + sums[own, z] * value
-        above = above + sums[own, DZ + z] * value
-    extra[0, start : start + count, :] = below
-    extra[1, start : start + count, :] = above
+    for half in range(2):
+        part = slice(128 * half, 128 * half + 128)
+        below = jnp.zeros((count, 128), f32)
+        above = jnp.zeros((count, 128), f32)
+        for z in range(DZ):
+            value = rows[first : first + count, z, part]
+            below = below + sums[own, z : z + 1, :] * value
+            above = above + sums[own, DZ + z : DZ + z + 1, :] * value
+        extra[0, start : start + count, part] = below
+        extra[1, start : start + count, part] = above
 
 
 def outer_kernel(
-    last, end, mid_high, end_high, mid_low, end_low, strips, middle, from_low, from_high, move, gain, w_ref, weight,
-    sums, extra_in, *rest,
+    last, end, mid_high, end_high, mid_low, end_low, strips, middle, x_first, x_second, move, gain, w_ref,
+    sums, table, extra_in, *rest,
 ):
     if last:
         out, extra = rest
     else:
-        table, coefs_left, coefs_right, middle_in, out, out_high, out_low, extra, up, down, new_middle = rest
+        coefs_first, coefs_second, middle_in, out, out_high, out_low, extra, up, down, new_middle = rest
     halo = strips.at[0 if last else 1]
-    weight_sum = total_weight(weight)
+    weight_sum = table[49:50, :]
     zero = jnp.zeros((DZ, 128), f32)
 
     def halo_rows(slabs):
         return [jnp.concatenate([slabs[2 * row], slabs[2 * row + 1]], axis=1) for row in range(3)]
 
+    from_high, from_low = zip(*(by_parity("gx", x_first[slab], x_second[slab]) for slab in range(7)))
     low_rows, high_rows = halo_rows(from_low), halo_rows(from_high)
     low_split, high_split = [split(row) for row in low_rows], [split(row) for row in high_rows]
     low_middle, high_middle = zero, zero
@@ -413,13 +442,12 @@
         taps = [None, None, strip_taps(table, *beyond)]
         for group in range(2):
             flux = extra_in[group] + strip_flux(taps, group)
-            left, right = coefs_left[group], coefs_right[group]
+            right, left = by_parity("gy", coefs_first[group], coefs_second[group])
             extra[0, group] = stepped(
                 halo[group], flux, two_sides(left, right),
                 two_sides(pltpu.roll(left, 124, 1), pltpu.roll(right, 4, 1)), weight_sum,
             )
-        up[6] = extra[0, 1]
-        down[6] = extra[0, 0]
+        up[6], down[6] = by_parity("gx", extra[0, 1], extra[0, 0])
 
 
 def depth_tables():
@@ -477,17 +505,25 @@
             mix[block, 4] = from_above(block, partner)
         else:
             mix[block, 6] = from_below(block, partner)
-    return [jnp.asarray(table, f32) for table in (sums, solve, reply, mix)]
-
-
-def mix_kernel(own_sums, partner_sums, mix, send, near):
+    rows = [jnp.asarray(np.repeat(table[:, :, None], 128, axis=2), f32) for table in (sums, reply)]
+    return rows[0], jnp.asarray(solve, f32), rows[1], mix
+
+
+def own_of(mix, column):
     own = lax.axis_index("gz")
+    value = jnp.float32(mix[0, column])
+    for block in range(1, 4):
+        value = jnp.where(own == block, jnp.float32(mix[block, column]), value)
+    return value
+
+
+def mix_kernel(mix, own_sums, partner_sums, send, near):
     send[...] = (
-        mix[own, 0] * own_sums[0] + mix[own, 1] * partner_sums[0]
-        + mix[own, 2] * own_sums[1] + mix[own, 3] * partner_sums[1]
+        own_of(mix, 0) * own_sums[0] + own_of(mix, 1) * partner_sums[0]
+        + own_of(mix, 2) * own_sums[1] + own_of(mix, 3) * partner_sums[1]
     )
-    near[0] = mix[own, 4] * partner_sums[0]
-    near[1] = mix[own, 6] * partner_sums[1]
+    near[0] = own_of(mix, 4) * partner_sums[0]
+    near[1] = own_of(mix, 6) * partner_sums[1]
 
 
 def sweep_kernel(mid, end, solve, sweep, buf):
@@ -509,27 +545,36 @@
         sweep[z] = 2.0 * value - buf[z]
 
 
-def finish_kernel(swept, near, far, mix, reply, out, buf, out_sem):
+def finish_kernel(mix, swept, near, far, reply, out, buf, out_sem):
     own = lax.axis_index("gz")
-    above = near[0] + mix[own, 5] * far[...]
-    below = near[1] + mix[own, 7] * far[...]
-    parts = range(0, DZ, 16)
+    above = near[0] + own_of(mix, 5) * far[...]
+    below = near[1] + own_of(mix, 7) * far[...]
+    size = 8
 
     def copy(z):
-        part = pl.ds(z, 16)
-        return pltpu.make_async_copy(buf.at[part], out.at[part], out_sem.at[z // 16])
-
-    for start in parts:
-        for z in range(start, start + 16):
-            buf[z] = swept[z] + reply[own, z] * above + reply[own, DZ + z] * below
+        part = pl.ds(z, size)
+        return pltpu.make_async_copy(buf.at[part], out.at[part], out_sem.at[z // size])
+
+    for start in range(0, DZ, size):
+        for z in range(start, start + size):
+            for half in range(2):
+                part = slice(128 * half, 128 * half + 128)
+                buf[z, :, part] = (
+                    swept[z, :, part] + reply[own, z : z + 1, :] * above[:, part]
+                    + reply[own, DZ + z : DZ + z + 1, :] * below[:, part]
+                )
         copy(start).start()
-    for start in parts:
+    for start in range(0, DZ, size):
         copy(start).wait()
 
 
-def shift(value, axis, step):
+def swaps(first, second, axis):
     count = lax.axis_size(axis)
-    return lax.ppermute(value, axis, [(i, (i + step) % count) for i in range(count)])
+    moved = []
+    for start, value in ((0, first), (1, second)):
+        pairs = [(i, (i + 1) % count) for i in range(start, count, 2)]
+        moved.append(lax.ppermute(value, axis, pairs + [(target, source) for source, target in pairs]))
+    return moved
 
 
 def local(conc, pit, phase, offsets, damage, weight, diffusivity, rate):
@@ -538,11 +583,13 @@
         first_kernel, "first", PARTS + (PACK, PACK, SLABS, SLABS), [HBM], (VMEM,) * 10,
         [pltpu.VMEM((DX, DZ, DY), f32), SEM((4,))], nbytes=4 << 20, limit=48,
     )(conc)
-    left, right = shift(lasts, "gy", 1), shift(firsts, "gy", -1)
+    left, right = swaps(lasts, firsts, "gy")
     w, move, gain, table, to_high, to_low, middle = call(
-        prepare_kernel, "prepare", (struct(9, DY, DY, dtype=bf16), WHOLE, WHOLE, struct(64), PACK, PACK, PACK),
-        [SMEM] * 4 + [HBM] * 3 + [VMEM] * 2, (VMEM, VMEM, VMEM, SMEM, VMEM, VMEM, VMEM),
-        [pltpu.VMEM((DX, DZ, DY), jnp.int32)] * 3 + [SEM((4,))],
+        prepare_kernel, "prepare", (struct(9, DY, DY, dtype=bf16), WHOLE, WHOLE, struct(56, 128), PACK, PACK, PACK),
+        [ANY] * 4 + [HBM] * 3 + [VMEM] * 2, (VMEM,) * 7,
+        [pltpu.VMEM((DX, DZ, DY), jnp.int32)] * 3
+        + [pltpu.SMEM((2, BONDS), jnp.int32), pltpu.SMEM((BONDS,), f32), pltpu.SMEM((4,), f32), pltpu.SMEM((4,), f32)]
+        + [pltpu.SMEM((64,), f32), SEM((4,)), SEM((4,))],
         nbytes=8 << 20, limit=45,
     )(offsets.T, weight, diffusivity, rate, pit, phase, damage, parts[0], parts[1])
     strips, up, down = call(
@@ -550,21 +597,21 @@
     )(left, right, lasts, firsts, up, down)
     for substep in range(2):
         last = substep == 1
-        from_low, from_high = shift(up, "gx", 1), shift(down, "gx", -1)
+        x_first, x_second = swaps(up, down, "gx")
         if not last:
             to_high, to_low, up, down = lax.optimization_barrier((to_high, to_low, up, down))
-            coefs = [shift(to_high, "gy", 1), shift(to_low, "gy", -1)]
+            coefs = swaps(to_high, to_low, "gy")
         mid, end, mid_high, end_high, mid_low, end_low = parts
         tiny = struct(1, 16, 128, dtype=bf16)
         inner_split = (tiny, tiny) if last else (PARTS[2], PARTS[4])
         new_mid, new_mid_high, new_mid_low, more, more_middle = call(
             functools.partial(inner_kernel, last), f"inner{substep}",
             (PARTS[0],) + inner_split + ((struct(2, DX, DY) if last else PACK), struct(1, 8, 128) if last else PACK),
-            [VMEM] * 10 + [SMEM] * 3, (VMEM,) * 5, flops=2 * INNER * DZ * DY * 3328, nbytes=12 << 20,
-        )(mid, mid_high, end_high, mid_low, end_low, strips, middle, move, gain, w, weight, sums, table)
-        args = (end, mid_high, end_high, mid_low, end_low, strips, middle, from_low, from_high, move, gain, w, weight)
-        args = args + (sums, more)
-        specs = [VMEM] * 12 + [SMEM] * 2 + [VMEM]
+            [VMEM] * 12, (VMEM,) * 5, flops=2 * INNER * DZ * DY * 3328, nbytes=12 << 20,
+        )(mid, mid_high, end_high, mid_low, end_low, strips, middle, move, gain, w, sums, table)
+        args = (end, mid_high, end_high, mid_low, end_low, strips, middle, x_first, x_second, move, gain, w)
+        args = args + (sums, table, more)
+        specs = [VMEM] * 15
         cost = dict(flops=2 * 8 * DZ * DY * 3328, nbytes=6 << 20)
         if last:
             new_end, ends = call(
@@ -574,13 +621,13 @@
             new_end, new_end_high, new_end_low, strips, up, down, middle = call(
                 functools.partial(outer_kernel, last), "outer0",
                 (PARTS[1], PARTS[3], PARTS[5], struct(1, 2, DZ, 128), SLABS, SLABS, PACK),
-                specs + [SMEM, VMEM, VMEM, VMEM], (VMEM,) * 7, **cost,
-            )(*args, table, *coefs, more_middle)
+                specs + [VMEM] * 3, (VMEM,) * 7, **cost,
+            )(*args, *coefs, more_middle)
             parts = [new_mid, new_end, new_mid_high, new_end_high, new_mid_low, new_end_low]
     partner = lax.ppermute(ends, "gz", [(0, 1), (1, 0), (2, 3), (3, 2)])
     send, near = call(
-        mix_kernel, "mix", (struct(DX, DY), struct(2, DX, DY)), [VMEM, VMEM, SMEM], (VMEM,) * 2,
-    )(ends, partner, mix)
+        functools.partial(mix_kernel, mix), "mix", (struct(DX, DY), struct(2, DX, DY)), [VMEM, VMEM], (VMEM,) * 2,
+    )(ends, partner)
     send, new_mid, new_end = lax.optimization_barrier((send, new_mid, new_end))
     far = lax.ppermute(send, "gz", [(0, 2), (2, 0), (1, 3), (3, 1)])
     swept = call(
@@ -588,9 +635,9 @@
         flops=20 << 20, nbytes=4 << 20,
     )(new_mid, new_end, solve)
     return call(
-        finish_kernel, "finish", struct(DZ, DX, DY), [VMEM, VMEM, VMEM, SMEM, SMEM], HBM,
-        [pltpu.VMEM((DZ, DX, DY), f32), SEM((4,))], nbytes=6 << 20,
-    )(swept, near, far, mix, reply)
+        functools.partial(finish_kernel, mix), "finish", struct(DZ, DX, DY), [VMEM] * 4, HBM,
+        [pltpu.VMEM((DZ, DX, DY), f32), SEM((8,))], nbytes=6 << 20,
+    )(swept, near, far, reply)
 
 
 def solution(mesh):

time: 49.4 us -> 45 us (0.911)
  Pallas kernels: 26.1 us -> 21.5 us
    ppermute x1, starting transfers between devices: 2.58 us -> 3.85 us  [local(): partner = lax.ppermute(ends, 'gz', [(0, 1), (1, 0), (2, 3), (3, 2)])]
    ppermute x8, starting transfers between devices: 16.7 us -> 15.5 us  [swaps(): lax.ppermute(value, axis, pairs + [(target, source) for source, target in...]
    pallas_call x2, Pallas kernels: 2.62 us -> 1.45 us  [the longest x1 1.43 us: local(): call(functools.partial(finish_kernel, mix), 'finish', struct(DZ, DX, DY),...]
    pallas_call x2, Pallas kernels: 9.46 us -> 8.34 us  [local(): call(functools.partial(inner_kernel, last), f'inner{substep}', (PARTS[0],...]
    pallas_call x1, Pallas kernels: 5.57 us -> 4.49 us  [local(): call(prepare_kernel, 'prepare', (struct(9, DY, DY, dtype=bf16), WHOLE, WH...]
    pallas_call x1, Pallas kernels: 1.98 us -> 1.38 us  [local(): call(functools.partial(outer_kernel, last), 'outer1', (PARTS[1], struct(2...]
    pallas_call x1, Pallas kernels: 1.85 us -> 1.29 us  [local(): call(functools.partial(outer_kernel, last), 'outer0', (PARTS[1], PARTS[3]...]
  transfers between devices with their start and end apart: 10 -> 10, of which waited for: 1 -> 2; matrix products, arithmetic and copies ran while one was open for 0% -> 0% of each run, Pallas kernels for 35% -> 33%
where the time goes in v5:
time: 45 us; the launch traced here: 44.9 us
  starting transfers between devices  21.9 us (49%)
  Pallas kernels  21.5 us (48%)
  waiting for transfers between devices  1.08 us (2%)
    ppermute x8, starting transfers between devices, swaps(): lax.ppermute(value, axis, pairs + [(target, source) for source, target in...  15.5 us
    pallas_call x2, Pallas kernels, local(): call(functools.partial(inner_kernel, last), f'inner{substep}', (PARTS[0],...  8.34 us
    pallas_call x1, Pallas kernels, local(): call(prepare_kernel, 'prepare', (struct(9, DY, DY, dtype=bf16), WHOLE, WH...  4.49 us
    ppermute x1, starting transfers between devices, local(): partner = lax.ppermute(ends, 'gz', [(0, 1), (1, 0), (2, 3), (3, 2)])  3.85 us
    ppermute x1, starting transfers between devices, local(): far = lax.ppermute(send, 'gz', [(0, 2), (2, 0), (1, 3), (3, 1)])  2.53 us
    pallas_call x1, Pallas kernels, local(): call(sweep_kernel, 'sweep', struct(DZ, DX, DY), [VMEM, VMEM, SMEM], VMEM,...  2.2 us
    pallas_call x1, Pallas kernels, local(): call(first_kernel, 'first', PARTS + (PACK, PACK, SLABS, SLABS), [HBM], (V...  2.18 us
    pallas_call x1, Pallas kernels, local(): call(functools.partial(finish_kernel, mix), 'finish', struct(DZ, DX, DY),...  1.43 us
  transfers between devices with their start and end apart: 10, of which 2 were waited for; matrix products, arithmetic and copies ran while one was open for 0% of the time, Pallas kernels for 33%

profile of v5, /device:TPU:1, one launch (start us, length us, event | category | flops | bytes accessed | tf_op | source)
XLA Modules:
  0.0 44.9 jit_solution(16095375826392156074)
XLA Ops:
  0.0 0.0 copy-start.6
  0.0 0.0 copy-start.5
  0.0 0.0 copy-start.4
  0.0 0.0 copy-start.3
  0.0 2.2 %first.1 = (f32[26,64,256]{2,1,0:T(8,128)S(1)}, f32[6,64,256]{2,1,0:T(8,128)S(1)}, bf16[26,64,256]{2,1,0:T(8,128)(2,1)S(1)}, bf16[6,64,256]{2,1,0:T(8,128)(2,1)S...) custom-call(f32[64,32,256]{2,1,0:T(8,128)} %conc.1), custom_call_target="tpu_custom_call" | custom-call | bytes 4194304 | tf_op jit(solution)/shard_map/first/pallas_call | solution.py:582
  2.2 2.2 %collective-permute-start = (f32[2,64,128]{2,1,0:T(8,128)S(1)}, f32[2,64,128]{2,1,0:T(8,128)S(1)}, u32[]{:S(2)}, u32[]{:S(2)}) collective-permute-start(f32[2,64,128]{2,1,0:T(8,128)S(1)} %get-tuple-element.53.own_first), channel_id=1, source_target_pairs={{0,4},{8,12},{4,0},{12,8},{1,5},{9,13},{5,1},{13,9},{2,6},{10,14},... | collective-permute-start | bytes 196616 | tf_op jit(solution)/shard_map/ppermute | solution.py:576
  4.4 1.9 %collective-permute-start.1 = (f32[2,64,128]{2,1,0:T(8,128)S(1)}, f32[2,64,128]{2,1,0:T(8,128)S(1)}, u32[]{:S(2)}, u32[]{:S(2)}) collective-permute-start(f32[2,64,128]{2,1,0:T(8,128)S(1)} %get-tuple-element.54.own_second), channel_id=1, source_target_pairs={{4,8},{12,0},{8,4},{0,12},{5,9},{13,1},{9,5},{1,13},{6,10},{14,2},... | collective-permute-start | bytes 196616 | tf_op jit(solution)/shard_map/ppermute | solution.py:576
  6.3 0.0 copy-done.6
  6.3 0.0 copy-done.5
  6.3 0.0 copy-done.4
  6.3 0.0 copy-done.3
  6.3 0.0 copy-start
  6.3 4.5 %prepare.1 = (bf16[9,256,256]{2,1,0:T(8,128)(2,1)S(1)}, f32[32,64,256]{2,1,0:T(8,128)S(1)}, f32[32,64,256]{2,1,0:T(8,128)S(1)}, f32[56,128]{1,0:T(8,128)S(1)}, f...) custom-call(s32[2,28]{1,0:T(2,128)S(1)} %bitcast.1, f32[28]{0:T(128)S(1)} %copy-done.4, ...), custom_call_target="tpu_custom_call" | custom-call | bytes 8388608 | tf_op jit(solution)/shard_map/prepare/pallas_call | solution.py:587
  10.8 0.0 collective-permute-done.y_first
  10.8 0.0 collective-permute-done.1.y_second
  10.8 0.2 join.1
  11.1 1.7 %collective-permute-start.2 = (f32[7,64,128]{2,1,0:T(8,128)S(1)}, f32[7,64,128]{2,1,0:T(8,128)S(1)}, u32[]{:S(2)}, u32[]{:S(2)}) collective-permute-start(f32[7,64,128]{2,1,0:T(8,128)S(1)} %get-tuple-element.60), channel_id=1, source_target_pairs={{0,16},{32,48},{64,80},{96,112},{128,144},{160,176},{192,208},{224... | collective-permute-start | bytes 688136 | tf_op jit(solution)/shard_map/ppermute | solution.py:576
  12.8 5.6 %collective-permute-start.3 = (f32[7,64,128]{2,1,0:T(8,128)S(1)}, f32[7,64,128]{2,1,0:T(8,128)S(1)}, u32[]{:S(2)}, u32[]{:S(2)}) collective-permute-start(f32[7,64,128]{2,1,0:T(8,128)S(1)} %get-tuple-element.61), channel_id=1, source_target_pairs={{16,32},{48,64},{80,96},{112,128},{144,160},{176,192},{208,224},{2... | collective-permute-start | bytes 688136 | tf_op jit(solution)/shard_map/ppermute | solution.py:576
  18.4 0.4 collective-permute-start.4
  18.8 0.6 %collective-permute-start.5 = (f32[2,64,128]{2,1,0:T(8,128)S(1)}, f32[2,64,128]{2,1,0:T(8,128)S(1)}, u32[]{:S(2)}, u32[]{:S(2)}) collective-permute-start(f32[2,64,128]{2,1,0:T(8,128)S(1)} %get-tuple-element.70), channel_id=1, source_target_pairs={{4,8},{12,0},{8,4},{0,12},{5,9},{13,1},{9,5},{1,13},{6,10},{14,2},... | collective-permute-start | bytes 196616 | tf_op jit(solution)/shard_map/ppermute | solution.py:576
  19.4 0.0 copy-done
  19.4 3.8 %inner0.1 = (f32[26,64,256]{2,1,0:T(8,128)S(1)}, bf16[26,64,256]{2,1,0:T(8,128)(2,1)S(1)}, bf16[26,64,256]{2,1,0:T(8,128)(2,1)S(1)}, f32[2,64,128]{2,1,0:T(8,128)S(1)}, f32[2,64,128]{2,1,0:T(8,128)S(1)}) custom-call(f32[26,64,256]{2,1,0:T(8,128)S(1)} %get-tuple-element.58.mid, bf16[26,64,256]{2,1,0:T(8,128)(2,1)S(1)} %get-tuple-element.49.mid_high, ...), custom_call_target="tpu_custom_call" | custom-call | flops 2835349504 | bytes 12582912 | tf_op jit(solution)/shard_map/inner0/pallas_call | solution.py:607
  23.2 0.0 collective-permute-done.4.rest_0_
  23.2 0.2 collective-permute-done.5.rest_1_
  23.4 0.0 collective-permute-done.2.x_first
  23.4 0.0 collective-permute-done.3.x_second
  23.4 1.3 %outer0.1 = (f32[6,64,256]{2,1,0:T(8,128)S(1)}, bf16[6,64,256]{2,1,0:T(8,128)(2,1)S(1)}, bf16[6,64,256]{2,1,0:T(8,128)(2,1)S(1)}, f32[1,2,64,128]{3,2,1,0:T(8,12...) custom-call(f32[6,64,256]{2,1,0:T(8,128)S(1)} %get-tuple-element.48.end, ...), custom_call_target="tpu_custom_call" | custom-call | flops 872415232 | bytes 6291456 | tf_op jit(solution)/shard_map/outer0/pallas_call | solution.py:621
  24.7 0.1 collective-permute-start.6
  24.8 3.0 %collective-permute-start.7 = (f32[7,64,128]{2,1,0:T(8,128)S(1)}, f32[7,64,128]{2,1,0:T(8,128)S(1)}, u32[]{:S(2)}, u32[]{:S(2)}) collective-permute-start(f32[7,64,128]{2,1,0:T(8,128)S(1)} %get-tuple-element.80), channel_id=1, source_target_pairs={{16,32},{48,64},{80,96},{112,128},{144,160},{176,192},{208,224},{2... | collective-permute-start | bytes 688136 | tf_op jit(solution)/shard_map/ppermute | solution.py:576
  27.8 4.5 %inner1.1 = (f32[26,64,256]{2,1,0:T(8,128)S(1)}, bf16[1,16,128]{2,1,0:T(8,128)(2,1)}, bf16[1,16,128]{2,1,0:T(8,128)(2,1)}, f32[2,32,256]{2,1,0:T(8,128)S(1)}, f32[1,8,128]{2,1,0:T(8,128)}) custom-call(f32[26,64,256]{2,1,0:T(8,128)S(1)} %get-tuple-element.81.mid, bf16[26,64,256]{2,1,0:T(8,128)(2,1)S(1)} %get-tuple-element.73.mid_high, ...), custom_call_target="tpu_custom_call" | custom-call | flops 2835349504 | bytes 12582912 | tf_op jit(solution)/shard_map/inner1/pallas_call | solution.py:607
  32.3 0.0 collective-permute-done.6.x_first
  32.3 0.0 collective-permute-done.7.x_second
  32.3 0.0 copy-start.2
  32.4 1.4 %outer1.1 = (f32[6,64,256]{2,1,0:T(8,128)S(1)}, f32[2,32,256]{2,1,0:T(8,128)S(1)}) custom-call(f32[6,64,256]{2,1,0:T(8,128)S(1)} %get-tuple-element.72.end, bf16[26,64,256]{2,1,0:T(8,128)(2,1)S(1)} %get-tuple-element.73.mid_high, bf16[6,64,256]{2,1,0:T(8,128)(2,1)S(1)} %get-tuple-element.74.end_high, bf16[26,64,256]{2,1,0:T(8,128)(2,1)S(1)} %get-tuple-element.75.mid_low, ...), custom_call_target="tpu_custom_call" | custom-call | flops 872415232 | bytes 6291456 | tf_op jit(solution)/shard_map/outer1/pallas_call | solution.py:617
  33.7 3.8 %collective-permute-start.8 = (f32[2,32,256]{2,1,0:T(8,128)S(1)}, f32[2,32,256]{2,1,0:T(8,128)S(1)}, u32[]{:S(2)}, u32[]{:S(2)}) collective-permute-start(f32[2,32,256]{2,1,0:T(8,128)S(1)} %get-tuple-element.83.own_sums), channel_id=1, source_target_pairs={{0,1},{1,0},{2,3},{3,2},{4,5},{5,4},{6,7},{7,6},{8,9},{9,8},{10,11... | collective-permute-start | bytes 196616 | tf_op jit(solution)/shard_map/ppermute | solution.py:627
  37.6 0.9 %collective-permute-done.8.partner_sums = f32[2,32,256]{2,1,0:T(8,128)S(1)} collective-permute-done((f32[2,32,256]{2,1,0:T(8,128)S(1)}, f32[2,32,256]{2,1,0:T(8,128)S(1)}, u32[]{:S(2)}, u32[]{:S(2)}) %collective-permute-start.8) | collective-permute-done | bytes 65568 | tf_op jit(solution)/shard_map/ppermute | solution.py:627
  38.5 0.0 copy-start.1
  38.5 2.5 %collective-permute-start.9 = (f32[32,256]{1,0:T(8,128)S(1)}, f32[32,256]{1,0:T(8,128)S(1)}, u32[]{:S(2)}, u32[]{:S(2)}) collective-permute-start(f32[32,256]{1,0:T(8,128)S(1)} %get-tuple-element.90), channel_id=1, source_target_pairs={{0,2},{2,0},{1,3},{3,1},{4,6},{6,4},{5,7},{7,5},{8,10},{10,8},{9,1... | collective-permute-start | bytes 98312 | tf_op jit(solution)/shard_map/ppermute | solution.py:632
  41.1 0.0 copy-done.2
  41.1 2.2 %sweep.1.swept = f32[64,32,256]{2,1,0:T(8,128)S(1)} custom-call(f32[26,64,256]{2,1,0:T(8,128)S(1)} %get-tuple-element.87.mid, f32[6,64,256]{2,1,0:T(8,128)S(1)} %get-tuple-element.88.end, f32[4,128]{1,0:T(4,128)S(1)} %copy-done.2), custom_call_target="tpu_custom_call" | custom-call | flops 20971520 | bytes 4194304 | tf_op jit(solution)/shard_map/sweep/pallas_call | solution.py:633
  43.3 0.0 collective-permute-done.9.far
  43.3 0.0 copy-done.1
  43.3 1.4 %finish.1 = f32[64,32,256]{2,1,0:T(8,128)} custom-call(f32[64,32,256]{2,1,0:T(8,128)S(1)} %sweep.1.swept, f32[2,32,256]{2,1,0:T(8,128)S(1)} %get-tuple-element.89.near, f32[32,256]{1,0:T(8,128)S(1)} %collective-permute-done.9.far, f32[4,128,128]{2,1,0:T(8,128)S(1)} %copy-done.1), custom_call_target="tpu_custom_call" | custom-call | bytes 6291456 | tf_op jit(solution)/shard_map/finish/pallas_call | solution.py:637
  (1 shorter events, 0.0 us)
Async XLA Ops:
  0.0 6.3 %copy-start.6 = (f32[4]{0:T(128)S(1)}, f32[4]{0:T(128)}, u32[]{:S(2)}) copy-start(f32[4]{0:T(128)} %rate_in.1) | copy-start | bytes 52
  0.0 6.3 %copy-start.5 = (f32[4]{0:T(128)S(1)}, f32[4]{0:T(128)}, u32[]{:S(2)}) copy-start(f32[4]{0:T(128)} %diffusivity_in.1) | copy-start | bytes 52
  0.0 6.3 %copy-start.4 = (f32[28]{0:T(128)S(1)}, f32[28]{0:T(128)}, u32[]{:S(2)}) copy-start(f32[28]{0:T(128)} %weight_in.1) | copy-start | bytes 340
  0.0 6.3 %copy-start.3 = (s32[28,2]{0,1:T(2,128)S(1)}, s32[28,2]{0,1:T(2,128)}, u32[]{:S(2)}) copy-start(s32[28,2]{0,1:T(2,128)} %param.14) | copy-start | bytes 676
  2.2 8.6 %collective-permute-start = (f32[2,64,128]{2,1,0:T(8,128)S(1)}, f32[2,64,128]{2,1,0:T(8,128)S(1)}, u32[]{:S(2)}, u32[]{:S(2)}) collective-permute-start(f32[2,64,128]{2,1,0:T(8,128)S(1)} %get-tuple-element.53.own_first), channel_id=1, source_target_pairs={{0,4},{8,12},{4,0},{12,8},{1,5},{9,13},{5,1},{13,9},{2,6},{10,14},... | collective-permute-start | bytes 196616 | tf_op jit(solution)/shard_map/ppermute | solution.py:576
  4.4 6.4 %collective-permute-start.1 = (f32[2,64,128]{2,1,0:T(8,128)S(1)}, f32[2,64,128]{2,1,0:T(8,128)S(1)}, u32[]{:S(2)}, u32[]{:S(2)}) collective-permute-start(f32[2,64,128]{2,1,0:T(8,128)S(1)} %get-tuple-element.54.own_second), channel_id=1, source_target_pairs={{4,8},{12,0},{8,4},{0,12},{5,9},{13,1},{9,5},{1,13},{6,10},{14,2},... | collective-permute-start | bytes 196616 | tf_op jit(solution)/shard_map/ppermute | solution.py:576
  6.3 13.1 %copy-start = (f32[4,128,128]{2,1,0:T(8,128)S(1)}, f32[4,128,128]{2,1,0:T(8,128)}, u32[]{:S(2)}) copy-start(f32[4,128,128]{2,1,0:T(8,128)} %constant.6.clone.sums) | copy-start | bytes 786436
  11.1 12.3 %collective-permute-start.2 = (f32[7,64,128]{2,1,0:T(8,128)S(1)}, f32[7,64,128]{2,1,0:T(8,128)S(1)}, u32[]{:S(2)}, u32[]{:S(2)}) collective-permute-start(f32[7,64,128]{2,1,0:T(8,128)S(1)} %get-tuple-element.60), channel_id=1, source_target_pairs={{0,16},{32,48},{64,80},{96,112},{128,144},{160,176},{192,208},{224... | collective-permute-start | bytes 688136 | tf_op jit(solution)/shard_map/ppermute | solution.py:576
  12.8 10.6 %collective-permute-start.3 = (f32[7,64,128]{2,1,0:T(8,128)S(1)}, f32[7,64,128]{2,1,0:T(8,128)S(1)}, u32[]{:S(2)}, u32[]{:S(2)}) collective-permute-start(f32[7,64,128]{2,1,0:T(8,128)S(1)} %get-tuple-element.61), channel_id=1, source_target_pairs={{16,32},{48,64},{80,96},{112,128},{144,160},{176,192},{208,224},{2... | collective-permute-start | bytes 688136 | tf_op jit(solution)/shard_map/ppermute | solution.py:576
  18.4 4.9 %collective-permute-start.4 = (f32[2,64,128]{2,1,0:T(8,128)S(1)}, f32[2,64,128]{2,1,0:T(8,128)S(1)}, u32[]{:S(2)}, u32[]{:S(2)}) collective-permute-start(f32[2,64,128]{2,1,0:T(8,128)S(1)} %get-tuple-element.69), channel_id=1, source_target_pairs={{0,4},{8,12},{4,0},{12,8},{1,5},{9,13},{5,1},{13,9},{2,6},{10,14},... | collective-permute-start | bytes 196616 | tf_op jit(solution)/shard_map/ppermute | solution.py:576
  18.8 4.6 %collective-permute-start.5 = (f32[2,64,128]{2,1,0:T(8,128)S(1)}, f32[2,64,128]{2,1,0:T(8,128)S(1)}, u32[]{:S(2)}, u32[]{:S(2)}) collective-permute-start(f32[2,64,128]{2,1,0:T(8,128)S(1)} %get-tuple-element.70), channel_id=1, source_target_pairs={{4,8},{12,0},{8,4},{0,12},{5,9},{13,1},{9,5},{1,13},{6,10},{14,2},... | collective-permute-start | bytes 196616 | tf_op jit(solution)/shard_map/ppermute | solution.py:576
  24.7 7.6 %collective-permute-start.6 = (f32[7,64,128]{2,1,0:T(8,128)S(1)}, f32[7,64,128]{2,1,0:T(8,128)S(1)}, u32[]{:S(2)}, u32[]{:S(2)}) collective-permute-start(f32[7,64,128]{2,1,0:T(8,128)S(1)} %get-tuple-element.79), channel_id=1, source_target_pairs={{0,16},{32,48},{64,80},{96,112},{128,144},{160,176},{192,208},{224... | collective-permute-start | bytes 688136 | tf_op jit(solution)/shard_map/ppermute | solution.py:576
  24.8 7.5 %collective-permute-start.7 = (f32[7,64,128]{2,1,0:T(8,128)S(1)}, f32[7,64,128]{2,1,0:T(8,128)S(1)}, u32[]{:S(2)}, u32[]{:S(2)}) collective-permute-start(f32[7,64,128]{2,1,0:T(8,128)S(1)} %get-tuple-element.80), channel_id=1, source_target_pairs={{16,32},{48,64},{80,96},{112,128},{144,160},{176,192},{208,224},{2... | collective-permute-start | bytes 688136 | tf_op jit(solution)/shard_map/ppermute | solution.py:576
  32.3 8.7 %copy-start.2 = (f32[4,128]{1,0:T(4,128)S(1)}, f32[4,128]{1,0:T(4,128)}, u32[]{:S(2)}) copy-start(f32[4,128]{1,0:T(4,128)} %constant.8.clone.solve) | copy-start | bytes 6148
  33.7 4.8 %collective-permute-start.8 = (f32[2,32,256]{2,1,0:T(8,128)S(1)}, f32[2,32,256]{2,1,0:T(8,128)S(1)}, u32[]{:S(2)}, u32[]{:S(2)}) collective-permute-start(f32[2,32,256]{2,1,0:T(8,128)S(1)} %get-tuple-element.83.own_sums), channel_id=1, source_target_pairs={{0,1},{1,0},{2,3},{3,2},{4,5},{5,4},{6,7},{7,6},{8,9},{9,8},{10,11... | collective-permute-start | bytes 196616 | tf_op jit(solution)/shard_map/ppermute | solution.py:627
  38.5 4.8 %copy-start.1 = (f32[4,128,128]{2,1,0:T(8,128)S(1)}, f32[4,128,128]{2,1,0:T(8,128)}, u32[]{:S(2)}) copy-start(f32[4,128,128]{2,1,0:T(8,128)} %constant.7.clone.reply) | copy-start | bytes 786436
  38.5 4.7 %collective-permute-start.9 = (f32[32,256]{1,0:T(8,128)S(1)}, f32[32,256]{1,0:T(8,128)S(1)}, u32[]{:S(2)}, u32[]{:S(2)}) collective-permute-start(f32[32,256]{1,0:T(8,128)S(1)} %get-tuple-element.90), channel_id=1, source_target_pairs={{0,2},{2,0},{1,3},{3,1},{4,6},{6,4},{5,7},{7,5},{8,10},{10,8},{9,1... | collective-permute-start | bytes 98312 | tf_op jit(solution)/shard_map/ppermute | solution.py:632

commit v6 on v5

--- a/solution.py
+++ b/solution.py
@@ -42,7 +42,8 @@
 
 PARTS = tuple(struct(n, DZ, DY, dtype=t) for t in (f32, bf16, bf16) for n in (INNER, 6))
 PACK = struct(2, DZ, 128)
-SLABS = struct(7, DZ, 128)
+SLABS = struct(6 * DZ, 128)
+TAIL = DZ // 4
 WHOLE = struct(DX, DZ, DY)
 
 
@@ -61,8 +62,30 @@
 
 
 def by_parity(axis, first, second):
-    even = lanes() < jnp.where(lax.axis_index(axis) % 2 == 0, 128, 0)
-    return jnp.where(even, first, second), jnp.where(even, second, first)
+    lane = lax.broadcasted_iota(jnp.int32, first.shape, 1)
+    odd = lane < jnp.where(lax.axis_index(axis) % 2 == 1, 128, 0)
+    return jnp.where(odd, first, second), jnp.where(odd, second, first)
+
+
+def fold(strip, start):
+    lane = lax.broadcasted_iota(jnp.int32, (TAIL, 128), 1)
+    folded = jnp.zeros((TAIL, 128), f32)
+    for part in range(4):
+        moved = pltpu.roll(strip[TAIL * part : TAIL * part + TAIL], (32 * part - start) % 128, 1)
+        folded = jnp.where(lane // 32 == part, moved, folded)
+    return folded
+
+
+def unfold(folded, start):
+    return jnp.concatenate([pltpu.roll(folded, (start - 32 * part) % 128, 1) for part in range(4)], axis=0)
+
+
+def slab(index):
+    return pl.ds(DZ * index, DZ)
+
+
+def tail(index):
+    return pl.ds(6 * DZ + TAIL * index, TAIL)
 
 
 def split(value):
@@ -93,8 +116,8 @@
 
 
 def prepare_kernel(
-    offsets_in, weight_in, diffusivity_in, rate_in, pit, phase, damage, mid, end,
-    w_ref, move, gain, table_rows, to_high, to_low, middle,
+    offsets_in, weight_in, diffusivity_in, rate_in, pit, phase, damage,
+    w_ref, move, gain, table_rows, to_high, to_low,
     pv, hv, dv, offsets, weight, diffusivity, rate, table, sem, scalar_sem,
 ):
     def copies(group):
@@ -153,11 +176,6 @@
     high, low = split(edge)
     for row, value in enumerate((high, high, low, jnp.zeros((64, DY), bf16))):
         w_ref[8, 64 * row : 64 * row + 64, :] = value
-    packed = [jnp.zeros((DZ, 128), f32)] * 2
-    for x in range(DX):
-        packed[x // 16] = add_middle(packed[x // 16], end[OUTER.index(x)] if x in OUTER else mid[x - 3], x)
-    middle[0], middle[1] = packed
-
     def look(ids, values, scale):
         value = jnp.where(ids == 0, values[0] * scale, values[1] * scale)
         return jnp.where(ids < 2, value, jnp.where(ids == 2, values[2] * scale, values[3] * scale))
@@ -209,37 +227,33 @@
     return center + move * (flux - weight_sum * center) + gain * (1.0 - center)
 
 
-def first_kernel(conc, mid, end, mid_high, end_high, mid_low, end_low, lasts, firsts, up, down, buf, sem):
+def first_kernel(conc, mid, end, lasts, firsts, up, down, sem):
+    def row_ref(x):
+        return end.at[OUTER.index(x)] if x in OUTER else mid.at[x - 3]
+
     for x in range(DX):
-        pltpu.make_async_copy(conc.at[:, x, :], buf.at[x], sem.at[x // 8]).start()
+        pltpu.make_async_copy(conc.at[:, x, :], row_ref(x), sem.at[x // 8]).start()
     for group in range(4):
         for x in range(8 * group, 8 * group + 8):
-            pltpu.make_async_copy(conc.at[:, x, :], buf.at[x], sem.at[group]).wait()
+            pltpu.make_async_copy(conc.at[:, x, :], row_ref(x), sem.at[group]).wait()
         if group % 2 == 0:
             high_side, low_side = jnp.zeros((DZ, 128), f32), jnp.zeros((DZ, 128), f32)
         for x in range(8 * group, 8 * group + 8):
-            row = buf[x]
-            high, low = split(row)
-            if x in OUTER:
-                place = OUTER.index(x)
-                end[place], end_high[place], end_low[place] = row, high, low
-            else:
-                mid[x - 3], mid_high[x - 3], mid_low[x - 3] = row, high, low
             slot = 8 * (x % 16)
+            row = row_ref(x)
             high_side = at_lanes(high_side, row[:, 128:], 122, slot, 6)
             low_side = at_lanes(low_side, row[:, :128], 0, slot, 6)
         if group % 2:
             lasts[group // 2], firsts[group // 2] = by_parity("gy", high_side, low_side)
-    fill_slabs(lambda row: buf[OUTER[row]], up, down)
-    down[6] = jnp.zeros((DZ, 128), f32)
-    up[6] = jnp.zeros((DZ, 128), f32)
+    fill_slabs(lambda row: end[row], up, down)
 
 
 def fill_slabs(row_of, up, down):
     for row in range(3):
         for half in range(2):
             part = slice(128 * half, 128 * half + 128)
-            up[2 * row + half], down[2 * row + half] = by_parity("gx", row_of(3 + row)[:, part], row_of(row)[:, part])
+            place = slab(2 * row + half)
+            up[place], down[place] = by_parity("gx", row_of(3 + row)[:, part], row_of(row)[:, part])
 
 
 def join_kernel(y_first, y_second, own_first, own_second, up_in, down_in, strips, up, down):
@@ -249,19 +263,11 @@
         strips[0, group] = two_sides(left, pltpu.roll(lasts, 1, 1))
         strips[1, group] = two_sides(pltpu.roll(left, 125, 1), pltpu.roll(right, 4, 1))
         strips[2, group] = two_sides(firsts, pltpu.roll(right, 1, 1))
-    for slab in range(6):
-        up[slab] = up_in[slab]
-        down[slab] = down_in[slab]
-    lane = lanes()
-    to_next = jnp.where(
-        lane >= 104, strips[1, 1],
-        jnp.where(lane >= 72, pltpu.roll(strips[0, 1], 96, 1), pltpu.roll(strips[2, 1], 64, 1)),
-    )
-    to_last = jnp.where(
-        lane < 32, strips[1, 0],
-        jnp.where(lane < 64, pltpu.roll(strips[0, 0], 32, 1), pltpu.roll(strips[2, 0], 64, 1)),
-    )
-    up[6], down[6] = by_parity("gx", to_next, to_last)
+    for index in range(6):
+        up[slab(index)] = up_in[slab(index)]
+        down[slab(index)] = down_in[slab(index)]
+    for index in range(3):
+        up[tail(index)], down[tail(index)] = by_parity("gx", fold(strips[index, 1], 96), fold(strips[index, 0], 0))
 
 
 def strip_taps(table, first, second, third):
@@ -307,10 +313,25 @@
     return total
 
 
-def inner_kernel(
-    last, mid, mid_high, end_high, mid_low, end_low, strips, middle, move, gain, w_ref, sums, table,
-    out, out_high, out_low, extra, new_middle,
-):
+def inner_kernel(last, mid, *rest):
+    if last:
+        mid_high, end_high, mid_low, end_low, strips, middle, move, gain, w_ref, sums, table, out, extra = rest
+    else:
+        (
+            end, strips, move, gain, w_ref, table,
+            out, out_high, out_low, extra, new_middle, mid_high, end_high, mid_low, end_low, middle,
+        ) = rest
+        packed = [jnp.zeros((DZ, 128), f32)] * 2
+        for x in range(DX):
+            if x in OUTER:
+                place = OUTER.index(x)
+                row = end[place]
+                end_high[place], end_low[place] = split(row)
+            else:
+                row = mid[x - 3]
+                mid_high[x - 3], mid_low[x - 3] = split(row)
+            packed[x // 16] = add_middle(packed[x // 16], row, x)
+        middle[0], middle[1] = packed
     halo = strips.at[0 if last else 1]
     weight_sum = table[49:50, :]
     pairs = range(3, DX - 3, 2)
@@ -381,14 +402,20 @@
     def halo_rows(slabs):
         return [jnp.concatenate([slabs[2 * row], slabs[2 * row + 1]], axis=1) for row in range(3)]
 
-    from_high, from_low = zip(*(by_parity("gx", x_first[slab], x_second[slab]) for slab in range(7)))
+    def received(place):
+        return by_parity("gx", x_first[place], x_second[place])
+
+    from_high, from_low = zip(*(received(slab(index)) for index in range(6)))
+    tails = [received(tail(index)) for index in range(1 if last else 3)]
+    high_strips, low_strips = [unfold(high, 0) for high, _ in tails], [unfold(low, 96) for _, low in tails]
     low_rows, high_rows = halo_rows(from_low), halo_rows(from_high)
     low_split, high_split = [split(row) for row in low_rows], [split(row) for row in high_rows]
     low_middle, high_middle = zero, zero
     for row in range(3):
         low_middle = add_middle(low_middle, low_rows[row], 13 + row)
         high_middle = add_middle(high_middle, high_rows[row], row)
-    sides = [from_low[6], halo[0], halo[1], from_high[6]]
+    here = 0 if last else 1
+    sides = [low_strips[here], halo[0], halo[1], high_strips[here]]
     middles = [low_middle, middle[0], middle[1], high_middle]
 
     def row_of(which, mid_part, end_part):
@@ -433,12 +460,7 @@
         new_middle[0], new_middle[1] = packed
         fill_slabs(lambda row: out[row], up, down)
         lane = lanes()
-        low, high = from_low[6], from_high[6]
-        beyond = [
-            jnp.where(lane < 64, pltpu.roll(high, 96, 1), pltpu.roll(low, 32, 1)),
-            jnp.where(lane < 64, high, low),
-            jnp.where(lane < 64, pltpu.roll(high, 64, 1), pltpu.roll(low, 64, 1)),
-        ]
+        beyond = [jnp.where(lane < 64, high, low) for high, low in zip(high_strips, low_strips)]
         taps = [None, None, strip_taps(table, *beyond)]
         for group in range(2):
             flux = extra_in[group] + strip_flux(taps, group)
@@ -447,7 +469,7 @@
                 halo[group], flux, two_sides(left, right),
                 two_sides(pltpu.roll(left, 124, 1), pltpu.roll(right, 4, 1)), weight_sum,
             )
-        up[6], down[6] = by_parity("gx", extra[0, 1], extra[0, 0])
+        up[tail(0)], down[tail(0)] = by_parity("gx", fold(extra[0, 1], 96), fold(extra[0, 0], 0))
 
 
 def depth_tables():
@@ -571,7 +593,7 @@
 def swaps(first, second, axis):
     count = lax.axis_size(axis)
     moved = []
-    for start, value in ((0, first), (1, second)):
+    for start, value in ((1, first), (0, second)):
         pairs = [(i, (i + 1) % count) for i in range(start, count, 2)]
         moved.append(lax.ppermute(value, axis, pairs + [(target, source) for source, target in pairs]))
     return moved
@@ -579,61 +601,63 @@
 
 def local(conc, pit, phase, offsets, damage, weight, diffusivity, rate):
     sums, solve, reply, mix = depth_tables()
-    *parts, lasts, firsts, up, down = call(
-        first_kernel, "first", PARTS + (PACK, PACK, SLABS, SLABS), [HBM], (VMEM,) * 10,
-        [pltpu.VMEM((DX, DZ, DY), f32), SEM((4,))], nbytes=4 << 20, limit=48,
+    mid, end, lasts, firsts, up, down = call(
+        first_kernel, "first", PARTS[:2] + (PACK, PACK, SLABS, SLABS), [HBM], (VMEM,) * 6, [SEM((4,))],
+        nbytes=4 << 20, limit=51,
     )(conc)
     left, right = swaps(lasts, firsts, "gy")
-    w, move, gain, table, to_high, to_low, middle = call(
-        prepare_kernel, "prepare", (struct(9, DY, DY, dtype=bf16), WHOLE, WHOLE, struct(56, 128), PACK, PACK, PACK),
-        [ANY] * 4 + [HBM] * 3 + [VMEM] * 2, (VMEM,) * 7,
+    w, move, gain, table, to_high, to_low = call(
+        prepare_kernel, "prepare", (struct(9, DY, DY, dtype=bf16), WHOLE, WHOLE, struct(56, 128), PACK, PACK),
+        [ANY] * 4 + [HBM] * 3, (VMEM,) * 6,
         [pltpu.VMEM((DX, DZ, DY), jnp.int32)] * 3
         + [pltpu.SMEM((2, BONDS), jnp.int32), pltpu.SMEM((BONDS,), f32), pltpu.SMEM((4,), f32), pltpu.SMEM((4,), f32)]
         + [pltpu.SMEM((64,), f32), SEM((4,)), SEM((4,))],
-        nbytes=8 << 20, limit=45,
-    )(offsets.T, weight, diffusivity, rate, pit, phase, damage, parts[0], parts[1])
+        nbytes=8 << 20, limit=47,
+    )(offsets.T, weight, diffusivity, rate, pit, phase, damage)
     strips, up, down = call(
-        join_kernel, "join", (struct(3, 2, DZ, 128), SLABS, SLABS), [VMEM] * 6, (VMEM,) * 3,
+        join_kernel, "join", (struct(3, 2, DZ, 128), struct(6 * DZ + 3 * TAIL, 128), struct(6 * DZ + 3 * TAIL, 128)), [VMEM] * 6, (VMEM,) * 3,
     )(left, right, lasts, firsts, up, down)
-    for substep in range(2):
-        last = substep == 1
-        x_first, x_second = swaps(up, down, "gx")
-        if not last:
-            to_high, to_low, up, down = lax.optimization_barrier((to_high, to_low, up, down))
-            coefs = swaps(to_high, to_low, "gy")
-        mid, end, mid_high, end_high, mid_low, end_low = parts
-        tiny = struct(1, 16, 128, dtype=bf16)
-        inner_split = (tiny, tiny) if last else (PARTS[2], PARTS[4])
-        new_mid, new_mid_high, new_mid_low, more, more_middle = call(
-            functools.partial(inner_kernel, last), f"inner{substep}",
-            (PARTS[0],) + inner_split + ((struct(2, DX, DY) if last else PACK), struct(1, 8, 128) if last else PACK),
-            [VMEM] * 12, (VMEM,) * 5, flops=2 * INNER * DZ * DY * 3328, nbytes=12 << 20,
-        )(mid, mid_high, end_high, mid_low, end_low, strips, middle, move, gain, w, sums, table)
-        args = (end, mid_high, end_high, mid_low, end_low, strips, middle, x_first, x_second, move, gain, w)
-        args = args + (sums, table, more)
-        specs = [VMEM] * 15
-        cost = dict(flops=2 * 8 * DZ * DY * 3328, nbytes=6 << 20)
-        if last:
-            new_end, ends = call(
-                functools.partial(outer_kernel, last), "outer1", (PARTS[1], struct(2, DX, DY)), specs, (VMEM,) * 2, **cost
-            )(*args)
-        else:
-            new_end, new_end_high, new_end_low, strips, up, down, middle = call(
-                functools.partial(outer_kernel, last), "outer0",
-                (PARTS[1], PARTS[3], PARTS[5], struct(1, 2, DZ, 128), SLABS, SLABS, PACK),
-                specs + [VMEM] * 3, (VMEM,) * 7, **cost,
-            )(*args, *coefs, more_middle)
-            parts = [new_mid, new_end, new_mid_high, new_end_high, new_mid_low, new_end_low]
+    inner_cost = dict(flops=2 * INNER * DZ * DY * 3328, nbytes=12 << 20)
+    outer_cost = dict(flops=2 * 8 * DZ * DY * 3328, nbytes=6 << 20)
+
+    x_first, x_second = swaps(up, down, "gx")
+    to_high, to_low, up, down = lax.optimization_barrier((to_high, to_low, up, down))
+    coefs = swaps(to_high, to_low, "gy")
+    new_mid, new_mid_high, new_mid_low, flux, new_middle, mid_high, end_high, mid_low, end_low, middle = call(
+        functools.partial(inner_kernel, False), "inner0",
+        (PARTS[0], PARTS[2], PARTS[4], PACK, PACK, PARTS[2], PARTS[3], PARTS[4], PARTS[5], PACK),
+        [VMEM] * 7, (VMEM,) * 10, **inner_cost,
+    )(mid, end, strips, move, gain, w, table)
+    new_end, new_end_high, new_end_low, strips, up, down, new_middle = call(
+        functools.partial(outer_kernel, False), "outer0",
+        (PARTS[1], PARTS[3], PARTS[5], struct(1, 2, DZ, 128), struct(6 * DZ + TAIL, 128), struct(6 * DZ + TAIL, 128), PACK),
+        [VMEM] * 18, (VMEM,) * 7, **outer_cost,
+    )(
+        end, mid_high, end_high, mid_low, end_low, strips, middle, x_first, x_second, move, gain, w, sums, table, flux,
+        *coefs, new_middle,
+    )
+
+    x_first, x_second = swaps(up, down, "gx")
+    fields = (new_mid_high, new_end_high, new_mid_low, new_end_low, strips, new_middle)
+    mid, inner_sums = call(
+        functools.partial(inner_kernel, True), "inner1", (PARTS[0], struct(2, DX, DY)), [VMEM] * 12, (VMEM,) * 2,
+        **inner_cost,
+    )(new_mid, *fields, move, gain, w, sums, table)
+    end, ends = call(
+        functools.partial(outer_kernel, True), "outer1", (PARTS[1], struct(2, DX, DY)), [VMEM] * 15, (VMEM,) * 2,
+        **outer_cost,
+    )(new_end, *fields, x_first, x_second, move, gain, w, sums, table, inner_sums)
+
     partner = lax.ppermute(ends, "gz", [(0, 1), (1, 0), (2, 3), (3, 2)])
     send, near = call(
         functools.partial(mix_kernel, mix), "mix", (struct(DX, DY), struct(2, DX, DY)), [VMEM, VMEM], (VMEM,) * 2,
     )(ends, partner)
-    send, new_mid, new_end = lax.optimization_barrier((send, new_mid, new_end))
+    send, mid, end = lax.optimization_barrier((send, mid, end))
     far = lax.ppermute(send, "gz", [(0, 2), (2, 0), (1, 3), (3, 1)])
     swept = call(
         sweep_kernel, "sweep", struct(DZ, DX, DY), [VMEM, VMEM, SMEM], VMEM, [pltpu.VMEM((DZ, DX, DY), f32)],
         flops=20 << 20, nbytes=4 << 20,
-    )(new_mid, new_end, solve)
+    )(mid, end, solve)
     return call(
         functools.partial(finish_kernel, mix), "finish", struct(DZ, DX, DY), [VMEM] * 4, HBM,
         [pltpu.VMEM((DZ, DX, DY), f32), SEM((8,))], nbytes=6 << 20,

time: 45 us -> 43.6 us (0.969)
  starting transfers between devices: 21.9 us -> 20.2 us
    ppermute x8, starting transfers between devices: 15.5 us -> 14.2 us  [swaps(): lax.ppermute(value, axis, pairs + [(target, source) for source, target in...]
  transfers between devices with their start and end apart: 10 -> 10, of which waited for: 2 -> 3; matrix products, arithmetic and copies ran while one was open for 0% -> 0% of each run, Pallas kernels for 33% -> 35%
where the time goes in v6:
time: 43.6 us; the launch traced here: 43.4 us
  Pallas kernels  21.6 us (50%)
  starting transfers between devices  20.2 us (46%)
  waiting for transfers between devices  1.28 us (3%)
    ppermute x8, starting transfers between devices, swaps(): lax.ppermute(value, axis, pairs + [(target, source) for source, target in...  14.2 us
    pallas_call x1, Pallas kernels, local(): call(functools.partial(inner_kernel, True), 'inner1', (PARTS[0], struct(2...  4.48 us
    pallas_call x1, Pallas kernels, local(): call(prepare_kernel, 'prepare', (struct(9, DY, DY, dtype=bf16), WHOLE, WH...  4.44 us
    pallas_call x1, Pallas kernels, local(): call(functools.partial(inner_kernel, False), 'inner0', (PARTS[0], PARTS[2...  3.88 us
    ppermute x1, starting transfers between devices, local(): partner = lax.ppermute(ends, 'gz', [(0, 1), (1, 0), (2, 3), (3, 2)])  3.45 us
    ppermute x1, starting transfers between devices, local(): far = lax.ppermute(send, 'gz', [(0, 2), (2, 0), (1, 3), (3, 1)])  2.53 us
    pallas_call x1, Pallas kernels, local(): call(sweep_kernel, 'sweep', struct(DZ, DX, DY), [VMEM, VMEM, SMEM], VMEM,...  2.2 us
    pallas_call x1, Pallas kernels, local(): call(first_kernel, 'first', PARTS[:2] + (PACK, PACK, SLABS, SLABS), [HBM]...  2.15 us
  transfers between devices with their start and end apart: 10, of which 3 were waited for; matrix products, arithmetic and copies ran while one was open for 0% of the time, Pallas kernels for 35%

profile of v6, /device:TPU:1, one launch (start us, length us, event | category | flops | bytes accessed | tf_op | source)
XLA Modules:
  0.0 43.4 jit_solution(13170583308236488306)
XLA Ops:
  0.0 0.0 copy-start.6
  0.0 0.0 copy-start.5
  0.0 0.0 copy-start.4
  0.0 0.0 copy-start.3
  0.0 2.2 %first.1 = (f32[26,64,256]{2,1,0:T(8,128)S(1)}, f32[6,64,256]{2,1,0:T(8,128)S(1)}, f32[2,64,128]{2,1,0:T(8,128)S(1)}, f32[2,64,128]{2,1,0:T(8,128)S(1)}, f32[384,128]{1,0:T(8,128)S(1)}, /*index=5*/f32[384,128]{1,0:T(8,128)S(1)}) custom-call(f32[64,32,256]{2,1,0:T(8,128)} %conc.1), custom_call_target="tpu_custom_call" | custom-call | bytes 4194304 | tf_op jit(solution)/shard_map/first/pallas_call | solution.py:604
  2.2 3.6 %collective-permute-start = (f32[2,64,128]{2,1,0:T(8,128)S(1)}, f32[2,64,128]{2,1,0:T(8,128)S(1)}, u32[]{:S(2)}, u32[]{:S(2)}) collective-permute-start(f32[2,64,128]{2,1,0:T(8,128)S(1)} %get-tuple-element.50.own_first), channel_id=1, source_target_pairs={{4,8},{12,0},{8,4},{0,12},{5,9},{13,1},{9,5},{1,13},{6,10},{14,2},... | collective-permute-start | bytes 196616 | tf_op jit(solution)/shard_map/ppermute | solution.py:598
  5.8 0.0 collective-permute-start.1
  5.8 0.0 copy-done.6
  5.8 0.0 copy-done.5
  5.8 0.0 copy-done.4
  5.8 0.0 copy-done.3
  5.8 4.4 %prepare.1 = (bf16[9,256,256]{2,1,0:T(8,128)(2,1)S(1)}, f32[32,64,256]{2,1,0:T(8,128)S(1)}, f32[32,64,256]{2,1,0:T(8,128)S(1)}, f32[56,128]{1,0:T(8,128)S(1)}, f...) custom-call(s32[2,28]{1,0:T(2,128)S(1)} %bitcast.1, f32[28]{0:T(128)S(1)} %copy-done.4, f32[4]{0:T(128)S(1)} %copy-done.5, ...), custom_call_target="tpu_custom_call" | custom-call | bytes 8388608 | tf_op jit(solution)/shard_map/prepare/pallas_call | solution.py:609
  10.3 0.0 collective-permute-done.y_first
  10.3 0.0 collective-permute-done.1.y_second
  10.3 0.2 join.1
  10.5 6.6 %collective-permute-start.2 = (f32[432,128]{1,0:T(8,128)S(1)}, f32[432,128]{1,0:T(8,128)S(1)}, u32[]{:S(2)}, u32[]{:S(2)}) collective-permute-start(f32[432,128]{1,0:T(8,128)S(1)} %get-tuple-element.64), channel_id=1, source_target_pairs={{16,32},{48,64},{80,96},{112,128},{144,160},{176,192},{208,224},{2... | collective-permute-start | bytes 663560 | tf_op jit(solution)/shard_map/ppermute | solution.py:598
  17.1 0.0 collective-permute-start.3
  17.1 0.6 %collective-permute-start.4 = (f32[2,64,128]{2,1,0:T(8,128)S(1)}, f32[2,64,128]{2,1,0:T(8,128)S(1)}, u32[]{:S(2)}, u32[]{:S(2)}) collective-permute-start(f32[2,64,128]{2,1,0:T(8,128)S(1)} %get-tuple-element.69), channel_id=1, source_target_pairs={{4,8},{12,0},{8,4},{0,12},{5,9},{13,1},{9,5},{1,13},{6,10},{14,2},... | collective-permute-start | bytes 196616 | tf_op jit(solution)/shard_map/ppermute | solution.py:598
  17.8 0.8 %collective-permute-start.5 = (f32[2,64,128]{2,1,0:T(8,128)S(1)}, f32[2,64,128]{2,1,0:T(8,128)S(1)}, u32[]{:S(2)}, u32[]{:S(2)}) collective-permute-start(f32[2,64,128]{2,1,0:T(8,128)S(1)} %get-tuple-element.70), channel_id=1, source_target_pairs={{0,4},{8,12},{4,0},{12,8},{1,5},{9,13},{5,1},{13,9},{2,6},{10,14},... | collective-permute-start | bytes 196616 | tf_op jit(solution)/shard_map/ppermute | solution.py:598
  18.6 0.0 copy-start
  18.6 3.9 %inner0.1 = (f32[26,64,256]{2,1,0:T(8,128)S(1)}, bf16[26,64,256]{2,1,0:T(8,128)(2,1)S(1)}, bf16[26,64,256]{2,1,0:T(8,128)(2,1)S(1)}, f32[2,64,128]{2,1,0:T(8,128...) custom-call(f32[26,64,256]{2,1,0:T(8,128)S(1)} %get-tuple-element.49, ...), custom_call_target="tpu_custom_call" | custom-call | flops 2835349504 | bytes 12582912 | tf_op jit(solution)/shard_map/inner0/pallas_call | solution.py:626
  22.5 0.0 collective-permute-done.4.rest_0_
  22.5 0.0 collective-permute-done.5.rest_1_
  22.5 0.0 collective-permute-done.2.x_first
  22.5 0.3 collective-permute-done.3.x_second
  22.8 0.0 copy-done
  22.8 1.4 %outer0.1 = (f32[6,64,256]{2,1,0:T(8,128)S(1)}, bf16[6,64,256]{2,1,0:T(8,128)(2,1)S(1)}, bf16[6,64,256]{2,1,0:T(8,128)(2,1)S(1)}, f32[1,2,64,128]{3,2,1,0:T(8,12...) custom-call(f32[6,64,256]{2,1,0:T(8,128)S(1)} %get-tuple-element.48.rest_0_.end, ...), custom_call_target="tpu_custom_call" | custom-call | flops 872415232 | bytes 6291456 | tf_op jit(solution)/shard_map/outer0/pallas_call | solution.py:631
  24.2 2.5 %collective-permute-start.6 = (f32[400,128]{1,0:T(8,128)S(1)}, f32[400,128]{1,0:T(8,128)S(1)}, u32[]{:S(2)}, u32[]{:S(2)}) collective-permute-start(f32[400,128]{1,0:T(8,128)S(1)} %get-tuple-element.79), channel_id=1, source_target_pairs={{16,32},{48,64},{80,96},{112,128},{144,160},{176,192},{208,224},{2... | collective-permute-start | bytes 614408 | tf_op jit(solution)/shard_map/ppermute | solution.py:598
  26.7 0.0 collective-permute-start.7
  26.7 4.5 %inner1.1 = (f32[26,64,256]{2,1,0:T(8,128)S(1)}, f32[2,32,256]{2,1,0:T(8,128)S(1)}) custom-call(f32[26,64,256]{2,1,0:T(8,128)S(1)} %get-tuple-element.81.mid, bf16[26,64,256]{2,1,0:T(8,128)(2,1)S(1)} %get-tuple-element.73.rest_0_.mid_high, bf16[6,64,256]{2,1,0:T(8,128)(2,1)S(1)} %get-tuple-element.74.rest_1_.end_high, ...), custom_call_target="tpu_custom_call" | custom-call | flops 2835349504 | bytes 12582912 | tf_op jit(solution)/shard_map/inner1/pallas_call | solution.py:642
  31.2 0.0 collective-permute-done.6.x_first
  31.2 0.1 collective-permute-done.7.x_second
  31.3 0.0 copy-start.2
  31.3 1.4 %outer1.1 = (f32[6,64,256]{2,1,0:T(8,128)S(1)}, f32[2,32,256]{2,1,0:T(8,128)S(1)}) custom-call(f32[6,64,256]{2,1,0:T(8,128)S(1)} %get-tuple-element.72.end, bf16[26,64,256]{2,1,0:T(8,128)(2,1)S(1)} %get-tuple-element.73.rest_0_.mid_high, bf16[6,64,256]{2,1,0:T(8,128)(2,1)S(1)} %get-tuple-element.74.rest_1_.end_high, ...), custom_call_target="tpu_custom_call" | custom-call | flops 872415232 | bytes 6291456 | tf_op jit(solution)/shard_map/outer1/pallas_call | solution.py:646
  32.7 3.4 %collective-permute-start.8 = (f32[2,32,256]{2,1,0:T(8,128)S(1)}, f32[2,32,256]{2,1,0:T(8,128)S(1)}, u32[]{:S(2)}, u32[]{:S(2)}) collective-permute-start(f32[2,32,256]{2,1,0:T(8,128)S(1)} %get-tuple-element.83.own_sums), channel_id=1, source_target_pairs={{0,1},{1,0},{2,3},{3,2},{4,5},{5,4},{6,7},{7,6},{8,9},{9,8},{10,11... | collective-permute-start | bytes 196616 | tf_op jit(solution)/shard_map/ppermute | solution.py:651
  36.1 0.9 %collective-permute-done.8.partner_sums = f32[2,32,256]{2,1,0:T(8,128)S(1)} collective-permute-done((f32[2,32,256]{2,1,0:T(8,128)S(1)}, f32[2,32,256]{2,1,0:T(8,128)S(1)}, u32[]{:S(2)}, u32[]{:S(2)}) %collective-permute-start.8) | collective-permute-done | bytes 65568 | tf_op jit(solution)/shard_map/ppermute | solution.py:651
  37.0 0.0 copy-start.1
  37.1 2.5 %collective-permute-start.9 = (f32[32,256]{1,0:T(8,128)S(1)}, f32[32,256]{1,0:T(8,128)S(1)}, u32[]{:S(2)}, u32[]{:S(2)}) collective-permute-start(f32[32,256]{1,0:T(8,128)S(1)} %get-tuple-element.90), channel_id=1, source_target_pairs={{0,2},{2,0},{1,3},{3,1},{4,6},{6,4},{5,7},{7,5},{8,10},{10,8},{9,1... | collective-permute-start | bytes 98312 | tf_op jit(solution)/shard_map/ppermute | solution.py:656
  39.6 0.0 copy-done.2
  39.6 2.2 %sweep.1.swept = f32[64,32,256]{2,1,0:T(8,128)S(1)} custom-call(f32[26,64,256]{2,1,0:T(8,128)S(1)} %get-tuple-element.87.mid, f32[6,64,256]{2,1,0:T(8,128)S(1)} %get-tuple-element.88.end, f32[4,128]{1,0:T(4,128)S(1)} %copy-done.2), custom_call_target="tpu_custom_call" | custom-call | flops 20971520 | bytes 4194304 | tf_op jit(solution)/shard_map/sweep/pallas_call | solution.py:657
  41.8 0.0 collective-permute-done.9.far
  41.8 0.0 copy-done.1
  41.8 1.4 %finish.1 = f32[64,32,256]{2,1,0:T(8,128)} custom-call(f32[64,32,256]{2,1,0:T(8,128)S(1)} %sweep.1.swept, f32[2,32,256]{2,1,0:T(8,128)S(1)} %get-tuple-element.89.near, f32[32,256]{1,0:T(8,128)S(1)} %collective-permute-done.9.far, f32[4,128,128]{2,1,0:T(8,128)S(1)} %copy-done.1), custom_call_target="tpu_custom_call" | custom-call | bytes 6291456 | tf_op jit(solution)/shard_map/finish/pallas_call | solution.py:661
  (1 shorter events, 0.0 us)
Async XLA Ops:
  0.0 5.8 %copy-start.6 = (f32[4]{0:T(128)S(1)}, f32[4]{0:T(128)}, u32[]{:S(2)}) copy-start(f32[4]{0:T(128)} %rate_in.1) | copy-start | bytes 52
  0.0 5.8 %copy-start.5 = (f32[4]{0:T(128)S(1)}, f32[4]{0:T(128)}, u32[]{:S(2)}) copy-start(f32[4]{0:T(128)} %diffusivity_in.1) | copy-start | bytes 52
  0.0 5.8 %copy-start.4 = (f32[28]{0:T(128)S(1)}, f32[28]{0:T(128)}, u32[]{:S(2)}) copy-start(f32[28]{0:T(128)} %weight_in.1) | copy-start | bytes 340
  0.0 5.8 %copy-start.3 = (s32[28,2]{0,1:T(2,128)S(1)}, s32[28,2]{0,1:T(2,128)}, u32[]{:S(2)}) copy-start(s32[28,2]{0,1:T(2,128)} %param.14) | copy-start | bytes 676
  2.2 8.1 %collective-permute-start = (f32[2,64,128]{2,1,0:T(8,128)S(1)}, f32[2,64,128]{2,1,0:T(8,128)S(1)}, u32[]{:S(2)}, u32[]{:S(2)}) collective-permute-start(f32[2,64,128]{2,1,0:T(8,128)S(1)} %get-tuple-element.50.own_first), channel_id=1, source_target_pairs={{4,8},{12,0},{8,4},{0,12},{5,9},{13,1},{9,5},{1,13},{6,10},{14,2},... | collective-permute-start | bytes 196616 | tf_op jit(solution)/shard_map/ppermute | solution.py:598
  5.8 4.5 %collective-permute-start.1 = (f32[2,64,128]{2,1,0:T(8,128)S(1)}, f32[2,64,128]{2,1,0:T(8,128)S(1)}, u32[]{:S(2)}, u32[]{:S(2)}) collective-permute-start(f32[2,64,128]{2,1,0:T(8,128)S(1)} %get-tuple-element.51.own_second), channel_id=1, source_target_pairs={{0,4},{8,12},{4,0},{12,8},{1,5},{9,13},{5,1},{13,9},{2,6},{10,14},... | collective-permute-start | bytes 196616 | tf_op jit(solution)/shard_map/ppermute | solution.py:598
  10.5 12.0 %collective-permute-start.2 = (f32[432,128]{1,0:T(8,128)S(1)}, f32[432,128]{1,0:T(8,128)S(1)}, u32[]{:S(2)}, u32[]{:S(2)}) collective-permute-start(f32[432,128]{1,0:T(8,128)S(1)} %get-tuple-element.64), channel_id=1, source_target_pairs={{16,32},{48,64},{80,96},{112,128},{144,160},{176,192},{208,224},{2... | collective-permute-start | bytes 663560 | tf_op jit(solution)/shard_map/ppermute | solution.py:598
  17.1 5.6 %collective-permute-start.3 = (f32[432,128]{1,0:T(8,128)S(1)}, f32[432,128]{1,0:T(8,128)S(1)}, u32[]{:S(2)}, u32[]{:S(2)}) collective-permute-start(f32[432,128]{1,0:T(8,128)S(1)} %get-tuple-element.65), channel_id=1, source_target_pairs={{0,16},{32,48},{64,80},{96,112},{128,144},{160,176},{192,208},{224... | collective-permute-start | bytes 663560 | tf_op jit(solution)/shard_map/ppermute | solution.py:598
  17.1 5.3 %collective-permute-start.4 = (f32[2,64,128]{2,1,0:T(8,128)S(1)}, f32[2,64,128]{2,1,0:T(8,128)S(1)}, u32[]{:S(2)}, u32[]{:S(2)}) collective-permute-start(f32[2,64,128]{2,1,0:T(8,128)S(1)} %get-tuple-element.69), channel_id=1, source_target_pairs={{4,8},{12,0},{8,4},{0,12},{5,9},{13,1},{9,5},{1,13},{6,10},{14,2},... | collective-permute-start | bytes 196616 | tf_op jit(solution)/shard_map/ppermute | solution.py:598
  17.8 4.7 %collective-permute-start.5 = (f32[2,64,128]{2,1,0:T(8,128)S(1)}, f32[2,64,128]{2,1,0:T(8,128)S(1)}, u32[]{:S(2)}, u32[]{:S(2)}) collective-permute-start(f32[2,64,128]{2,1,0:T(8,128)S(1)} %get-tuple-element.70), channel_id=1, source_target_pairs={{0,4},{8,12},{4,0},{12,8},{1,5},{9,13},{5,1},{13,9},{2,6},{10,14},... | collective-permute-start | bytes 196616 | tf_op jit(solution)/shard_map/ppermute | solution.py:598
  18.6 4.2 %copy-start = (f32[4,128,128]{2,1,0:T(8,128)S(1)}, f32[4,128,128]{2,1,0:T(8,128)}, u32[]{:S(2)}) copy-start(f32[4,128,128]{2,1,0:T(8,128)} %constant.6.clone.sums.rest_9_) | copy-start | bytes 786436
  24.2 7.0 %collective-permute-start.6 = (f32[400,128]{1,0:T(8,128)S(1)}, f32[400,128]{1,0:T(8,128)S(1)}, u32[]{:S(2)}, u32[]{:S(2)}) collective-permute-start(f32[400,128]{1,0:T(8,128)S(1)} %get-tuple-element.79), channel_id=1, source_target_pairs={{16,32},{48,64},{80,96},{112,128},{144,160},{176,192},{208,224},{2... | collective-permute-start | bytes 614408 | tf_op jit(solution)/shard_map/ppermute | solution.py:598
  26.7 4.6 %collective-permute-start.7 = (f32[400,128]{1,0:T(8,128)S(1)}, f32[400,128]{1,0:T(8,128)S(1)}, u32[]{:S(2)}, u32[]{:S(2)}) collective-permute-start(f32[400,128]{1,0:T(8,128)S(1)} %get-tuple-element.80), channel_id=1, source_target_pairs={{0,16},{32,48},{64,80},{96,112},{128,144},{160,176},{192,208},{224... | collective-permute-start | bytes 614408 | tf_op jit(solution)/shard_map/ppermute | solution.py:598
  31.3 8.3 %copy-start.2 = (f32[4,128]{1,0:T(4,128)S(1)}, f32[4,128]{1,0:T(4,128)}, u32[]{:S(2)}) copy-start(f32[4,128]{1,0:T(4,128)} %constant.8.clone.solve) | copy-start | bytes 6148
  32.7 4.4 %collective-permute-start.8 = (f32[2,32,256]{2,1,0:T(8,128)S(1)}, f32[2,32,256]{2,1,0:T(8,128)S(1)}, u32[]{:S(2)}, u32[]{:S(2)}) collective-permute-start(f32[2,32,256]{2,1,0:T(8,128)S(1)} %get-tuple-element.83.own_sums), channel_id=1, source_target_pairs={{0,1},{1,0},{2,3},{3,2},{4,5},{5,4},{6,7},{7,6},{8,9},{9,8},{10,11... | collective-permute-start | bytes 196616 | tf_op jit(solution)/shard_map/ppermute | solution.py:651
  37.0 4.8 %copy-start.1 = (f32[4,128,128]{2,1,0:T(8,128)S(1)}, f32[4,128,128]{2,1,0:T(8,128)}, u32[]{:S(2)}) copy-start(f32[4,128,128]{2,1,0:T(8,128)} %constant.7.clone.reply) | copy-start | bytes 786436
  37.1 4.7 %collective-permute-start.9 = (f32[32,256]{1,0:T(8,128)S(1)}, f32[32,256]{1,0:T(8,128)S(1)}, u32[]{:S(2)}, u32[]{:S(2)}) collective-permute-start(f32[32,256]{1,0:T(8,128)S(1)} %get-tuple-element.90), channel_id=1, source_target_pairs={{0,2},{2,0},{1,3},{3,1},{4,6},{6,4},{5,7},{7,5},{8,10},{10,8},{9,1... | collective-permute-start | bytes 98312 | tf_op jit(solution)/shard_map/ppermute | solution.py:656

commit v7 on v6

--- a/solution.py
+++ b/solution.py
@@ -621,7 +621,6 @@
     outer_cost = dict(flops=2 * 8 * DZ * DY * 3328, nbytes=6 << 20)
 
     x_first, x_second = swaps(up, down, "gx")
-    to_high, to_low, up, down = lax.optimization_barrier((to_high, to_low, up, down))
     coefs = swaps(to_high, to_low, "gy")
     new_mid, new_mid_high, new_mid_low, flux, new_middle, mid_high, end_high, mid_low, end_low, middle = call(
         functools.partial(inner_kernel, False), "inner0",

time: 43.6 us -> 45.2 us (1.037)
  waiting for transfers between devices: 1.28 us -> 2.29 us
  starting transfers between devices: 20.2 us -> 20.8 us
    ppermute x8, waiting for transfers between devices: 0.37 us -> 1.39 us  [swaps(): lax.ppermute(value, axis, pairs + [(target, source) for source, target in...]
  transfers between devices with their start and end apart: 10 -> 10, of which waited for: 3 -> 4; matrix products, arithmetic and copies ran while one was open for 0% -> 0% of each run, Pallas kernels for 35% -> 34%
where the time goes in v7:
time: 45.2 us; the launch traced here: 45 us
  Pallas kernels  21.6 us (48%)
  starting transfers between devices  20.8 us (46%)
  waiting for transfers between devices  2.29 us (5%)
    ppermute x8, starting transfers between devices, swaps(): lax.ppermute(value, axis, pairs + [(target, source) for source, target in...  14.4 us
    pallas_call x1, Pallas kernels, local(): call(functools.partial(inner_kernel, True), 'inner1', (PARTS[0], struct(2...  4.49 us
    pallas_call x1, Pallas kernels, local(): call(prepare_kernel, 'prepare', (struct(9, DY, DY, dtype=bf16), WHOLE, WH...  4.44 us
    ppermute x1, starting transfers between devices, local(): partner = lax.ppermute(ends, 'gz', [(0, 1), (1, 0), (2, 3), (3, 2)])  3.89 us
    pallas_call x1, Pallas kernels, local(): call(functools.partial(inner_kernel, False), 'inner0', (PARTS[0], PARTS[2...  3.88 us
    ppermute x1, starting transfers between devices, local(): far = lax.ppermute(send, 'gz', [(0, 2), (2, 0), (1, 3), (3, 1)])  2.53 us
    pallas_call x1, Pallas kernels, local(): call(sweep_kernel, 'sweep', struct(DZ, DX, DY), [VMEM, VMEM, SMEM], VMEM,...  2.2 us
    pallas_call x1, Pallas kernels, local(): call(first_kernel, 'first', PARTS[:2] + (PACK, PACK, SLABS, SLABS), [HBM]...  2.15 us
  transfers between devices with their start and end apart: 10, of which 4 were waited for; matrix products, arithmetic and copies ran while one was open for 0% of the time, Pallas kernels for 34%

profile of v7, /device:TPU:1, one launch (start us, length us, event | category | flops | bytes accessed | tf_op | source)
XLA Modules:
  0.0 45.0 jit_solution(8802609940991570552)
XLA Ops:
  0.0 0.0 copy-start.6
  0.0 0.0 copy-start.5
  0.0 0.0 copy-start.4
  0.0 0.0 copy-start.3
  0.0 2.2 %first.1 = (f32[26,64,256]{2,1,0:T(8,128)S(1)}, f32[6,64,256]{2,1,0:T(8,128)S(1)}, f32[2,64,128]{2,1,0:T(8,128)S(1)}, f32[2,64,128]{2,1,0:T(8,128)S(1)}, f32[384,128]{1,0:T(8,128)S(1)}, /*index=5*/f32[384,128]{1,0:T(8,128)S(1)}) custom-call(f32[64,32,256]{2,1,0:T(8,128)} %conc.1), custom_call_target="tpu_custom_call" | custom-call | bytes 4194304 | tf_op jit(solution)/shard_map/first/pallas_call | solution.py:604
  2.2 3.6 %collective-permute-start = (f32[2,64,128]{2,1,0:T(8,128)S(1)}, f32[2,64,128]{2,1,0:T(8,128)S(1)}, u32[]{:S(2)}, u32[]{:S(2)}) collective-permute-start(f32[2,64,128]{2,1,0:T(8,128)S(1)} %get-tuple-element.48.own_first), channel_id=1, source_target_pairs={{4,8},{12,0},{8,4},{0,12},{5,9},{13,1},{9,5},{1,13},{6,10},{14,2},... | collective-permute-start | bytes 196616 | tf_op jit(solution)/shard_map/ppermute | solution.py:598
  5.8 0.0 collective-permute-start.1
  5.8 0.0 copy-done.6
  5.8 0.0 copy-done.5
  5.8 0.0 copy-done.4
  5.8 0.0 copy-done.3
  5.8 4.4 %prepare.1 = (bf16[9,256,256]{2,1,0:T(8,128)(2,1)S(1)}, f32[32,64,256]{2,1,0:T(8,128)S(1)}, f32[32,64,256]{2,1,0:T(8,128)S(1)}, f32[56,128]{1,0:T(8,128)S(1)}, f...) custom-call(s32[2,28]{1,0:T(2,128)S(1)} %bitcast.1, f32[28]{0:T(128)S(1)} %copy-done.4, f32[4]{0:T(128)S(1)} %copy-done.5, ...), custom_call_target="tpu_custom_call" | custom-call | bytes 8388608 | tf_op jit(solution)/shard_map/prepare/pallas_call | solution.py:609
  10.3 0.7 %collective-permute-start.4 = (f32[2,64,128]{2,1,0:T(8,128)S(1)}, f32[2,64,128]{2,1,0:T(8,128)S(1)}, u32[]{:S(2)}, u32[]{:S(2)}) collective-permute-start(f32[2,64,128]{2,1,0:T(8,128)S(1)} %get-tuple-element.65), channel_id=1, source_target_pairs={{4,8},{12,0},{8,4},{0,12},{5,9},{13,1},{9,5},{1,13},{6,10},{14,2},... | collective-permute-start | bytes 196616 | tf_op jit(solution)/shard_map/ppermute | solution.py:598
  11.0 0.9 %collective-permute-start.5 = (f32[2,64,128]{2,1,0:T(8,128)S(1)}, f32[2,64,128]{2,1,0:T(8,128)S(1)}, u32[]{:S(2)}, u32[]{:S(2)}) collective-permute-start(f32[2,64,128]{2,1,0:T(8,128)S(1)} %get-tuple-element.66), channel_id=1, source_target_pairs={{0,4},{8,12},{4,0},{12,8},{1,5},{9,13},{5,1},{13,9},{2,6},{10,14},... | collective-permute-start | bytes 196616 | tf_op jit(solution)/shard_map/ppermute | solution.py:598
  11.9 0.0 collective-permute-done.y_first
  11.9 0.0 collective-permute-done.1.y_second
  11.9 0.2 join.1
  12.2 6.6 %collective-permute-start.2 = (f32[432,128]{1,0:T(8,128)S(1)}, f32[432,128]{1,0:T(8,128)S(1)}, u32[]{:S(2)}, u32[]{:S(2)}) collective-permute-start(f32[432,128]{1,0:T(8,128)S(1)} %get-tuple-element.62), channel_id=1, source_target_pairs={{16,32},{48,64},{80,96},{112,128},{144,160},{176,192},{208,224},{2... | collective-permute-start | bytes 663560 | tf_op jit(solution)/shard_map/ppermute | solution.py:598
  18.8 0.0 collective-permute-start.3
  18.8 0.0 copy-start
  18.8 3.9 %inner0.1 = (f32[26,64,256]{2,1,0:T(8,128)S(1)}, bf16[26,64,256]{2,1,0:T(8,128)(2,1)S(1)}, bf16[26,64,256]{2,1,0:T(8,128)(2,1)S(1)}, f32[2,64,128]{2,1,0:T(8,128...) custom-call(f32[26,64,256]{2,1,0:T(8,128)S(1)} %get-tuple-element.47, ...), custom_call_target="tpu_custom_call" | custom-call | flops 2835349504 | bytes 12582912 | tf_op jit(solution)/shard_map/inner0/pallas_call | solution.py:625
  22.7 0.0 collective-permute-done.4.rest_0_
  22.7 0.0 collective-permute-done.5.rest_1_
  22.7 0.4 collective-permute-done.2.x_first
  23.0 0.9 %collective-permute-done.3.x_second = f32[432,128]{1,0:T(8,128)S(1)} collective-permute-done((f32[432,128]{1,0:T(8,128)S(1)}, f32[432,128]{1,0:T(8,128)S(1)}, u32[]{:S(2)}, u32[]{:S(2)}) %collective-permute-start.3) | collective-permute-done | bytes 221216 | tf_op jit(solution)/shard_map/ppermute | solution.py:598
  23.9 0.0 copy-done
  23.9 1.4 %outer0.1 = (f32[6,64,256]{2,1,0:T(8,128)S(1)}, bf16[6,64,256]{2,1,0:T(8,128)(2,1)S(1)}, bf16[6,64,256]{2,1,0:T(8,128)(2,1)S(1)}, f32[1,2,64,128]{3,2,1,0:T(8,12...) custom-call(f32[6,64,256]{2,1,0:T(8,128)S(1)} %get-tuple-element.46.rest_0_.end, ...), custom_call_target="tpu_custom_call" | custom-call | flops 872415232 | bytes 6291456 | tf_op jit(solution)/shard_map/outer0/pallas_call | solution.py:630
  25.4 2.5 %collective-permute-start.6 = (f32[400,128]{1,0:T(8,128)S(1)}, f32[400,128]{1,0:T(8,128)S(1)}, u32[]{:S(2)}, u32[]{:S(2)}) collective-permute-start(f32[400,128]{1,0:T(8,128)S(1)} %get-tuple-element.75), channel_id=1, source_target_pairs={{16,32},{48,64},{80,96},{112,128},{144,160},{176,192},{208,224},{2... | collective-permute-start | bytes 614408 | tf_op jit(solution)/shard_map/ppermute | solution.py:598
  27.8 0.0 collective-permute-start.7
  27.9 4.5 %inner1.1 = (f32[26,64,256]{2,1,0:T(8,128)S(1)}, f32[2,32,256]{2,1,0:T(8,128)S(1)}) custom-call(f32[26,64,256]{2,1,0:T(8,128)S(1)} %get-tuple-element.77.mid, bf16[26,64,256]{2,1,0:T(8,128)(2,1)S(1)} %get-tuple-element.69.rest_0_.mid_high, bf16[6,64,256]{2,1,0:T(8,128)(2,1)S(1)} %get-tuple-element.70.rest_1_.end_high, ...), custom_call_target="tpu_custom_call" | custom-call | flops 2835349504 | bytes 12582912 | tf_op jit(solution)/shard_map/inner1/pallas_call | solution.py:641
  32.3 0.0 collective-permute-done.6.x_first
  32.4 0.1 collective-permute-done.7.x_second
  32.5 0.0 copy-start.2
  32.5 1.4 %outer1.1 = (f32[6,64,256]{2,1,0:T(8,128)S(1)}, f32[2,32,256]{2,1,0:T(8,128)S(1)}) custom-call(f32[6,64,256]{2,1,0:T(8,128)S(1)} %get-tuple-element.68.end, bf16[26,64,256]{2,1,0:T(8,128)(2,1)S(1)} %get-tuple-element.69.rest_0_.mid_high, bf16[6,64,256]{2,1,0:T(8,128)(2,1)S(1)} %get-tuple-element.70.rest_1_.end_high, ...), custom_call_target="tpu_custom_call" | custom-call | flops 872415232 | bytes 6291456 | tf_op jit(solution)/shard_map/outer1/pallas_call | solution.py:645
  33.8 3.9 %collective-permute-start.8 = (f32[2,32,256]{2,1,0:T(8,128)S(1)}, f32[2,32,256]{2,1,0:T(8,128)S(1)}, u32[]{:S(2)}, u32[]{:S(2)}) collective-permute-start(f32[2,32,256]{2,1,0:T(8,128)S(1)} %get-tuple-element.79.own_sums), channel_id=1, source_target_pairs={{0,1},{1,0},{2,3},{3,2},{4,5},{5,4},{6,7},{7,6},{8,9},{9,8},{10,11... | collective-permute-start | bytes 196616 | tf_op jit(solution)/shard_map/ppermute | solution.py:650
  37.7 0.9 %collective-permute-done.8.partner_sums = f32[2,32,256]{2,1,0:T(8,128)S(1)} collective-permute-done((f32[2,32,256]{2,1,0:T(8,128)S(1)}, f32[2,32,256]{2,1,0:T(8,128)S(1)}, u32[]{:S(2)}, u32[]{:S(2)}) %collective-permute-start.8) | collective-permute-done | bytes 65568 | tf_op jit(solution)/shard_map/ppermute | solution.py:650
  38.6 0.0 copy-start.1
  38.7 2.5 %collective-permute-start.9 = (f32[32,256]{1,0:T(8,128)S(1)}, f32[32,256]{1,0:T(8,128)S(1)}, u32[]{:S(2)}, u32[]{:S(2)}) collective-permute-start(f32[32,256]{1,0:T(8,128)S(1)} %get-tuple-element.86), channel_id=1, source_target_pairs={{0,2},{2,0},{1,3},{3,1},{4,6},{6,4},{5,7},{7,5},{8,10},{10,8},{9,1... | collective-permute-start | bytes 98312 | tf_op jit(solution)/shard_map/ppermute | solution.py:655
  41.2 0.0 copy-done.2
  41.2 2.2 %sweep.1.swept = f32[64,32,256]{2,1,0:T(8,128)S(1)} custom-call(f32[26,64,256]{2,1,0:T(8,128)S(1)} %get-tuple-element.83.mid, f32[6,64,256]{2,1,0:T(8,128)S(1)} %get-tuple-element.84.end, f32[4,128]{1,0:T(4,128)S(1)} %copy-done.2), custom_call_target="tpu_custom_call" | custom-call | flops 20971520 | bytes 4194304 | tf_op jit(solution)/shard_map/sweep/pallas_call | solution.py:656
  43.4 0.0 collective-permute-done.9.far
  43.4 0.0 copy-done.1
  43.4 1.4 %finish.1 = f32[64,32,256]{2,1,0:T(8,128)} custom-call(f32[64,32,256]{2,1,0:T(8,128)S(1)} %sweep.1.swept, f32[2,32,256]{2,1,0:T(8,128)S(1)} %get-tuple-element.85.near, f32[32,256]{1,0:T(8,128)S(1)} %collective-permute-done.9.far, f32[4,128,128]{2,1,0:T(8,128)S(1)} %copy-done.1), custom_call_target="tpu_custom_call" | custom-call | bytes 6291456 | tf_op jit(solution)/shard_map/finish/pallas_call | solution.py:660
  (1 shorter events, 0.0 us)
Async XLA Ops:
  0.0 5.8 %copy-start.6 = (f32[4]{0:T(128)S(1)}, f32[4]{0:T(128)}, u32[]{:S(2)}) copy-start(f32[4]{0:T(128)} %rate_in.1) | copy-start | bytes 52
  0.0 5.8 %copy-start.5 = (f32[4]{0:T(128)S(1)}, f32[4]{0:T(128)}, u32[]{:S(2)}) copy-start(f32[4]{0:T(128)} %diffusivity_in.1) | copy-start | bytes 52
  0.0 5.8 %copy-start.4 = (f32[28]{0:T(128)S(1)}, f32[28]{0:T(128)}, u32[]{:S(2)}) copy-start(f32[28]{0:T(128)} %weight_in.1) | copy-start | bytes 340
  0.0 5.8 %copy-start.3 = (s32[28,2]{0,1:T(2,128)S(1)}, s32[28,2]{0,1:T(2,128)}, u32[]{:S(2)}) copy-start(s32[28,2]{0,1:T(2,128)} %param.14) | copy-start | bytes 676
  2.2 9.8 %collective-permute-start = (f32[2,64,128]{2,1,0:T(8,128)S(1)}, f32[2,64,128]{2,1,0:T(8,128)S(1)}, u32[]{:S(2)}, u32[]{:S(2)}) collective-permute-start(f32[2,64,128]{2,1,0:T(8,128)S(1)} %get-tuple-element.48.own_first), channel_id=1, source_target_pairs={{4,8},{12,0},{8,4},{0,12},{5,9},{13,1},{9,5},{1,13},{6,10},{14,2},... | collective-permute-start | bytes 196616 | tf_op jit(solution)/shard_map/ppermute | solution.py:598
  5.8 6.1 %collective-permute-start.1 = (f32[2,64,128]{2,1,0:T(8,128)S(1)}, f32[2,64,128]{2,1,0:T(8,128)S(1)}, u32[]{:S(2)}, u32[]{:S(2)}) collective-permute-start(f32[2,64,128]{2,1,0:T(8,128)S(1)} %get-tuple-element.49.own_second), channel_id=1, source_target_pairs={{0,4},{8,12},{4,0},{12,8},{1,5},{9,13},{5,1},{13,9},{2,6},{10,14},... | collective-permute-start | bytes 196616 | tf_op jit(solution)/shard_map/ppermute | solution.py:598
  10.3 12.4 %collective-permute-start.4 = (f32[2,64,128]{2,1,0:T(8,128)S(1)}, f32[2,64,128]{2,1,0:T(8,128)S(1)}, u32[]{:S(2)}, u32[]{:S(2)}) collective-permute-start(f32[2,64,128]{2,1,0:T(8,128)S(1)} %get-tuple-element.65), channel_id=1, source_target_pairs={{4,8},{12,0},{8,4},{0,12},{5,9},{13,1},{9,5},{1,13},{6,10},{14,2},... | collective-permute-start | bytes 196616 | tf_op jit(solution)/shard_map/ppermute | solution.py:598
  11.0 11.7 %collective-permute-start.5 = (f32[2,64,128]{2,1,0:T(8,128)S(1)}, f32[2,64,128]{2,1,0:T(8,128)S(1)}, u32[]{:S(2)}, u32[]{:S(2)}) collective-permute-start(f32[2,64,128]{2,1,0:T(8,128)S(1)} %get-tuple-element.66), channel_id=1, source_target_pairs={{0,4},{8,12},{4,0},{12,8},{1,5},{9,13},{5,1},{13,9},{2,6},{10,14},... | collective-permute-start | bytes 196616 | tf_op jit(solution)/shard_map/ppermute | solution.py:598
  12.2 10.9 %collective-permute-start.2 = (f32[432,128]{1,0:T(8,128)S(1)}, f32[432,128]{1,0:T(8,128)S(1)}, u32[]{:S(2)}, u32[]{:S(2)}) collective-permute-start(f32[432,128]{1,0:T(8,128)S(1)} %get-tuple-element.62), channel_id=1, source_target_pairs={{16,32},{48,64},{80,96},{112,128},{144,160},{176,192},{208,224},{2... | collective-permute-start | bytes 663560 | tf_op jit(solution)/shard_map/ppermute | solution.py:598
  18.8 5.2 %collective-permute-start.3 = (f32[432,128]{1,0:T(8,128)S(1)}, f32[432,128]{1,0:T(8,128)S(1)}, u32[]{:S(2)}, u32[]{:S(2)}) collective-permute-start(f32[432,128]{1,0:T(8,128)S(1)} %get-tuple-element.63), channel_id=1, source_target_pairs={{0,16},{32,48},{64,80},{96,112},{128,144},{160,176},{192,208},{224... | collective-permute-start | bytes 663560 | tf_op jit(solution)/shard_map/ppermute | solution.py:598
  18.8 5.2 %copy-start = (f32[4,128,128]{2,1,0:T(8,128)S(1)}, f32[4,128,128]{2,1,0:T(8,128)}, u32[]{:S(2)}) copy-start(f32[4,128,128]{2,1,0:T(8,128)} %constant.6.clone.sums.rest_9_) | copy-start | bytes 786436
  25.4 7.0 %collective-permute-start.6 = (f32[400,128]{1,0:T(8,128)S(1)}, f32[400,128]{1,0:T(8,128)S(1)}, u32[]{:S(2)}, u32[]{:S(2)}) collective-permute-start(f32[400,128]{1,0:T(8,128)S(1)} %get-tuple-element.75), channel_id=1, source_target_pairs={{16,32},{48,64},{80,96},{112,128},{144,160},{176,192},{208,224},{2... | collective-permute-start | bytes 614408 | tf_op jit(solution)/shard_map/ppermute | solution.py:598
  27.8 4.6 %collective-permute-start.7 = (f32[400,128]{1,0:T(8,128)S(1)}, f32[400,128]{1,0:T(8,128)S(1)}, u32[]{:S(2)}, u32[]{:S(2)}) collective-permute-start(f32[400,128]{1,0:T(8,128)S(1)} %get-tuple-element.76), channel_id=1, source_target_pairs={{0,16},{32,48},{64,80},{96,112},{128,144},{160,176},{192,208},{224... | collective-permute-start | bytes 614408 | tf_op jit(solution)/shard_map/ppermute | solution.py:598
  32.5 8.7 %copy-start.2 = (f32[4,128]{1,0:T(4,128)S(1)}, f32[4,128]{1,0:T(4,128)}, u32[]{:S(2)}) copy-start(f32[4,128]{1,0:T(4,128)} %constant.8.clone.solve) | copy-start | bytes 6148
  33.8 4.8 %collective-permute-start.8 = (f32[2,32,256]{2,1,0:T(8,128)S(1)}, f32[2,32,256]{2,1,0:T(8,128)S(1)}, u32[]{:S(2)}, u32[]{:S(2)}) collective-permute-start(f32[2,32,256]{2,1,0:T(8,128)S(1)} %get-tuple-element.79.own_sums), channel_id=1, source_target_pairs={{0,1},{1,0},{2,3},{3,2},{4,5},{5,4},{6,7},{7,6},{8,9},{9,8},{10,11... | collective-permute-start | bytes 196616 | tf_op jit(solution)/shard_map/ppermute | solution.py:650
  38.6 4.8 %copy-start.1 = (f32[4,128,128]{2,1,0:T(8,128)S(1)}, f32[4,128,128]{2,1,0:T(8,128)}, u32[]{:S(2)}) copy-start(f32[4,128,128]{2,1,0:T(8,128)} %constant.7.clone.reply) | copy-start | bytes 786436
  38.7 4.7 %collective-permute-start.9 = (f32[32,256]{1,0:T(8,128)S(1)}, f32[32,256]{1,0:T(8,128)S(1)}, u32[]{:S(2)}, u32[]{:S(2)}) collective-permute-start(f32[32,256]{1,0:T(8,128)S(1)} %get-tuple-element.86), channel_id=1, source_target_pairs={{0,2},{2,0},{1,3},{3,1},{4,6},{6,4},{5,7},{7,5},{8,10},{10,8},{9,1... | collective-permute-start | bytes 98312 | tf_op jit(solution)/shard_map/ppermute | solution.py:655
